TPU v7x, 128 devices: a whole 4x4x4 slice. The times are simulated.
128 devices in a mesh: freq: 8 (over z, x_hi), rcv: 16 (over x_lo, y, core).
Axes of the slice: x: 4 (x_hi: 2, x_lo: 2; x = x_hi * 2 + x_lo), y: 4, z: 4, core: 2. Of those that a mesh axis runs over, the one named last changes fastest.
Arguments:
- reflection: float32 [128, 2, 1024, 2048], P('freq', None, None, 'rcv'), may hold values from -0.09375 to 0.09375
- focusing_input: float32 [128, 2, 32, 2048], P('freq', None, None, 'rcv'), may hold values from -6 to 6
- direct_wave: float32 [256, 32, 2048], P(None, 'freq', 'rcv'), may hold values from -6 to 6
- mute_source: int32 [32, 1024], P('rcv', 'freq'), may hold values from 32 to 127
- mute_receiver: int32 [32, 2048], P('freq', 'rcv'), may hold values from 32 to 127
Outputs:
- focus_minus: float32 [256, 32, 1024], P(None, 'rcv', 'freq')
- focus_plus: float32 [256, 32, 2048], P(None, 'freq', 'rcv')
All inputs are finite; a program needn't handle non-finite values.
Results may differ from a plain program's by a relative error of at most 0.00007.
Values sent between devices are 32-bit elements; how exact they have to be, the bound alone decides.
No kernel may reach another device: no remote copies, remote signals or barrier semaphores. Data moves between devices by JAX's collectives and lax.ppermute only.
A program may use at most 128 MiB of HBM per device.

v0:
```python
import math

import jax
import jax.numpy as jnp
from jax import lax
from jax.sharding import PartitionSpec as P

MAXIMUM_ACCURACY = lax.Precision.HIGHEST


def dft_tables(freqs, samples):
    index_freq = lax.broadcasted_iota(jnp.int32, (freqs, samples), 0) + 1
    index_time = lax.broadcasted_iota(jnp.int32, (freqs, samples), 1)
    phase_turns = jnp.mod(index_freq * index_time, samples).astype(jnp.float32) * (
        2.0 * math.pi / samples
    )
    return (jnp.cos(phase_turns), jnp.sin(phase_turns))


def window(traces, mute_table):
    samples = traces.shape[0]
    time_index = lax.broadcasted_iota(jnp.int32, (samples, 1, 1), 0)
    kept_mask = (time_index < mute_table[None]) | (time_index > samples - mute_table[None])
    return jnp.where(kept_mask, traces, jnp.zeros_like(traces))


def forward_panel(reflection, focusing_input):
    reflection_real = reflection[:, 0]
    reflection_imaginary = reflection[:, 1]
    real_part = jnp.einsum(
        "ual,uel->eua", reflection_real, focusing_input[:, 0], precision=MAXIMUM_ACCURACY
    ) - jnp.einsum(
        "ual,uel->eua", reflection_imaginary, focusing_input[:, 1], precision=MAXIMUM_ACCURACY
    )
    imag_part = jnp.einsum(
        "ual,uel->eua", reflection_real, focusing_input[:, 1], precision=MAXIMUM_ACCURACY
    ) + jnp.einsum(
        "ual,uel->eua", reflection_imaginary, focusing_input[:, 0], precision=MAXIMUM_ACCURACY
    )
    return jnp.stack((real_part, imag_part), axis=2)


def adjoint_panel(reflection, receiver_panel):
    reflection_real = reflection[:, 0]
    reflection_imaginary = reflection[:, 1]
    real_part = jnp.einsum(
        "klh,lhc->klc", receiver_panel[:, :, 0], reflection_real, precision=MAXIMUM_ACCURACY
    ) + jnp.einsum(
        "klh,lhc->klc", receiver_panel[:, :, 1], reflection_imaginary, precision=MAXIMUM_ACCURACY
    )
    imag_part = jnp.einsum(
        "klh,lhc->klc", receiver_panel[:, :, 1], reflection_real, precision=MAXIMUM_ACCURACY
    ) - jnp.einsum(
        "klh,lhc->klc", receiver_panel[:, :, 0], reflection_imaginary, precision=MAXIMUM_ACCURACY
    )
    return jnp.stack((real_part, imag_part), axis=2)


def to_time(spectrum, cosine, sine_table, factor):
    return factor * (
        jnp.einsum("akb,kt->tab", spectrum[:, :, 0], cosine, precision=MAXIMUM_ACCURACY)
        - jnp.einsum("akb,kt->tab", spectrum[:, :, 1], sine_table, precision=MAXIMUM_ACCURACY)
    )


def to_freq(traces, cosine, sine_table, factor):
    real_part = factor * jnp.einsum("tab,kt->akb", traces, cosine, precision=MAXIMUM_ACCURACY)
    imag_part = -factor * jnp.einsum("tab,kt->akb", traces, sine_table, precision=MAXIMUM_ACCURACY)
    return jnp.stack((real_part, imag_part), axis=2)


def body(reflection, focusing_input, direct_wave, mute_source, mute_receiver):
    freqs = reflection.shape[0] * lax.axis_size("freq")
    samples = 2 * freqs
    factor = 1.0 / math.sqrt(freqs)
    cosine, sine_table = dft_tables(freqs, samples)
    share = mute_source.shape[0]
    term = forward_panel(reflection, focusing_input)
    summed = lax.psum(term, "rcv")
    spectrum = lax.all_to_all(summed, "freq", split_axis=3, concat_axis=1, tiled=True)
    mutes_all = lax.all_gather(mute_source, "rcv", axis=0, tiled=True)
    windowed = window(to_time(spectrum, cosine, sine_table, factor), mutes_all)
    focus_minus = lax.dynamic_slice_in_dim(windowed, lax.axis_index("rcv") * share, share, 1)
    back_local = to_freq(windowed, cosine, sine_table, factor)
    back_spec = lax.all_to_all(back_local, "freq", split_axis=1, concat_axis=3, tiled=True)
    adjoint = adjoint_panel(reflection, back_spec)
    receiver_spec = lax.all_to_all(adjoint, "freq", split_axis=0, concat_axis=1, tiled=True)
    adj_time = to_time(receiver_spec, cosine, sine_table, factor)
    focus_plus = direct_wave - window(adj_time, mute_receiver)
    return (focus_minus, focus_plus)


def solution(mesh):
    placed = (
        P("freq", None, None, "rcv"),
        P("freq", None, None, "rcv"),
        P(None, "freq", "rcv"),
        P("rcv", "freq"),
        P("freq", "rcv"),
    )
    return jax.shard_map(
        body,
        mesh=mesh,
        in_specs=placed,
        out_specs=(P(None, "rcv", "freq"), P(None, "freq", "rcv")),
        check_vma=False,
    )
```

profile of v0, /device:TPU:0, one launch (start us, length us, event | category | flops | bytes accessed | tf_op | source)
XLA Modules:
  0.0 455.7 jit_solution(1087763690156176081)
XLA Ops:
  7.2 0.0 all-reduce.2.cloned.1.call-start
  7.2 0.0 copy-start
  7.2 10.8 %fusion.4 = f32[16,32,1024]{2,1,0:T(8,128)S(1)} fusion(f32[16,2,1024,128]{3,2,1,0:T(8,128)} %param.5, f32[16,2,32,128]{3,2,1,0:T(8,128)} %param.6), kind=kOutput, calls=%fused_computation.4 | convolution fusion | flops 805306368 | bytes 10747904 | tf_op jit(solution)/shard_map/ual,uel->eua/dot_general | solution.py:37
  18.1 11.1 %fusion.6 = f32[16,32,1024]{2,1,0:T(8,128)S(1)} fusion(f32[16,2,1024,128]{3,2,1,0:T(8,128)} %param.5, f32[16,2,32,128]{3,2,1,0:T(8,128)S(1)} %copy-done.4), kind=kOutput, calls=%fused_computation.6 | convolution fusion | flops 805306368 | bytes 10747904 | tf_op jit(solution)/shard_map/ual,uel->eua/dot_general | solution.py:32
  29.2 0.0 copy-done
  29.2 8.4 %add_bitcast_fusion = f32[32,16,1,1024]{3,0,1,2:T(8,128)S(1)} fusion(f32[16,32,1024]{2,1,0:T(8,128)S(1)} %fusion.4, f32[16,2,1024,128]{3,2,1,0:T(8,128)S(1)} %copy-done, f32[16,2,32,128]{3,2,1,0:T(8,128)S(1)} %copy-done.4), kind=kOutput, calls=%fused_computation.38 | convolution fusion | flops 805830656 | bytes 12845056 | tf_op jit(solution)/shard_map/ual,uel->eua/dot_general | solution.py:35
  37.6 8.6 %subtract_bitcast_fusion = f32[32,16,1,1024]{3,0,1,2:T(8,128)S(1)} fusion(f32[16,32,1024]{2,1,0:T(8,128)S(1)} %fusion.6, f32[16,2,1024,128]{3,2,1,0:T(8,128)S(1)} %copy-done, f32[16,2,32,128]{3,2,1,0:T(8,128)S(1)} %copy-done.4), kind=kOutput, calls=%fused_computation.39 | convolution fusion | flops 805830656 | bytes 12845056 | tf_op jit(solution)/shard_map/ual,uel->eua/dot_general | solution.py:30
  46.2 2.6 pad_maximum_fusion
  48.8 0.0 all-reduce.2.cloned.1.call-update
  48.8 132.0 %all-reduce.2.cloned.1.call-done = f32[32,16,2,1024]{3,0,1,2:T(8,128)} async-done(((f32[32,16,2,1024]{3,0,1,2:T(8,128)}), f32[32,16,2,1024]{3,0,1,2:T(8,128)}) %all-reduce.2.cloned.1.call-update) | async-done | bytes 4194320 | tf_op jit(solution)/shard_map/psum | solution.py:79
  180.8 14.3 %copy.23 = f32[32,16,2,1024]{0,1,2,3:T(8,128)} copy(f32[32,16,2,1024]{3,0,1,2:T(8,128)} %all-reduce.2.cloned.1.call-done) | data formatting | bytes 8388608 | tf_op jit(solution)/shard_map/psum | solution.py:79
  195.1 12.8 %reshape.16 = f32[8,1,131072]{2,1,0:T(1,128)} reshape(f32[1024,2,16,32]{3,2,1,0:T(8,128)} %bitcast.140) | data formatting | bytes 8388608
  207.9 6.7 %all-to-all-start = ((f32[8,1,131072]{2,1,0:T(1,128)}), f32[8,1,131072]{2,1,0:T(1,128)}, u32[]{:S(2)}, u32[]{:S(2)}) async-start(f32[8,1,131072]{2,1,0:T(1,128)} %reshape.16), calls=%async_computation | async-start | bytes 8388608 | tf_op jit(solution)/shard_map/all_to_all | solution.py:80
  214.6 0.0 copy-done.7
  214.6 58.8 %all-gather = s32[16,2,128]{2,1,0:T(2,128)S(1)} all-gather(s32[1,2,128]{2,1,0:T(2,128)S(1)} %bitcast.151), channel_id=1, replica_groups=mesh['freq'=8,'rcv'=16] {'rcv'}, dimensions={0}, use_global_device_ids=true | all-gather | bytes 17408 | tf_op jit(solution)/shard_map/all_gather | solution.py:81
  273.4 0.0 all-to-all-done
  273.5 0.5 broadcast.42
  274.0 13.7 %reduce = f32[8,131072]{1,0:T(8,128)} reduce(f32[8,1,131072]{2,1,0:T(1,128)} %all-to-all-done, f32[]{:T(128)} %broadcast.42), dimensions={1}, to_apply=%all_to_all.39.reduce_sub_computation | reduce | bytes 8388612 | tf_op jit(solution)/shard_map/all_to_all | solution.py:80
  287.7 13.4 %reshape.17 = f32[1024,2,16,32]{3,2,1,0:T(8,128)} reshape(f32[8,131072]{1,0:T(8,128)} %reduce) | data formatting | bytes 8388608
  301.0 13.5 %copy.24 = f32[32,16,2,8,128]{4,1,3,0,2:T(8,128)} copy(f32[32,16,2,8,128]{0,1,2,4,3:T(8,128)} %bitcast.141) | data formatting | bytes 8388608 | tf_op jit(solution)/shard_map/all_to_all | solution.py:80
  314.6 0.0 copy-start.3
  314.6 5.8 %fusion.25 = f32[256,32,128]{2,0,1:T(8,128)S(1)} fusion(f32[32,128,2,128]{3,1,0,2:T(8,128)} %bitcast.142, s32[128]{0:T(128)S(1)} %iota_add_fusion), kind=kOutput, calls=%fused_computation.35 | convolution fusion | flops 1611071488 | bytes 6291968 | tf_op jit(solution)/shard_map/akb,kt->tab/dot_general | solution.py:61
  320.4 0.0 copy-done.3
  320.4 5.0 %multiply_select_fusion = f32[256,32,128]{2,0,1:T(8,128)S(1)} fusion(f32[256,32,128]{2,0,1:T(8,128)S(1)} %fusion.25, f32[32,128,2,128]{3,1,0,2:T(8,128)S(1)} %bitcast.143, s32[32,128]{1,0:T(8,128)S(1)} %broadcast_subtract_fusion, s32[32,128]{1,0:T(8,128)S(1)} %bitcast.150, s32[128]{0:T(128)S(1)} %iota_add_fusion), kind=kOutput, calls=%fused_computation.27 | convolution fusion | flops 1617362944 | bytes 10519040 | tf_op jit(solution)/shard_map/akb,kt->tab/dot_general | solution.py:62
  325.4 0.0 copy-start.1
  325.4 2.8 multiply_bitcast_fusion
  328.2 3.0 multiply_bitcast_fusion.1
  331.2 0.5 pad_maximum_fusion.1
  331.7 2.4 copy.27
  334.2 58.4 %all_to_all.54 = f32[32,128,2,128]{3,0,2,1:T(8,128)S(1)} all-to-all(f32[32,128,2,128]{3,0,2,1:T(8,128)S(1)} %copy.27), channel_id=1, replica_groups=mesh['freq'=8,'rcv'=16] {'freq'}, dimensions={1} | all-to-all | bytes 8388608 | tf_op jit(solution)/shard_map/all_to_all | solution.py:85
  392.6 5.8 %copy.44 = f32[32,8,16,2,128]{4,1,0,2,3:T(8,128)} copy(f32[32,8,16,2,128]{4,0,3,2,1:T(8,128)S(1)} %bitcast.144) | data formatting | bytes 8388608 | tf_op jit(solution)/shard_map/all_to_all | solution.py:85
  398.4 4.9 %all_to_all.46 = f32[32,16,2,1024]{3,0,1,2:T(8,128)} reshape(f32[32,16,2,8,128]{4,3,0,1,2:T(8,128)} %bitcast.145) | data formatting | bytes 8388608 | tf_op jit(solution)/shard_map/all_to_all | solution.py:85
  403.3 7.3 %fusion = f32[16,32,128]{2,1,0:T(8,128)S(1)} fusion(f32[16,2,1024,128]{3,2,1,0:T(8,128)} %param.5, f32[32,16,2,1024]{3,0,1,2:T(8,128)} %all_to_all.46), kind=kOutput, calls=%fused_computation | convolution fusion | flops 805306368 | bytes 10747904 | tf_op jit(solution)/shard_map/klh,lhc->klc/dot_general | solution.py:53
  410.6 0.0 slice-start.2
  410.6 7.3 %fusion.2 = f32[16,32,128]{2,1,0:T(8,128)S(1)} fusion(f32[16,2,1024,128]{3,2,1,0:T(8,128)} %param.5, f32[32,16,2,1024]{3,0,1,2:T(8,128)} %all_to_all.46), kind=kOutput, calls=%fused_computation.2 | convolution fusion | flops 805306368 | bytes 10747904 | tf_op jit(solution)/shard_map/klh,lhc->klc/dot_general | solution.py:48
  417.9 0.0 slice-start.3
  417.9 7.2 %fusion.42 = f32[32,16,1,128]{3,0,1,2:T(8,128)S(1)} fusion(f32[16,32,128]{2,1,0:T(8,128)S(1)} %fusion, f32[16,2,1024,128]{3,2,1,0:T(8,128)} %param.5, f32[32,16,2,1024]{3,0,1,2:T(8,128)S(1)} %copy-done.2), kind=kOutput, calls=%fused_computation.47 | convolution fusion | flops 805371904 | bytes 11010048 | tf_op jit(solution)/shard_map/klh,lhc->klc/dot_general | solution.py:51
  425.1 0.0 copy-start.6
  425.1 4.5 fusion.36
  429.6 0.0 copy-start.5
  429.6 1.1 copy.29
  430.7 3.5 all-to-all-start.2
  434.3 1.0 constant_dynamic-slice_fusion
  435.2 0.9 copy.32
  436.1 9.0 %all-to-all-done.2 = f32[32,16,2,128]{3,1,2,0:T(8,128)S(1)} async-done(((f32[32,16,2,128]{3,1,2,0:T(8,128)}), f32[32,16,2,128]{3,1,2,0:T(8,128)S(1)}, u32[]{:S(2)}, u32[]{:S(2)}) %all-to-all-start.2) | async-done | bytes 524320 | tf_op jit(solution)/shard_map/all_to_all | solution.py:87
  445.2 1.1 fusion.46
  446.2 1.2 fusion.32
  447.5 1.1 copy.33
  (20 shorter events, 0.1 us)
Async XLA Ops:
  7.2 10.9 %copy-start.4 = (f32[16,2,32,128]{3,2,1,0:T(8,128)S(1)}, f32[16,2,32,128]{3,2,1,0:T(8,128)}, u32[]{:S(2)}) copy-start(f32[16,2,32,128]{3,2,1,0:T(8,128)} %param.6) | copy-start | bytes 1572868
  7.2 173.6 %all-reduce.2.cloned.1.call-start = ((), (), s32[]{:S(2)}) async-start(), calls=%async_computation.3 | async-start | bytes 8388608 | tf_op jit(solution)/shard_map/psum | solution.py:79
  7.2 22.0 %copy-start = (f32[16,2,1024,128]{3,2,1,0:T(8,128)S(1)}, f32[16,2,1024,128]{3,2,1,0:T(8,128)}, u32[]{:S(2)}) copy-start(f32[16,2,1024,128]{3,2,1,0:T(8,128)} %param.5) | copy-start | bytes 50331652
  207.9 6.7 %copy-start.7 = (s32[2,128]{1,0:T(2,128)S(1)}, s32[2,128]{1,0:T(2,128)}, u32[]{:S(2)}) copy-start(s32[2,128]{1,0:T(2,128)} %param.8) | copy-start | bytes 3076
  207.9 65.5 %all-to-all-start = ((f32[8,1,131072]{2,1,0:T(1,128)}), f32[8,1,131072]{2,1,0:T(1,128)}, u32[]{:S(2)}, u32[]{:S(2)}) async-start(f32[8,1,131072]{2,1,0:T(1,128)} %reshape.16), calls=%async_computation | async-start | bytes 8388608 | tf_op jit(solution)/shard_map/all_to_all | solution.py:80
  314.6 5.8 %copy-start.3 = (f32[32,16,2,8,128]{4,1,3,0,2:T(8,128)S(1)}, f32[32,16,2,8,128]{4,1,3,0,2:T(8,128)}, u32[]{:S(2)}) copy-start(f32[32,16,2,8,128]{4,1,3,0,2:T(8,128)} %copy.24) | copy-start | bytes 12582916
  325.4 2.9 copy-start.1
  403.3 21.8 %slice-start = ((s8[16777216]{0:T(1024)(128)(4,1)}), s8[4194304]{0:T(1024)(128)(4,1)S(1)}, s32[]{:S(2)}) async-start(s8[16777216]{0:T(1024)(128)(4,1)} %bitcast.138), calls=%async_computation.4 | async-start | bytes 8388608
  403.3 21.8 %slice-start.1 = ((s8[16777216]{0:T(1024)(128)(4,1)}), s8[4194304]{0:T(1024)(128)(4,1)S(1)}, s32[]{:S(2)}) async-start(s8[16777216]{0:T(1024)(128)(4,1)} %bitcast.138), calls=%async_computation.5 | async-start | bytes 8388608
  410.6 7.3 %copy-start.2 = (f32[32,16,2,1024]{3,0,1,2:T(8,128)S(1)}, f32[32,16,2,1024]{3,0,1,2:T(8,128)}, u32[]{:S(2)}) copy-start(f32[32,16,2,1024]{3,0,1,2:T(8,128)} %all_to_all.46) | copy-start | bytes 12582916
  410.6 14.5 %slice-start.2 = ((s8[16777216]{0:T(1024)(128)(4,1)}), s8[4194304]{0:T(1024)(128)(4,1)S(1)}, s32[]{:S(2)}) async-start(s8[16777216]{0:T(1024)(128)(4,1)} %bitcast.138), calls=%async_computation.6 | async-start | bytes 8388608
  417.9 7.2 %slice-start.3 = ((s8[16777216]{0:T(1024)(128)(4,1)}), s8[4194304]{0:T(1024)(128)(4,1)S(1)}, s32[]{:S(2)}) async-start(s8[16777216]{0:T(1024)(128)(4,1)} %bitcast.138), calls=%async_computation.7 | async-start | bytes 8388608
  425.1 9.2 %copy-start.6 = (s32[4,128]{1,0:T(4,128)S(1)}, s32[4,128]{1,0:T(4,128)}, u32[]{:S(2)}) copy-start(s32[4,128]{1,0:T(4,128)} %param.9) | copy-start | bytes 6148
  429.6 16.6 %copy-start.5 = (f32[256,4,128]{2,1,0:T(4,128)S(1)}, f32[256,4,128]{2,1,0:T(4,128)}, u32[]{:S(2)}) copy-start(f32[256,4,128]{2,1,0:T(4,128)} %param.7) | copy-start | bytes 1572868
  430.7 14.4 %all-to-all-start.2 = ((f32[32,16,2,128]{3,1,2,0:T(8,128)}), f32[32,16,2,128]{3,1,2,0:T(8,128)S(1)}, u32[]{:S(2)}, u32[]{:S(2)}) async-start(f32[32,16,2,128]{3,1,2,0:T(8,128)} %copy.29), calls=%async_computation.2 | async-start | bytes 1048576 | tf_op jit(solution)/shard_map/all_to_all | solution.py:87
Sparse Core Ops, SparseCore 0:
  48.9 131.7 all-reduce.1
where the time goes:
time: 462 us; the launch traced here: 456 us
  waiting for transfers between devices  141 us (31%)
  blocking collectives  117 us (25%)
  matrix products  84 us (18%)
  local copies, waits for them, and re-layouts  71.9 us (16%)
  other arithmetic  16.8 us (4%)
  between operations  14.6 us (3%)
  starting transfers between devices  10.2 us (2%)
    psum x1, waiting for transfers between devices, body(): summed = lax.psum(term, 'rcv')  132 us
    all_gather x1, blocking collectives, body(): mutes_all = lax.all_gather(mute_source, 'rcv', axis=0, tiled=True)  58.8 us
    all_to_all x1, blocking collectives, body(): lax.all_to_all(back_local, 'freq', split_axis=1, concat_axis=3, tiled=True)  58.4 us
    unnamed x28, local copies, waits for them, and re-layouts  28.3 us
    psum x1, local copies, waits for them, and re-layouts, body(): summed = lax.psum(term, 'rcv')  14.3 us
    all_to_all x2, local copies, waits for them, and re-layouts, body(): lax.all_to_all(summed, 'freq', split_axis=3, concat_axis=1, tiled=True)  14 us
    all_to_all x1, other arithmetic, body(): lax.all_to_all(summed, 'freq', split_axis=3, concat_axis=1, tiled=True)  13.7 us
    dot_general x1, matrix products, forward_panel(): jnp.einsum('ual,uel->eua', reflection_imaginary, focusing_input[:, 1], pr...  11.1 us
  transfers between devices with their start and end apart: 3, of which 2 were waited for; matrix products, arithmetic and copies ran while one was open for 0% of the time, Pallas kernels for 0%

commit v1 on v0

v1 whole, which is shorter than its diff:
```python
import math

import numpy as np
import jax
import jax.numpy as jnp
from jax import lax
from jax.experimental import pallas as pl
from jax.experimental.pallas import tpu as pltpu
from jax.sharding import Mesh, PartitionSpec as P

F32, BF16 = jnp.float32, jnp.bfloat16
NT = 256
KB, KK = 8, 16


def dft_table():
    k = np.arange(1, KB * KK + 1)[None, :]
    t = np.arange(NT)[:, None]
    phase = 2.0 * math.pi * ((k * t) % NT) / NT
    c = 1.0 / math.sqrt(KB * KK)
    both = np.stack([c * np.cos(phase), -c * np.sin(phase)], axis=1)
    return both.reshape(NT, 2, KB, KK).transpose(0, 2, 1, 3).reshape(NT, NT)


def split_const(table):
    high = table.astype(np.float32).astype(jnp.bfloat16)
    low = (table - high.astype(np.float64)).astype(np.float32).astype(jnp.bfloat16)
    return np.asarray(high), np.asarray(low)


def split(x):
    high = x.astype(BF16)
    return high, (x - high.astype(F32)).astype(BF16)


def mm(a, b, contract=(1, 0)):
    return lax.dot_general(a, b, (((contract[0],), (contract[1],)), ((), ())), preferred_element_type=F32)


def mm3(a, b):
    return mm(a[0], b[0]) + (mm(a[0], b[1]) + mm(a[1], b[0]))


def forward_kernel(perm_ref, f_ref, r_ref, own_ref, oth_ref):
    perm = perm_ref[...]
    for q in range(2):
        fr, fi = f_ref[q, 0], f_ref[q, 1]
        x = jnp.concatenate(
            [jnp.concatenate([fr, -fi], axis=1), jnp.concatenate([fi, fr], axis=1)], axis=0
        )
        xh, xl = split(x)
        ph, plo = mm(perm, xh).astype(BF16), mm(perm, xl).astype(BF16)
        lhs = jnp.concatenate([ph, plo], axis=0)
        for z in range(4):
            rows = slice(z * 256, (z + 1) * 256)
            w = jnp.concatenate([r_ref[q, 0, rows, :], r_ref[q, 1, rows, :]], axis=1)
            wh, wl = split(w)
            acc = mm(lhs, wh, (1, 1))
            res = acc[:64] + (acc[64:] + mm(ph, wl, (1, 1)))
            res = res.reshape(2, 8, 4, 256)
            for xh_ in range(2):
                part = res[:, :, :, xh_ * 128 : (xh_ + 1) * 128]
                own_ref[xh_ * 8 : (xh_ + 1) * 8, z, q * 4 : (q + 1) * 4, :] = part[0]
                oth_ref[xh_ * 8 : (xh_ + 1) * 8, z, q * 4 : (q + 1) * 4, :] = part[1]


def forward_panel(reflection, focusing, perm):
    panel = jax.ShapeDtypeStruct((16, 4, 64, 128), F32)
    spec = pl.BlockSpec((16, 4, 8, 128), lambda i: (0, 0, i, 0))
    return pl.pallas_call(
        forward_kernel,
        grid=(8,),
        in_specs=[
            pl.BlockSpec((64, 64), lambda i: (0, 0)),
            pl.BlockSpec((2, 2, 32, 128), lambda i: (i, 0, 0, 0)),
            pl.BlockSpec((2, 2, 1024, 128), lambda i: (i, 0, 0, 0)),
        ],
        out_specs=[spec, spec],
        out_shape=[panel, panel],
        compiler_params=pltpu.CompilerParams(vmem_limit_bytes=40 * 2**20),
        cost_estimate=pl.CostEstimate(flops=3 * 2**30, bytes_accessed=21 * 2**20, transcendentals=0),
        name="forward_panel",
    )(perm, focusing, reflection)


def source_kernel(th_ref, tl_ref, tth_ref, ttl_ref, mute_ref, x_ref, time_ref, spec_ref):
    cols = []
    for j in range(2):
        pieces = [
            x_ref[kb, pl.ds(ri * 2 + j, KK, stride=4), :] for kb in range(KB) for ri in range(2)
        ]
        cols.append(jnp.concatenate(pieces, axis=0))
    u = split(jnp.concatenate(cols, axis=1))
    up = mm3((th_ref[...], tl_ref[...]), u)
    t = lax.broadcasted_iota(jnp.int32, (NT, 128), 0)
    kept = []
    for j in range(2):
        mute = jnp.broadcast_to(mute_ref[j : j + 1, :], (NT, 128))
        val = jnp.where((t < mute) | (t > NT - mute), up[:, j * 128 : (j + 1) * 128], 0.0)
        time_ref[pl.ds(j, NT, stride=2), :] = val
        kept.append(val)
    w = split(jnp.concatenate(kept, axis=1))
    back = mm3((tth_ref[...], ttl_ref[...]), w)
    for j in range(2):
        for kb in range(KB):
            for ri in range(2):
                row = kb * 32 + ri * 16
                spec_ref[kb, pl.ds(ri * 2 + j, KK, stride=4), :] = back[
                    row : row + 16, j * 128 : (j + 1) * 128
                ]


def source_traces(tables, mute, x):
    return pl.pallas_call(
        source_kernel,
        out_shape=[
            jax.ShapeDtypeStruct((NT * 2, 128), F32),
            jax.ShapeDtypeStruct((KB, 64, 128), F32),
        ],
        compiler_params=pltpu.CompilerParams(vmem_limit_bytes=40 * 2**20),
        name="source_traces",
    )(*tables, mute, x)


def adjoint_kernel(own_ref, oth_ref, r_ref, out_ref):
    sub = lax.broadcasted_iota(jnp.int32, (64, 128), 0)
    lower = (sub % 8) < 4
    first = (sub % 4) < 2

    def swap4(v):
        return jnp.where(lower, pltpu.roll(v, 60, 0), pltpu.roll(v, 4, 0))

    acc = [None, None]
    for z in range(4):
        lhs = [[], []]
        for xh_ in range(2):
            own = own_ref[xh_ * 8 : (xh_ + 1) * 8, z, :, :].reshape(64, 128)
            oth = oth_ref[xh_ * 8 : (xh_ + 1) * 8, z, :, :].reshape(64, 128)
            lhs[0].append(jnp.where(lower, own, swap4(oth)))
            lhs[1].append(jnp.where(lower, swap4(own), oth))
        for q in range(2):
            bh, bl = split(jnp.concatenate(lhs[q], axis=1))
            rows = slice(z * 256, (z + 1) * 256)
            wh, wl = split(jnp.concatenate([r_ref[q, 0, rows, :], r_ref[q, 1, rows, :]], axis=1))
            both = mm(jnp.concatenate([bh, bl], axis=0), wh)
            add = both[:64] + (both[64:] + mm(bh, wl))
            acc[q] = add if acc[q] is None else acc[q] + add
    for q in range(2):
        p_, q_ = acc[q][:, :128], acc[q][:, 128:]
        res = p_ + jnp.where(first, pltpu.roll(q_, 62, 0), -pltpu.roll(q_, 2, 0))
        out_ref[:, q * 8 : (q + 1) * 8, :] = res.reshape(8, 8, 128)


def adjoint_panel(own, oth, reflection):
    spec = pl.BlockSpec((16, 4, 8, 128), lambda i: (0, 0, i, 0))
    return pl.pallas_call(
        adjoint_kernel,
        grid=(8,),
        in_specs=[spec, spec, pl.BlockSpec((2, 2, 1024, 128), lambda i: (i, 0, 0, 0))],
        out_specs=pl.BlockSpec((8, 16, 128), lambda i: (0, i, 0)),
        out_shape=jax.ShapeDtypeStruct((8, 128, 128), F32),
        compiler_params=pltpu.CompilerParams(vmem_limit_bytes=40 * 2**20),
        cost_estimate=pl.CostEstimate(flops=3 * 2**30, bytes_accessed=21 * 2**20, transcendentals=0),
        name="adjoint_panel",
    )(own, oth, reflection)


def receiver_kernel(core_ref, th_ref, tl_ref, mute_ref, direct_ref, x_ref, out_ref):
    even = core_ref[0] == 0
    t = lax.broadcasted_iota(jnp.int32, (NT, 128), 0)
    for c in range(2):
        cols = []
        for j in range(2):
            pieces = []
            for kb in range(KB):
                for ri in range(2):
                    a = x_ref[kb, pl.ds(c * 4 + ri * 2 + j, KK, stride=8), :]
                    b = x_ref[kb, pl.ds((1 - c) * 4 + ri * 2 + j, KK, stride=8), :]
                    pieces.append(jnp.where(even, a, b))
            cols.append(jnp.concatenate(pieces, axis=0))
        adj = mm3((th_ref[...], tl_ref[...]), split(jnp.concatenate(cols, axis=1)))
        for j in range(2):
            p = c * 2 + j
            mute = jnp.broadcast_to(mute_ref[p : p + 1, :], (NT, 128))
            val = jnp.where((t < mute) | (t > NT - mute), adj[:, j * 128 : (j + 1) * 128], 0.0)
            rows = pl.ds(p, NT, stride=4)
            out_ref[rows, :] = direct_ref[rows, :] - val


def receiver_traces(core, tables, mute, direct, x):
    vmem = pl.BlockSpec(memory_space=pltpu.VMEM)
    return pl.pallas_call(
        receiver_kernel,
        in_specs=[pl.BlockSpec(memory_space=pltpu.SMEM)] + [vmem] * 5,
        out_specs=vmem,
        out_shape=jax.ShapeDtypeStruct((NT * 4, 128), F32),
        compiler_params=pltpu.CompilerParams(vmem_limit_bytes=40 * 2**20),
        name="receiver_traces",
    )(core, *tables, mute, direct, x)


def body(reflection, focusing, direct_wave, mute_source, mute_receiver):
    core = lax.axis_index("c")
    table = dft_table()
    th, tl = split_const(table)
    row = lax.broadcasted_iota(jnp.int32, (64, 64), 0)
    col = lax.broadcasted_iota(jnp.int32, (64, 64), 1)
    crel, dev, ri, j = row // 32, (row // 4) % 8, (row // 2) % 2, row % 2
    perm = (col == ri * 32 + dev * 4 + ((crel + core) % 2) * 2 + j).astype(BF16)

    swap = [(0, 1), (1, 0)]
    around = ("xh", "xl", "y")
    own, oth = forward_panel(reflection, focusing, perm)
    panel = own + lax.ppermute(oth, "c", swap)
    parts = lax.all_to_all(panel, around, split_axis=0, concat_axis=0, tiled=True)
    summed = jnp.sum(parts.reshape(2, 8, 4, 64, 128), axis=1).transpose(1, 0, 2, 3)
    spectrum = lax.all_to_all(summed, "z", split_axis=0, concat_axis=0, tiled=True)
    time, back = source_traces((th, tl, th.T, tl.T), mute_source, spectrum.reshape(8, 64, 128))
    back = lax.all_to_all(back.reshape(4, 2, 64, 128), "z", split_axis=0, concat_axis=0, tiled=True)
    wide = jnp.broadcast_to(back.transpose(1, 0, 2, 3)[:, None], (2, 8, 4, 64, 128))
    b_own = lax.all_to_all(wide.reshape(16, 4, 64, 128), around, split_axis=0, concat_axis=0, tiled=True)
    b_oth = lax.ppermute(b_own, "c", swap)
    adjoint = adjoint_panel(b_own, b_oth, reflection)
    received = lax.all_to_all(adjoint, ("z", "xh"), split_axis=0, concat_axis=0, tiled=True)
    plus = receiver_traces(
        core.reshape(1), (th, tl), mute_receiver, direct_wave.reshape(NT * 4, 128), received
    )
    return time.reshape(NT, 2, 128), plus.reshape(NT, 4, 128)


def solution(mesh):
    fine = Mesh(mesh.devices.reshape(4, 2, 2, 4, 2), ("z", "xh", "xl", "y", "c"))
    freq, rcv = ("z", "xh"), ("xl", "y", "c")
    return jax.shard_map(
        body,
        mesh=fine,
        in_specs=(
            P(freq, None, None, rcv),
            P(freq, None, None, rcv),
            P(None, freq, rcv),
            P(rcv, freq),
            P(freq, rcv),
        ),
        out_specs=(P(None, rcv, freq), P(None, freq, rcv)),
        check_vma=False,
    )
```

time: 462 us -> 136 us (0.29); the launches traced: 456 us -> 135 us
  waiting for transfers between devices: 141 us -> 8.3 us
  matrix products: 84 us -> 0 us
  local copies, waits for them, and re-layouts: 71.9 us -> 1.34 us
  Pallas kernels: 0 us -> 24.5 us
  blocking collectives: 117 us -> 99.3 us
  other arithmetic: 16.8 us -> 0.74 us
  between operations: 14.6 us -> 0.78 us
  starting transfers between devices: 10.2 us -> 0.09 us
    psum x1 -> x0, waiting for transfers between devices: 132 us -> none  [body(): summed = lax.psum(term, 'rcv')]
    dot_general x14 -> x0, matrix products: 84 us -> none  [the longest x1 11.1 us: forward_panel(): jnp.einsum('ual,uel->eua', reflection_imaginary, focusing_input[:, 1], pr...]
    all_gather x1 -> x0, blocking collectives: 58.8 us -> none  [body(): mutes_all = lax.all_gather(mute_source, 'rcv', axis=0, tiled=True)]
    all_to_all x1 -> x5, blocking collectives: 58.4 us -> 99.3 us  [the longest x1 35.6 us: body(): lax.all_to_all(panel, around, split_axis=0, concat_axis=0, tiled=True)]
    unnamed x28 -> x16, local copies, waits for them, and re-layouts: 28.3 us -> 1.07 us
    all_to_all x5 -> x0, local copies, waits for them, and re-layouts: 24.8 us -> none  [the longest x2 14 us: body(): lax.all_to_all(summed, 'freq', split_axis=3, concat_axis=1, tiled=True)]
    pallas_call x0 -> x4, Pallas kernels: none -> 24.5 us  [the longest x1 11.7 us: forward_panel(): pl.pallas_call(forward_kernel, grid=(8,), in_specs=[pl.BlockSpec((64, 64)...]
    psum x1 -> x0, local copies, waits for them, and re-layouts: 14.3 us -> none  [body(): summed = lax.psum(term, 'rcv')]
  transfers between devices with their start and end apart: 3 -> 2, of which waited for: 2 -> 2; matrix products, arithmetic and copies ran while one was open for 0% -> 0% of each run, Pallas kernels for 0% -> 0%
where the time goes in v1:
time: 136 us; the launch traced here: 135 us
  blocking collectives  99.3 us (73%)
  Pallas kernels  24.5 us (18%)
  waiting for transfers between devices  8.3 us (6%)
    all_to_all x1, blocking collectives, body(): lax.all_to_all(panel, around, split_axis=0, concat_axis=0, tiled=True)  35.6 us
    all_to_all x1, blocking collectives, body(): lax.all_to_all(wide.reshape(16, 4, 64, 128), around, split_axis=0, concat...  28.2 us
    all_to_all x1, blocking collectives, body(): lax.all_to_all(adjoint, ('z', 'xh'), split_axis=0, concat_axis=0, tiled=T...  14.6 us
    all_to_all x1, blocking collectives, body(): lax.all_to_all(summed, 'z', split_axis=0, concat_axis=0, tiled=True)  11.9 us
    pallas_call x1, Pallas kernels, forward_panel(): pl.pallas_call(forward_kernel, grid=(8,), in_specs=[pl.BlockSpec((64, 64)...  11.7 us
    pallas_call x1, Pallas kernels, adjoint_panel(): pl.pallas_call(adjoint_kernel, grid=(8,), in_specs=[spec, spec, pl.BlockS...  10.3 us
    all_to_all x1, blocking collectives, body(): lax.all_to_all(back.reshape(4, 2, 64, 128), 'z', split_axis=0, concat_axi...  9.05 us
    ppermute x1, waiting for transfers between devices, body(): b_oth = lax.ppermute(b_own, 'c', swap)  4.16 us
  transfers between devices with their start and end apart: 2, of which 2 were waited for; matrix products, arithmetic and copies ran while one was open for 0% of the time, Pallas kernels for 0%

profile of v1, /device:TPU:0, one launch (start us, length us, event | category | flops | bytes accessed | tf_op | source)
XLA Modules:
  0.0 135.1 jit_solution(3915259029239048909)
XLA Ops:
  0.7 0.2 fusion.10.perm_ref
  0.9 0.0 copy-start
  0.9 1.0 copy-done
  1.9 11.7 %forward_panel.1 = (f32[16,4,64,128]{3,2,1,0:T(8,128)S(1)}, f32[16,4,64,128]{3,2,1,0:T(8,128)S(1)}) custom-call(bf16[64,64]{1,0:T(8,128)(2,1)S(1)} %fusion.10.perm_ref, f32[16,2,32,128]{3,2,1,0:T(8,128)S(1)} %copy-done, f32[16,2,1024,128]{3,2,1,0:T(8,128)} %r_ref.3), custom_call_target="tpu_custom_call" | custom-call | flops 3221225472 | bytes 22020096 | tf_op jit(solution)/shard_map/forward_panel/pallas_call | solution.py:70
  13.7 0.1 collective-permute-start
  13.7 4.1 %collective-permute-done = f32[16,4,64,128]{3,2,1,0:T(8,128)S(1)} collective-permute-done((f32[16,4,64,128]{3,2,1,0:T(8,128)S(1)}, f32[16,4,64,128]{3,2,1,0:T(8,128)S(1)}, u32[]{:S(2)}, u32[]{:S(2)}) %collective-permute-start) | collective-permute-done | bytes 2097184 | tf_op jit(solution)/shard_map/ppermute | solution.py:214
  17.9 0.4 add.52
  18.3 35.6 %all_to_all.25 = f32[16,4,64,128]{3,2,1,0:T(8,128)S(1)} all-to-all(f32[16,4,64,128]{3,2,1,0:T(8,128)S(1)} %add.52), channel_id=1, replica_groups=mesh['z'=4,'xh'=2,'xl'=2,'y'=4,'c'=2] {'xh','xl','y'}, dimensions={0} | all-to-all | bytes 4194304 | tf_op jit(solution)/shard_map/all_to_all | solution.py:215
  53.9 0.0 copy-start.2
  53.9 0.0 copy-start.3
  53.9 0.0 copy-start.4
  53.9 0.0 copy-start.5
  53.9 0.0 copy-start.7
  53.9 0.1 bitcast_reduce_fusion
  54.0 11.9 %all_to_all.26 = f32[4,2,64,128]{3,2,1,0:T(8,128)S(1)} all-to-all(f32[4,2,64,128]{3,2,1,0:T(8,128)S(1)} %copy.14), channel_id=1, replica_groups=mesh['z'=4,'xh'=2,'xl'=2,'y'=4,'c'=2] {'z'}, dimensions={0} | all-to-all | bytes 524288 | tf_op jit(solution)/shard_map/all_to_all | solution.py:217
  66.0 0.0 copy-done.2
  66.0 0.0 copy-done.3
  66.0 0.0 copy-done.4
  66.0 0.0 copy-done.5
  66.0 0.0 copy-done.7
  66.0 1.2 source_traces.1
  67.2 9.1 %all_to_all.27 = f32[4,2,64,128]{3,2,1,0:T(8,128)S(1)} all-to-all(f32[4,2,64,128]{3,2,1,0:T(8,128)S(1)} %bitcast.13), channel_id=1, replica_groups=mesh['z'=4,'xh'=2,'xl'=2,'y'=4,'c'=2] {'z'}, dimensions={0} | all-to-all | bytes 524288 | tf_op jit(solution)/shard_map/all_to_all | solution.py:219
  76.3 0.2 broadcast_in_dim.2
  76.5 28.2 %all_to_all.28.own_ref = f32[16,4,64,128]{3,2,1,0:T(8,128)S(1)} all-to-all(f32[16,4,64,128]{3,2,1,0:T(8,128)S(1)} %bitcast.14), channel_id=1, replica_groups=mesh['z'=4,'xh'=2,'xl'=2,'y'=4,'c'=2] {'xh','xl','y'}, dimensions={0} | all-to-all | bytes 4194304 | tf_op jit(solution)/shard_map/all_to_all | solution.py:221
  104.7 0.0 copy-start.1
  104.7 0.0 copy-start.6
  104.7 0.0 collective-permute-start.1
  104.7 4.2 %collective-permute-done.1.oth_ref = f32[16,4,64,128]{3,2,1,0:T(8,128)S(1)} collective-permute-done((f32[16,4,64,128]{3,2,1,0:T(8,128)S(1)}, f32[16,4,64,128]{3,2,1,0:T(8,128)S(1)}, u32[]{:S(2)}, u32[]{:S(2)}) %collective-permute-start.1) | collective-permute-done | bytes 2097184 | tf_op jit(solution)/shard_map/ppermute | solution.py:222
  108.8 10.3 %adjoint_panel.1 = f32[8,128,128]{2,1,0:T(8,128)S(1)} custom-call(f32[16,4,64,128]{3,2,1,0:T(8,128)S(1)} %all_to_all.28.own_ref, f32[16,4,64,128]{3,2,1,0:T(8,128)S(1)} %collective-permute-done.1.oth_ref, f32[16,2,1024,128]{3,2,1,0:T(8,128)} %r_ref.3), custom_call_target="tpu_custom_call" | custom-call | flops 3221225472 | bytes 22020096 | tf_op jit(solution)/shard_map/adjoint_panel/pallas_call | solution.py:156
  119.1 14.6 %all_to_all.29.x_ref = f32[8,128,128]{2,1,0:T(8,128)S(1)} all-to-all(f32[8,128,128]{2,1,0:T(8,128)S(1)} %adjoint_panel.1), channel_id=1, replica_groups=mesh['z'=4,'xh'=2,'xl'=2,'y'=4,'c'=2] {'z','xh'}, dimensions={0} | all-to-all | bytes 1048576 | tf_op jit(solution)/shard_map/all_to_all | solution.py:224
  133.8 0.0 copy-done.1
  133.8 0.0 copy-done.6
  133.8 1.3 receiver_traces.1
  (8 shorter events, 0.1 us)
Async XLA Ops:
  0.9 1.0 copy-start
  13.7 4.2 %collective-permute-start = (f32[16,4,64,128]{3,2,1,0:T(8,128)S(1)}, f32[16,4,64,128]{3,2,1,0:T(8,128)S(1)}, u32[]{:S(2)}, u32[]{:S(2)}) collective-permute-start(f32[16,4,64,128]{3,2,1,0:T(8,128)S(1)} %get-tuple-element.7), channel_id=1, source_target_pairs={{0,1},{1,0},{2,3},{3,2},{4,5},{5,4},{6,7},{7,6},{8,9},{9,8},{10,11... | collective-permute-start | bytes 6291464 | tf_op jit(solution)/shard_map/ppermute | solution.py:214
  53.9 12.1 %copy-start.2 = (bf16[256,256]{1,0:T(8,128)(2,1)S(1)}, bf16[256,256]{1,0:T(8,128)(2,1)}, u32[]{:S(2)}) copy-start(bf16[256,256]{1,0:T(8,128)(2,1)} %constant.97.clone.tl_ref) | copy-start | bytes 393220
  53.9 12.1 %copy-start.3 = (bf16[256,256]{1,0:T(8,128)(2,1)S(1)}, bf16[256,256]{1,0:T(8,128)(2,1)}, u32[]{:S(2)}) copy-start(bf16[256,256]{1,0:T(8,128)(2,1)} %constant.96.clone.th_ref) | copy-start | bytes 393220
  53.9 12.1 %copy-start.4 = (bf16[256,256]{1,0:T(8,128)(2,1)S(1)}, bf16[256,256]{1,0:T(8,128)(2,1)}, u32[]{:S(2)}) copy-start(bf16[256,256]{1,0:T(8,128)(2,1)} %constant.99.clone.ttl_ref) | copy-start | bytes 393220
  53.9 12.1 %copy-start.5 = (bf16[256,256]{1,0:T(8,128)(2,1)S(1)}, bf16[256,256]{1,0:T(8,128)(2,1)}, u32[]{:S(2)}) copy-start(bf16[256,256]{1,0:T(8,128)(2,1)} %constant.98.clone.tth_ref) | copy-start | bytes 393220
  53.9 12.1 %copy-start.7 = (s32[2,128]{1,0:T(2,128)S(1)}, s32[2,128]{1,0:T(2,128)}, u32[]{:S(2)}) copy-start(s32[2,128]{1,0:T(2,128)} %mute_ref.2) | copy-start | bytes 3076
  104.7 29.1 %copy-start.1 = (f32[256,4,128]{2,1,0:T(4,128)S(1)}, f32[256,4,128]{2,1,0:T(4,128)}, u32[]{:S(2)}) copy-start(f32[256,4,128]{2,1,0:T(4,128)} %param.11) | copy-start | bytes 1572868
  104.7 29.1 %copy-start.6 = (s32[4,128]{1,0:T(4,128)S(1)}, s32[4,128]{1,0:T(4,128)}, u32[]{:S(2)}) copy-start(s32[4,128]{1,0:T(4,128)} %mute_ref.3) | copy-start | bytes 6148
  104.7 4.2 %collective-permute-start.1 = (f32[16,4,64,128]{3,2,1,0:T(8,128)S(1)}, f32[16,4,64,128]{3,2,1,0:T(8,128)S(1)}, u32[]{:S(2)}, u32[]{:S(2)}) collective-permute-start(f32[16,4,64,128]{3,2,1,0:T(8,128)S(1)} %all_to_all.28.own_ref), channel_id=1, source_target_pairs={{0,1},{1,0},{2,3},{3,2},{4,5},{5,4},{6,7},{7,6},{8,9},{9,8},{10,11... | collective-permute-start | bytes 6291464 | tf_op jit(solution)/shard_map/ppermute | solution.py:222

commit v2 on v1

v2 whole, which is shorter than its diff:
```python
import functools
import math

import numpy as np
import jax
import jax.numpy as jnp
from jax import lax
from jax.experimental import pallas as pl
from jax.experimental.pallas import tpu as pltpu
from jax.sharding import Mesh, PartitionSpec as P

F32, BF16 = jnp.float32, jnp.bfloat16
NT = 256
KB, KK = 8, 16
VMEM = pl.BlockSpec(memory_space=pltpu.VMEM)
SMEM = pl.BlockSpec(memory_space=pltpu.SMEM)
HBM = pl.BlockSpec(memory_space=pltpu.HBM)


def dft_table():
    k = np.arange(1, KB * KK + 1)[None, :]
    t = np.arange(NT)[:, None]
    phase = 2.0 * math.pi * ((k * t) % NT) / NT
    c = 1.0 / math.sqrt(KB * KK)
    return np.stack([c * np.cos(phase), -c * np.sin(phase)], axis=2).reshape(NT, NT)


def split_const(table):
    high = table.astype(np.float32).astype(jnp.bfloat16)
    low = (table - high.astype(np.float64)).astype(np.float32).astype(jnp.bfloat16)
    return np.asarray(high), np.asarray(low)


def split(x):
    high = x.astype(BF16)
    return high, (x - high.astype(F32)).astype(BF16)


def mm(a, b, contract=(1, 0)):
    return lax.dot_general(a, b, (((contract[0],), (contract[1],)), ((), ())), preferred_element_type=F32)


def mm3(a, b):
    return mm(a[0], b[0]) + (mm(a[0], b[1]) + mm(a[1], b[0]))


def params(mib):
    return pltpu.CompilerParams(vmem_limit_bytes=mib * 2**20)


def trade(v, pair, shift):
    t = v[(0 - shift) % 4]
    for m in range(1, 4):
        t = jnp.where(pair == m, v[(m - shift) % 4], t)
    return t


def unturn(x, y, sign):
    out = x
    for s in range(1, 4):
        out = jnp.where(y == s, pltpu.roll(x, (sign * 2 * s) % 8, 1), out)
    return out


def fetch_piece(r_hbm, r_ref, sem, g, z):
    cut = (pl.ds(g * 4, 4), slice(None), pl.ds(z * 256, 256))
    return pltpu.make_async_copy(r_hbm.at[cut], r_ref.at[cut], sem.at[g * 4 + z])


def forward_kernel(core_ref, f_hbm, r_hbm, own0, own1, oth0, oth1, f_ref, r_ref, fsem, sem):
    outs = (own0, own1, oth0, oth1)

    fetch = functools.partial(fetch_piece, r_hbm, r_ref, sem)
    fcopy = pltpu.make_async_copy(f_hbm, f_ref, fsem)
    fcopy.start()
    for g in range(4):
        for z in range(4):
            fetch(g, z).start()
    core = core_ref[0]
    row = lax.broadcasted_iota(jnp.int32, (64, 64), 0)
    col = lax.broadcasted_iota(jnp.int32, (64, 64), 1)
    perms = []
    for q in range(4):
        c = (row // 32 + core) % 2
        y = ((row // 2) % 4 + 4 - q) % 4
        src = (row % 2) * 32 + ((row // 8) % 2) * 16 + y * 4 + c * 2 + (row // 16) % 2
        perms.append(jnp.where(col == src, 1.0, 0.0).astype(BF16))
    pair = lax.broadcasted_iota(jnp.int32, (8, 128), 0) // 2
    fcopy.wait()

    @pl.loop(0, 4)
    def _(g):
        lhs = []
        for q in range(4):
            fr, fi = f_ref[g * 4 + q, 0], f_ref[g * 4 + q, 1]
            x = jnp.concatenate(
                [jnp.concatenate([fr, -fi], axis=1), jnp.concatenate([fi, fr], axis=1)], axis=0
            )
            xh, xl = split(x)
            ph, plo = mm(perms[q], xh).astype(BF16), mm(perms[q], xl).astype(BF16)
            lhs.append((ph, jnp.concatenate([ph, plo], axis=0)))
        g8 = pl.ds(pl.multiple_of(g * 8, 8), 8)
        for z in range(4):
            fetch(g, z).wait()
            rows = slice(z * 256, (z + 1) * 256)
            res = []
            for q in range(4):
                k = g * 4 + q
                wh, wl = split(jnp.concatenate([r_ref[k, 0, rows, :], r_ref[k, 1, rows, :]], axis=1))
                acc = mm(lhs[q][1], wh, (1, 1))
                res.append(acc[:64] + (acc[64:] + mm(lhs[q][0], wl, (1, 1))))
            for xh_ in range(2):
                for part in range(8):
                    v = [r[part * 8 : part * 8 + 8, xh_ * 128 : xh_ * 128 + 128] for r in res]
                    out, xlo = outs[part // 2], part % 2
                    for y in range(4):
                        out[xh_ * 8 + xlo * 4 + y, z, g8, :] = trade(v, pair, y)


def forward_panel(core, focusing, reflection):
    panel = jax.ShapeDtypeStruct((16, 4, 32, 128), F32)
    return pl.pallas_call(
        forward_kernel,
        in_specs=[SMEM, HBM, HBM],
        out_specs=[VMEM] * 4,
        out_shape=[panel] * 4,
        scratch_shapes=[
            pltpu.VMEM((KK, 2, 32, 128), F32),
            pltpu.VMEM((KK, 2, 1024, 128), F32),
            pltpu.SemaphoreType.DMA,
            pltpu.SemaphoreType.DMA((16,)),
        ],
        compiler_params=params(24),
        cost_estimate=pl.CostEstimate(flops=3 * 2**30, bytes_accessed=21 * 2**20, transcendentals=0),
        name="forward_panel",
    )(core, focusing, reflection)


def sum_kernel(pos_ref, x_ref, o0, o1, o2, o3):
    z = pos_ref[0]
    for d, out in enumerate((o0, o1, o2, o3)):
        zz = lax.rem(z + d, 4)
        for h in range(2):
            t = [x_ref[h * 8 + i, zz] for i in range(8)]
            out[h] = ((t[0] + t[1]) + (t[2] + t[3])) + ((t[4] + t[5]) + (t[6] + t[7]))


def sum_parts(pos, parts):
    piece = jax.ShapeDtypeStruct((2, 32, 128), F32)
    return pl.pallas_call(
        sum_kernel,
        in_specs=[SMEM, VMEM],
        out_specs=[VMEM] * 4,
        out_shape=[piece] * 4,
        compiler_params=params(4),
        name="sum_parts",
    )(pos, parts)


def source_kernel(j, pos_ref, th_ref, tl_ref, tth_ref, ttl_ref, mute_ref, x0, x1, x2, x3, *rest):
    time_ref, b0, b1, b2, b3, tmp = rest[-6:]
    z, y = pos_ref[0], pos_ref[1]
    for d, x in enumerate((x0, x1, x2, x3)):
        src = lax.rem(z + 4 - d, 4)
        tmp[src] = unturn(x[...].reshape(8, 8, 128), y, -1).reshape(2, 32, 128)
    up = mm3((th_ref[...], tl_ref[...]), split(tmp[...].reshape(256, 128)))
    t = lax.broadcasted_iota(jnp.int32, (NT, 128), 0)
    mute = jnp.broadcast_to(mute_ref[j : j + 1, :], (NT, 128))
    val = jnp.where((t < mute) | (t > NT - mute), up, 0.0)
    time_ref[pl.ds(j, NT, stride=2), :] = val
    if j == 1:
        time_ref[pl.ds(0, NT, stride=2), :] = rest[0][...]
    back = mm3((tth_ref[...], ttl_ref[...]), split(val))
    tmp[...] = unturn(back.reshape(32, 8, 128), y, 1).reshape(4, 2, 32, 128)
    for d, out in enumerate((b0, b1, b2, b3)):
        out[...] = tmp[lax.rem(z + d, 4)]


def source_traces(j, pos, tables, mute, pieces, first):
    piece = jax.ShapeDtypeStruct((2, 32, 128), F32)
    time = jax.ShapeDtypeStruct((NT * 2, 128), F32)
    if j == 0:
        kernel, extra, shape = functools.partial(source_first, source_kernel), (), (NT, 128)
        time = jax.ShapeDtypeStruct(shape, F32)
    else:
        kernel, extra = functools.partial(source_kernel, 1), (first,)
    return pl.pallas_call(
        kernel,
        in_specs=[SMEM] + [VMEM] * (9 + len(extra)),
        out_specs=[VMEM] * 5,
        out_shape=[time] + [piece] * 4,
        scratch_shapes=[pltpu.VMEM((4, 2, 32, 128), F32)],
        compiler_params=params(8),
        name=f"source_traces{j}",
    )(pos, *tables, mute, *pieces, *extra)


class _Rows:
    def __init__(self, ref):
        self.ref = ref

    def __setitem__(self, index, value):
        self.ref[...] = value


def source_first(kernel, *refs):
    refs = list(refs)
    refs[-6] = _Rows(refs[-6])
    kernel(0, *refs)


def spread_kernel(pos_ref, x0, x1, x2, x3, out_ref):
    z = pos_ref[0]
    for d, x in enumerate((x0, x1, x2, x3)):
        src = lax.rem(z + 4 - d, 4)
        for h in range(2):
            val = x[h]
            for i in range(8):
                out_ref[h * 8 + i, src] = val


def spread(pos, pieces):
    return pl.pallas_call(
        spread_kernel,
        in_specs=[SMEM] + [VMEM] * 4,
        out_specs=VMEM,
        out_shape=jax.ShapeDtypeStruct((16, 4, 32, 128), F32),
        compiler_params=params(4),
        name="spread",
    )(pos, *pieces)


def adjoint_kernel(o0, o1, t0, t1, r_hbm, out_ref, r_ref, sem):
    fetch = functools.partial(fetch_piece, r_hbm, r_ref, sem)
    for g in range(4):
        for z in range(4):
            fetch(g, z).start()
    pair = lax.broadcasted_iota(jnp.int32, (8, 128), 0) // 2
    even = (lax.broadcasted_iota(jnp.int32, (64, 128), 0) % 2) == 0

    @pl.loop(0, 4)
    def _(g):
        g8 = pl.ds(pl.multiple_of(g * 8, 8), 8)
        acc = [None] * 4
        for z in range(4):
            lhs = [[None] * 2 for _ in range(4)]
            for xh_ in range(2):
                tiles = [[] for _ in range(4)]
                for ref in (o0, t0, o1, t1):
                    for xlo in range(2):
                        v = [ref[xh_ * 8 + xlo * 4 + y, z, g8, :] for y in range(4)]
                        for q in range(4):
                            tiles[q].append(trade(v, pair, q))
                for q in range(4):
                    lhs[q][xh_] = jnp.concatenate(tiles[q], axis=0)
            rows = slice(z * 256, (z + 1) * 256)
            fetch(g, z).wait()
            for q in range(4):
                k = g * 4 + q
                bh, bl = split(jnp.concatenate(lhs[q], axis=1))
                wh, wl = split(jnp.concatenate([r_ref[k, 0, rows, :], r_ref[k, 1, rows, :]], axis=1))
                both = mm(jnp.concatenate([bh, bl], axis=0), wh)
                add = both[:64] + (both[64:] + mm(bh, wl))
                acc[q] = add if acc[q] is None else acc[q] + add
        res = []
        for q in range(4):
            a, b = acc[q][:, :128], acc[q][:, 128:]
            res.append(a + jnp.where(even, pltpu.roll(b, 63, 0), -pltpu.roll(b, 1, 0)))
        for part in range(8):
            v = [r[part * 8 : part * 8 + 8] for r in res]
            for y in range(4):
                out_ref[(part % 2) * 4 + y, part // 2, g8, :] = trade(v, pair, y)


def adjoint_panel(own, oth, reflection):
    return pl.pallas_call(
        adjoint_kernel,
        in_specs=[VMEM] * 4 + [HBM],
        out_specs=VMEM,
        out_shape=jax.ShapeDtypeStruct((8, 4, 32, 128), F32),
        scratch_shapes=[pltpu.VMEM((KK, 2, 1024, 128), F32), pltpu.SemaphoreType.DMA((16,))],
        compiler_params=params(24),
        cost_estimate=pl.CostEstimate(flops=3 * 2**30, bytes_accessed=21 * 2**20, transcendentals=0),
        name="adjoint_panel",
    )(*own, *oth, reflection)


def receiver_kernel(pos_ref, th_ref, tl_ref, mute_ref, direct_ref, x_ref, out_ref):
    even = pos_ref[2] == 0
    turn = pos_ref[3]
    t = lax.broadcasted_iota(jnp.int32, (NT, 128), 0)
    for c in range(2):
        cols = []
        for j in range(2):
            a = jnp.where(even, x_ref[:, j * 2 + c], x_ref[:, j * 2 + 1 - c])
            cols.append(unturn(a.reshape(32, 8, 128), turn, -1).reshape(256, 128))
        adj = mm3((th_ref[...], tl_ref[...]), split(jnp.concatenate(cols, axis=1)))
        for j in range(2):
            p = c * 2 + j
            mute = jnp.broadcast_to(mute_ref[p : p + 1, :], (NT, 128))
            val = jnp.where((t < mute) | (t > NT - mute), adj[:, j * 128 : (j + 1) * 128], 0.0)
            rows = pl.ds(p, NT, stride=4)
            out_ref[rows, :] = direct_ref[rows, :] - val


def receiver_traces(pos, tables, mute, direct, x):
    return pl.pallas_call(
        receiver_kernel,
        in_specs=[SMEM] + [VMEM] * 5,
        out_specs=VMEM,
        out_shape=jax.ShapeDtypeStruct((NT * 4, 128), F32),
        compiler_params=params(8),
        name="receiver_traces",
    )(pos, *tables, mute, direct, x)


AROUND = ("xh", "xl", "y")
SWAP = [(0, 1), (1, 0)]


def exchange_xy(x):
    return lax.all_to_all(x, AROUND, split_axis=0, concat_axis=0, tiled=True)


def exchange_z(pieces):
    moved = [lax.ppermute(pieces[d], "z", [(i, (i + d) % 4) for i in range(4)]) for d in range(1, 4)]
    return [pieces[0]] + moved


def body(reflection, focusing, direct_wave, mute_source, mute_receiver):
    core, z, y = lax.axis_index("c"), lax.axis_index("z"), lax.axis_index("y")
    pos = jnp.stack([z, y, core, (z % 2) * 2 + lax.axis_index("xh")])
    table = dft_table()
    th, tl = split_const(table)

    focusing = pltpu.with_memory_space_constraint(focusing, pltpu.HBM)
    reflection = pltpu.with_memory_space_constraint(reflection, pltpu.HBM)
    own0, own1, oth0, oth1 = forward_panel(core.reshape(1), focusing, reflection)
    chains = []
    for own, oth in ((own0, oth0), (own1, oth1)):
        panel = own + lax.ppermute(oth, "c", SWAP)
        chains.append(exchange_z(sum_parts(pos, exchange_xy(panel))))
    time, b_own, b_oth = None, [], []
    for j in range(2):
        time, *back = source_traces(j, pos, (th, tl, th.T, tl.T), mute_source, chains[j], time)
        b_own.append(exchange_xy(spread(pos, exchange_z(back))))
        b_oth.append(lax.ppermute(b_own[j], "c", SWAP))
    adjoint = adjoint_panel(b_own, b_oth, reflection)
    received = lax.all_to_all(adjoint, ("z", "xh"), split_axis=0, concat_axis=0, tiled=True)
    plus = receiver_traces(pos, (th, tl), mute_receiver, direct_wave.reshape(NT * 4, 128), received)
    return time.reshape(NT, 2, 128), plus.reshape(NT, 4, 128)


def solution(mesh):
    fine = Mesh(mesh.devices.reshape(4, 2, 2, 4, 2), ("z", "xh", "xl", "y", "c"))
    freq, rcv = ("z", "xh"), ("xl", "y", "c")
    return jax.shard_map(
        body,
        mesh=fine,
        in_specs=(
            P(freq, None, None, rcv),
            P(freq, None, None, rcv),
            P(None, freq, rcv),
            P(rcv, freq),
            P(freq, rcv),
        ),
        out_specs=(P(None, rcv, freq), P(None, freq, rcv)),
        check_vma=False,
    )
```

time: 136 us -> 143 us (1.051)
  blocking collectives: 99.3 us -> 15 us
  starting transfers between devices: 0.09 us -> 45.2 us
  waiting for transfers between devices: 8.3 us -> 46.8 us
  Pallas kernels: 24.5 us -> 30.8 us
  other arithmetic: 0.74 us -> 3.72 us
    all_to_all x4 -> x0, blocking collectives: 84.7 us -> none  [the longest x1 35.6 us: body(): lax.all_to_all(panel, around, split_axis=0, concat_axis=0, tiled=True)]
    all_to_all x0 -> x4, waiting for transfers between devices: none -> 28.5 us  [exchange_xy(): return lax.all_to_all(x, AROUND, split_axis=0, concat_axis=0, tiled=True)]
    all_to_all x0 -> x4, starting transfers between devices: none -> 25.5 us  [exchange_xy(): return lax.all_to_all(x, AROUND, split_axis=0, concat_axis=0, tiled=True)]
    ppermute x2 -> x16, starting transfers between devices: 0.09 us -> 19.6 us  [the longest x12 18.9 us: exchange_z(): lax.ppermute(pieces[d], 'z', [(i, (i + d) % 4) for i in range(4)])]
    ppermute x2 -> x16, waiting for transfers between devices: 8.3 us -> 18.3 us  [the longest x12 12.9 us: exchange_z(): lax.ppermute(pieces[d], 'z', [(i, (i + d) % 4) for i in range(4)])]
    pallas_call x4 -> x9, Pallas kernels: 24.5 us -> 30.8 us  [the longest x1 15.3 us: forward_panel(): pl.pallas_call(forward_kernel, in_specs=[SMEM, HBM, HBM], out_specs=[VMEM...]
    add x2, other arithmetic: 0.4 us -> 3.64 us  [body(): panel = own + lax.ppermute(oth, 'c', SWAP)]
  transfers between devices with their start and end apart: 2 -> 20, of which waited for: 2 -> 15; matrix products, arithmetic and copies ran while one was open for 0% -> 3% of each run, Pallas kernels for 0% -> 5%
where the time goes in v2:
time: 143 us; the launch traced here: 142 us
  waiting for transfers between devices  46.8 us (33%)
  starting transfers between devices  45.2 us (32%)
  Pallas kernels  30.8 us (22%)
  blocking collectives  15 us (10%)
  other arithmetic  3.72 us (3%)
    all_to_all x4, waiting for transfers between devices, exchange_xy(): return lax.all_to_all(x, AROUND, split_axis=0, concat_axis=0, tiled=True)  28.5 us
    all_to_all x4, starting transfers between devices, exchange_xy(): return lax.all_to_all(x, AROUND, split_axis=0, concat_axis=0, tiled=True)  25.5 us
    ppermute x12, starting transfers between devices, exchange_z(): lax.ppermute(pieces[d], 'z', [(i, (i + d) % 4) for i in range(4)])  18.9 us
    pallas_call x1, Pallas kernels, forward_panel(): pl.pallas_call(forward_kernel, in_specs=[SMEM, HBM, HBM], out_specs=[VMEM...  15.3 us
    all_to_all x1, blocking collectives, body(): lax.all_to_all(adjoint, ('z', 'xh'), split_axis=0, concat_axis=0, tiled=T...  15 us
    ppermute x12, waiting for transfers between devices, exchange_z(): lax.ppermute(pieces[d], 'z', [(i, (i + d) % 4) for i in range(4)])  12.9 us
    pallas_call x1, Pallas kernels, adjoint_panel(): pl.pallas_call(adjoint_kernel, in_specs=[VMEM] * 4 + [HBM], out_specs=VME...  6.3 us
    add x2, other arithmetic, body(): panel = own + lax.ppermute(oth, 'c', SWAP)  3.64 us
  transfers between devices with their start and end apart: 20, of which 15 were waited for; matrix products, arithmetic and copies ran while one was open for 3% of the time, Pallas kernels for 5%

profile of v2, /device:TPU:0, one launch (start us, length us, event | category | flops | bytes accessed | tf_op | source)
XLA Modules:
  0.0 142.3 jit_solution(1514197897681153785)
XLA Ops:
  0.6 0.0 copy-start.1
  0.7 15.3 %forward_panel.1 = (f32[16,4,32,128]{3,2,1,0:T(8,128)S(1)}, f32[16,4,32,128]{3,2,1,0:T(8,128)S(1)}, f32[16,4,32,128]{3,2,1,0:T(8,128)S(1)}, f32[16,4,32,128]{3,2,1,0:T(8,128)}) custom-call(s32[1]{0:T(128)} %bitcast.2.core_ref, f32[16,2,32,128]{3,2,1,0:T(8,128)} %f_hbm.1, f32[16,2,1024,128]{3,2,1,0:T(8,128)} %r_hbm.3), custom_call_target="tpu_custom_call" | custom-call | flops 3221225472 | bytes 22020096 | tf_op jit(solution)/shard_map/forward_panel/pallas_call | solution.py:122
  16.0 0.1 collective-permute-start.4
  16.1 0.5 collective-permute-start
  16.6 2.7 %collective-permute-done.4 = f32[16,4,32,128]{3,2,1,0:T(8,128)S(1)} collective-permute-done((f32[16,4,32,128]{3,2,1,0:T(8,128)S(1)}, f32[16,4,32,128]{3,2,1,0:T(8,128)S(1)}, u32[]{:S(2)}, u32[]{:S(2)}) %collective-permute-start.4) | collective-permute-done | bytes 1048608 | tf_op jit(solution)/shard_map/ppermute | solution.py:341
  19.3 1.2 add.16
  20.5 7.1 %all-to-all-start.1 = ((f32[16,4,32,128]{3,2,1,0:T(8,128)}), f32[16,4,32,128]{3,2,1,0:T(8,128)S(1)}, u32[]{:S(2)}, u32[]{:S(2)}) async-start(f32[16,4,32,128]{3,2,1,0:T(8,128)} %add.16), calls=%async_computation.1 | async-start | bytes 2097152 | tf_op jit(solution)/shard_map/all_to_all | solution.py:322
  27.6 2.4 %add.15 = f32[16,4,32,128]{3,2,1,0:T(8,128)} add(f32[16,4,32,128]{3,2,1,0:T(8,128)S(1)} %get-tuple-element.24, f32[16,4,32,128]{3,2,1,0:T(8,128)} %collective-permute-done) | non-fusion elementwise | flops 262144 | bytes 3145728 | tf_op jit(solution)/shard_map/add | solution.py:341
  30.1 15.7 %all-to-all-done.1.x_ref = f32[16,4,32,128]{3,2,1,0:T(8,128)S(1)} async-done(((f32[16,4,32,128]{3,2,1,0:T(8,128)}), f32[16,4,32,128]{3,2,1,0:T(8,128)S(1)}, u32[]{:S(2)}, u32[]{:S(2)}) %all-to-all-start.1) | async-done | bytes 1048608 | tf_op jit(solution)/shard_map/all_to_all | solution.py:322
  45.7 3.7 %all-to-all-start = ((f32[16,4,32,128]{3,2,1,0:T(8,128)}), f32[16,4,32,128]{3,2,1,0:T(8,128)S(1)}, u32[]{:S(2)}, u32[]{:S(2)}) async-start(f32[16,4,32,128]{3,2,1,0:T(8,128)} %add.15), calls=%async_computation | async-start | bytes 2097152 | tf_op jit(solution)/shard_map/all_to_all | solution.py:322
  49.4 0.1 pad_add_fusion.pos_ref.refs_0_
  49.5 0.6 sum_parts.3
  50.1 2.0 %collective-permute-start.5 = (f32[2,32,128]{2,1,0:T(8,128)S(1)}, f32[2,32,128]{2,1,0:T(8,128)S(1)}, u32[]{:S(2)}, u32[]{:S(2)}) collective-permute-start(f32[2,32,128]{2,1,0:T(8,128)S(1)} %get-tuple-element.33), channel_id=1, source_target_pairs={{0,32},{32,64},{64,96},{96,0},{1,33},{33,65},{65,97},{97,1},{2,34}... | collective-permute-start | bytes 98312 | tf_op jit(solution)/shard_map/ppermute | solution.py:326
  52.1 3.6 %collective-permute-start.6 = (f32[2,32,128]{2,1,0:T(8,128)S(1)}, f32[2,32,128]{2,1,0:T(8,128)S(1)}, u32[]{:S(2)}, u32[]{:S(2)}) collective-permute-start(f32[2,32,128]{2,1,0:T(8,128)S(1)} %get-tuple-element.34), channel_id=1, source_target_pairs={{0,64},{32,96},{64,0},{96,32},{1,65},{33,97},{65,1},{97,33},{2,66}... | collective-permute-start | bytes 98312 | tf_op jit(solution)/shard_map/ppermute | solution.py:326
  55.7 1.0 collective-permute-start.7
  56.7 1.2 collective-permute-done.6.refs_8_
  57.9 1.7 %collective-permute-done.7.refs_9_ = f32[2,32,128]{2,1,0:T(8,128)S(1)} collective-permute-done((f32[2,32,128]{2,1,0:T(8,128)S(1)}, f32[2,32,128]{2,1,0:T(8,128)S(1)}, u32[]{:S(2)}, u32[]{:S(2)}) %collective-permute-start.7) | collective-permute-done | bytes 32800 | tf_op jit(solution)/shard_map/ppermute | solution.py:326
  59.6 1.2 source_traces0.1
  60.8 0.1 collective-permute-start.8
  60.9 3.7 %collective-permute-start.9 = (f32[2,32,128]{2,1,0:T(8,128)S(1)}, f32[2,32,128]{2,1,0:T(8,128)S(1)}, u32[]{:S(2)}, u32[]{:S(2)}) collective-permute-start(f32[2,32,128]{2,1,0:T(8,128)S(1)} %get-tuple-element.40), channel_id=1, source_target_pairs={{0,64},{32,96},{64,0},{96,32},{1,65},{33,97},{65,1},{97,33},{2,66}... | collective-permute-start | bytes 98312 | tf_op jit(solution)/shard_map/ppermute | solution.py:326
  64.5 0.5 collective-permute-start.10
  65.0 1.0 collective-permute-done.8.x1
  66.0 0.8 collective-permute-done.9.x2
  66.8 1.7 %collective-permute-done.10.x3 = f32[2,32,128]{2,1,0:T(8,128)S(1)} collective-permute-done((f32[2,32,128]{2,1,0:T(8,128)S(1)}, f32[2,32,128]{2,1,0:T(8,128)S(1)}, u32[]{:S(2)}, u32[]{:S(2)}) %collective-permute-start.10) | collective-permute-done | bytes 32800 | tf_op jit(solution)/shard_map/ppermute | solution.py:326
  68.4 1.6 %spread.2 = f32[16,4,32,128]{3,2,1,0:T(8,128)} custom-call(s32[4]{0:T(128)S(1)} %pad_add_fusion.pos_ref.refs_0_, f32[2,32,128]{2,1,0:T(8,128)S(1)} %get-tuple-element.38.x0, f32[2,32,128]{2,1,0:T(8,128)S(1)} %collective-permute-done.8.x1, f32[2,32,128]{2,1,0:T(8,128)S(1)} %collective-permute-done.9.x2, f32[2,32,128]{2,1,0:T(8,128)S(1)} %collective-permute-done.10.x3), custom_call_target="tpu_custom_call" | custom-call | tf_op jit(solution)/shard_map/spread/pallas_call | solution.py:223
  70.0 7.2 %all-to-all-start.2 = ((f32[16,4,32,128]{3,2,1,0:T(8,128)}), f32[16,4,32,128]{3,2,1,0:T(8,128)S(1)}, u32[]{:S(2)}, u32[]{:S(2)}) async-start(f32[16,4,32,128]{3,2,1,0:T(8,128)} %spread.2), calls=%async_computation.2 | async-start | bytes 2097152 | tf_op jit(solution)/shard_map/all_to_all | solution.py:322
  77.2 0.6 sum_parts.2
  77.8 0.5 collective-permute-start.1
  78.3 2.7 %collective-permute-start.2 = (f32[2,32,128]{2,1,0:T(8,128)S(1)}, f32[2,32,128]{2,1,0:T(8,128)S(1)}, u32[]{:S(2)}, u32[]{:S(2)}) collective-permute-start(f32[2,32,128]{2,1,0:T(8,128)S(1)} %get-tuple-element.28), channel_id=1, source_target_pairs={{0,64},{32,96},{64,0},{96,32},{1,65},{33,97},{65,1},{97,33},{2,66}... | collective-permute-start | bytes 98312 | tf_op jit(solution)/shard_map/ppermute | solution.py:326
  81.0 1.0 collective-permute-start.3
  82.0 1.0 collective-permute-done.1.x1
  83.0 0.7 collective-permute-done.2.x2
  83.7 1.4 collective-permute-done.3.x3
  85.1 1.8 %source_traces1.1 = (f32[512,128]{1,0:T(8,128)}, f32[2,32,128]{2,1,0:T(8,128)S(1)}, f32[2,32,128]{2,1,0:T(8,128)S(1)}, f32[2,32,128]{2,1,0:T(8,128)S(1)}, f32[2,32,128]{2,1,0:T(8,128)S(1)}) custom-call(s32[4]{0:T(128)S(1)} %pad_add_fusion.pos_ref.refs_0_, bf16[256,256]{1,0:T(8,128)(2,1)S(1)} %copy-done.1, bf16[256,256]{1,0:T(8,128)(2,1)S(1)} %copy-done, ...), custom_call_target="tpu_custom_call" | custom-call | tf_op jit(solution)/shard_map/source_traces1/pallas_call | solution.py:187
  86.9 1.2 collective-permute-start.11
  88.1 2.3 %collective-permute-start.12 = (f32[2,32,128]{2,1,0:T(8,128)S(1)}, f32[2,32,128]{2,1,0:T(8,128)S(1)}, u32[]{:S(2)}, u32[]{:S(2)}) collective-permute-start(f32[2,32,128]{2,1,0:T(8,128)S(1)} %get-tuple-element.44), channel_id=1, source_target_pairs={{0,64},{32,96},{64,0},{96,32},{1,65},{33,97},{65,1},{97,33},{2,66}... | collective-permute-start | bytes 98312 | tf_op jit(solution)/shard_map/ppermute | solution.py:326
  90.4 0.5 collective-permute-start.13
  90.9 1.2 collective-permute-done.11.x1
  92.0 1.5 %collective-permute-done.12.x2 = f32[2,32,128]{2,1,0:T(8,128)S(1)} collective-permute-done((f32[2,32,128]{2,1,0:T(8,128)S(1)}, f32[2,32,128]{2,1,0:T(8,128)S(1)}, u32[]{:S(2)}, u32[]{:S(2)}) %collective-permute-start.12) | collective-permute-done | bytes 32800 | tf_op jit(solution)/shard_map/ppermute | solution.py:326
  93.5 0.8 collective-permute-done.13.x3
  94.3 1.6 %spread.3 = f32[16,4,32,128]{3,2,1,0:T(8,128)} custom-call(s32[4]{0:T(128)S(1)} %pad_add_fusion.pos_ref.refs_0_, f32[2,32,128]{2,1,0:T(8,128)S(1)} %get-tuple-element.42.x0, f32[2,32,128]{2,1,0:T(8,128)S(1)} %collective-permute-done.11.x1, f32[2,32,128]{2,1,0:T(8,128)S(1)} %collective-permute-done.12.x2, f32[2,32,128]{2,1,0:T(8,128)S(1)} %collective-permute-done.13.x3), custom_call_target="tpu_custom_call" | custom-call | tf_op jit(solution)/shard_map/spread/pallas_call | solution.py:223
  95.9 7.6 %all-to-all-start.3 = ((f32[16,4,32,128]{3,2,1,0:T(8,128)}), f32[16,4,32,128]{3,2,1,0:T(8,128)S(1)}, u32[]{:S(2)}, u32[]{:S(2)}) async-start(f32[16,4,32,128]{3,2,1,0:T(8,128)} %spread.3), calls=%async_computation.3 | async-start | bytes 2097152 | tf_op jit(solution)/shard_map/all_to_all | solution.py:322
  103.5 0.1 collective-permute-start.14
  103.6 12.8 %all-to-all-done.3.o1 = f32[16,4,32,128]{3,2,1,0:T(8,128)S(1)} async-done(((f32[16,4,32,128]{3,2,1,0:T(8,128)}), f32[16,4,32,128]{3,2,1,0:T(8,128)S(1)}, u32[]{:S(2)}, u32[]{:S(2)}) %all-to-all-start.3) | async-done | bytes 1048608 | tf_op jit(solution)/shard_map/all_to_all | solution.py:322
  116.5 2.7 %collective-permute-done.15.t1 = f32[16,4,32,128]{3,2,1,0:T(8,128)S(1)} collective-permute-done((f32[16,4,32,128]{3,2,1,0:T(8,128)S(1)}, f32[16,4,32,128]{3,2,1,0:T(8,128)S(1)}, u32[]{:S(2)}, u32[]{:S(2)}) %collective-permute-start.15) | collective-permute-done | bytes 1048608 | tf_op jit(solution)/shard_map/ppermute | solution.py:347
  119.1 6.3 %adjoint_panel.1 = f32[8,4,32,128]{3,2,1,0:T(8,128)S(1)} custom-call(f32[16,4,32,128]{3,2,1,0:T(8,128)S(1)} %all-to-all-done.2.o0, f32[16,4,32,128]{3,2,1,0:T(8,128)S(1)} %all-to-all-done.3.o1, f32[16,4,32,128]{3,2,1,0:T(8,128)S(1)} %collective-permute-done.14.t0, f32[16,4,32,128]{3,2,1,0:T(8,128)S(1)} %collective-permute-done.15.t1, f32[16,2,1024,128]{3,2,1,0:T(8,128)} %r_hbm.3), custom_call_target="tpu_custom_call" | custom-call | flops 3221225472 | bytes 22020096 | tf_op jit(solution)/shard_map/adjoint_panel/pallas_call | solution.py:276
  125.4 15.0 %all_to_all.25.x_ref = f32[8,4,32,128]{3,2,1,0:T(8,128)S(1)} all-to-all(f32[8,4,32,128]{3,2,1,0:T(8,128)S(1)} %adjoint_panel.1), channel_id=1, replica_groups=mesh['z'=4,'xh'=2,'xl'=2,'y'=4,'c'=2] {'z','xh'}, dimensions={0} | all-to-all | bytes 1048576 | tf_op jit(solution)/shard_map/all_to_all | solution.py:349
  140.4 1.9 %receiver_traces.1 = f32[1024,128]{1,0:T(8,128)} custom-call(s32[4]{0:T(128)S(1)} %pad_add_fusion.pos_ref.refs_0_, bf16[256,256]{1,0:T(8,128)(2,1)S(1)} %copy-done.1, bf16[256,256]{1,0:T(8,128)(2,1)S(1)} %copy-done, s32[4,128]{1,0:T(4,128)S(1)} %copy-done.6, f32[1024,128]{1,0:T(8,128)S(1)} %bitcast.7, f32[8,4,32,128]{3,2,1,0:T(8,128)S(1)} %all_to_all.25.x_ref), custom_call_target="tpu_custom_call" | custom-call | tf_op jit(solution)/shard_map/receiver_traces/pallas_call | solution.py:307
  (19 shorter events, 0.1 us)
Async XLA Ops:
  0.6 59.0 %copy-start = (bf16[256,256]{1,0:T(8,128)(2,1)S(1)}, bf16[256,256]{1,0:T(8,128)(2,1)}, u32[]{:S(2)}) copy-start(bf16[256,256]{1,0:T(8,128)(2,1)} %constant.38.clone.refs_2_.tl_ref) | copy-start | bytes 393220
  0.6 59.0 %copy-start.1 = (bf16[256,256]{1,0:T(8,128)(2,1)S(1)}, bf16[256,256]{1,0:T(8,128)(2,1)}, u32[]{:S(2)}) copy-start(bf16[256,256]{1,0:T(8,128)(2,1)} %constant.37.clone.refs_1_.th_ref) | copy-start | bytes 393220
  0.7 59.0 %copy-start.3 = (bf16[256,256]{1,0:T(8,128)(2,1)S(1)}, bf16[256,256]{1,0:T(8,128)(2,1)}, u32[]{:S(2)}) copy-start(bf16[256,256]{1,0:T(8,128)(2,1)} %constant.40.clone.refs_4_.ttl_ref) | copy-start | bytes 393220
  0.7 59.0 %copy-start.4 = (bf16[256,256]{1,0:T(8,128)(2,1)S(1)}, bf16[256,256]{1,0:T(8,128)(2,1)}, u32[]{:S(2)}) copy-start(bf16[256,256]{1,0:T(8,128)(2,1)} %constant.39.clone.refs_3_.tth_ref) | copy-start | bytes 393220
  0.7 58.9 %copy-start.5 = (s32[2,128]{1,0:T(2,128)S(1)}, s32[2,128]{1,0:T(2,128)}, u32[]{:S(2)}) copy-start(s32[2,128]{1,0:T(2,128)} %mute_ref.2) | copy-start | bytes 3076
  16.0 3.3 %collective-permute-start.4 = (f32[16,4,32,128]{3,2,1,0:T(8,128)S(1)}, f32[16,4,32,128]{3,2,1,0:T(8,128)S(1)}, u32[]{:S(2)}, u32[]{:S(2)}) collective-permute-start(f32[16,4,32,128]{3,2,1,0:T(8,128)S(1)} %get-tuple-element.31), channel_id=1, source_target_pairs={{0,1},{1,0},{2,3},{3,2},{4,5},{5,4},{6,7},{7,6},{8,9},{9,8},{10,11... | collective-permute-start | bytes 3145736 | tf_op jit(solution)/shard_map/ppermute | solution.py:341
  16.1 11.6 %collective-permute-start = (f32[16,4,32,128]{3,2,1,0:T(8,128)}, f32[16,4,32,128]{3,2,1,0:T(8,128)}, u32[]{:S(2)}, u32[]{:S(2)}) collective-permute-start(f32[16,4,32,128]{3,2,1,0:T(8,128)} %get-tuple-element.25), channel_id=1, source_target_pairs={{0,1},{1,0},{2,3},{3,2},{4,5},{5,4},{6,7},{7,6},{8,9},{9,8},{10,11... | collective-permute-start | bytes 3145736 | tf_op jit(solution)/shard_map/ppermute | solution.py:341
  20.5 25.2 %all-to-all-start.1 = ((f32[16,4,32,128]{3,2,1,0:T(8,128)}), f32[16,4,32,128]{3,2,1,0:T(8,128)S(1)}, u32[]{:S(2)}, u32[]{:S(2)}) async-start(f32[16,4,32,128]{3,2,1,0:T(8,128)} %add.16), calls=%async_computation.1 | async-start | bytes 2097152 | tf_op jit(solution)/shard_map/all_to_all | solution.py:322
  45.7 24.3 %all-to-all-start = ((f32[16,4,32,128]{3,2,1,0:T(8,128)}), f32[16,4,32,128]{3,2,1,0:T(8,128)S(1)}, u32[]{:S(2)}, u32[]{:S(2)}) async-start(f32[16,4,32,128]{3,2,1,0:T(8,128)} %add.15), calls=%async_computation | async-start | bytes 2097152 | tf_op jit(solution)/shard_map/all_to_all | solution.py:322
  49.4 91.0 %copy-start.6 = (s32[4,128]{1,0:T(4,128)S(1)}, s32[4,128]{1,0:T(4,128)}, u32[]{:S(2)}) copy-start(s32[4,128]{1,0:T(4,128)} %mute_ref.3) | copy-start | bytes 6148
  50.1 6.6 %collective-permute-start.5 = (f32[2,32,128]{2,1,0:T(8,128)S(1)}, f32[2,32,128]{2,1,0:T(8,128)S(1)}, u32[]{:S(2)}, u32[]{:S(2)}) collective-permute-start(f32[2,32,128]{2,1,0:T(8,128)S(1)} %get-tuple-element.33), channel_id=1, source_target_pairs={{0,32},{32,64},{64,96},{96,0},{1,33},{33,65},{65,97},{97,1},{2,34}... | collective-permute-start | bytes 98312 | tf_op jit(solution)/shard_map/ppermute | solution.py:326
  52.1 5.8 %collective-permute-start.6 = (f32[2,32,128]{2,1,0:T(8,128)S(1)}, f32[2,32,128]{2,1,0:T(8,128)S(1)}, u32[]{:S(2)}, u32[]{:S(2)}) collective-permute-start(f32[2,32,128]{2,1,0:T(8,128)S(1)} %get-tuple-element.34), channel_id=1, source_target_pairs={{0,64},{32,96},{64,0},{96,32},{1,65},{33,97},{65,1},{97,33},{2,66}... | collective-permute-start | bytes 98312 | tf_op jit(solution)/shard_map/ppermute | solution.py:326
  55.7 3.9 %collective-permute-start.7 = (f32[2,32,128]{2,1,0:T(8,128)S(1)}, f32[2,32,128]{2,1,0:T(8,128)S(1)}, u32[]{:S(2)}, u32[]{:S(2)}) collective-permute-start(f32[2,32,128]{2,1,0:T(8,128)S(1)} %get-tuple-element.35), channel_id=1, source_target_pairs={{0,96},{32,0},{64,32},{96,64},{1,97},{33,1},{65,33},{97,65},{2,98}... | collective-permute-start | bytes 98312 | tf_op jit(solution)/shard_map/ppermute | solution.py:326
  60.8 5.2 %collective-permute-start.8 = (f32[2,32,128]{2,1,0:T(8,128)S(1)}, f32[2,32,128]{2,1,0:T(8,128)S(1)}, u32[]{:S(2)}, u32[]{:S(2)}) collective-permute-start(f32[2,32,128]{2,1,0:T(8,128)S(1)} %get-tuple-element.39), channel_id=1, source_target_pairs={{0,32},{32,64},{64,96},{96,0},{1,33},{33,65},{65,97},{97,1},{2,34}... | collective-permute-start | bytes 98312 | tf_op jit(solution)/shard_map/ppermute | solution.py:326
  60.9 5.9 %collective-permute-start.9 = (f32[2,32,128]{2,1,0:T(8,128)S(1)}, f32[2,32,128]{2,1,0:T(8,128)S(1)}, u32[]{:S(2)}, u32[]{:S(2)}) collective-permute-start(f32[2,32,128]{2,1,0:T(8,128)S(1)} %get-tuple-element.40), channel_id=1, source_target_pairs={{0,64},{32,96},{64,0},{96,32},{1,65},{33,97},{65,1},{97,33},{2,66}... | collective-permute-start | bytes 98312 | tf_op jit(solution)/shard_map/ppermute | solution.py:326
  64.5 3.9 %collective-permute-start.10 = (f32[2,32,128]{2,1,0:T(8,128)S(1)}, f32[2,32,128]{2,1,0:T(8,128)S(1)}, u32[]{:S(2)}, u32[]{:S(2)}) collective-permute-start(f32[2,32,128]{2,1,0:T(8,128)S(1)} %get-tuple-element.41), channel_id=1, source_target_pairs={{0,96},{32,0},{64,32},{96,64},{1,97},{33,1},{65,33},{97,65},{2,98}... | collective-permute-start | bytes 98312 | tf_op jit(solution)/shard_map/ppermute | solution.py:326
  70.0 25.9 %all-to-all-start.2 = ((f32[16,4,32,128]{3,2,1,0:T(8,128)}), f32[16,4,32,128]{3,2,1,0:T(8,128)S(1)}, u32[]{:S(2)}, u32[]{:S(2)}) async-start(f32[16,4,32,128]{3,2,1,0:T(8,128)} %spread.2), calls=%async_computation.2 | async-start | bytes 2097152 | tf_op jit(solution)/shard_map/all_to_all | solution.py:322
  77.8 5.2 %collective-permute-start.1 = (f32[2,32,128]{2,1,0:T(8,128)S(1)}, f32[2,32,128]{2,1,0:T(8,128)S(1)}, u32[]{:S(2)}, u32[]{:S(2)}) collective-permute-start(f32[2,32,128]{2,1,0:T(8,128)S(1)} %get-tuple-element.27), channel_id=1, source_target_pairs={{0,32},{32,64},{64,96},{96,0},{1,33},{33,65},{65,97},{97,1},{2,34}... | collective-permute-start | bytes 98312 | tf_op jit(solution)/shard_map/ppermute | solution.py:326
  78.3 5.4 %collective-permute-start.2 = (f32[2,32,128]{2,1,0:T(8,128)S(1)}, f32[2,32,128]{2,1,0:T(8,128)S(1)}, u32[]{:S(2)}, u32[]{:S(2)}) collective-permute-start(f32[2,32,128]{2,1,0:T(8,128)S(1)} %get-tuple-element.28), channel_id=1, source_target_pairs={{0,64},{32,96},{64,0},{96,32},{1,65},{33,97},{65,1},{97,33},{2,66}... | collective-permute-start | bytes 98312 | tf_op jit(solution)/shard_map/ppermute | solution.py:326
  81.0 4.1 %collective-permute-start.3 = (f32[2,32,128]{2,1,0:T(8,128)S(1)}, f32[2,32,128]{2,1,0:T(8,128)S(1)}, u32[]{:S(2)}, u32[]{:S(2)}) collective-permute-start(f32[2,32,128]{2,1,0:T(8,128)S(1)} %get-tuple-element.29), channel_id=1, source_target_pairs={{0,96},{32,0},{64,32},{96,64},{1,97},{33,1},{65,33},{97,65},{2,98}... | collective-permute-start | bytes 98312 | tf_op jit(solution)/shard_map/ppermute | solution.py:326
  86.9 5.1 %collective-permute-start.11 = (f32[2,32,128]{2,1,0:T(8,128)S(1)}, f32[2,32,128]{2,1,0:T(8,128)S(1)}, u32[]{:S(2)}, u32[]{:S(2)}) collective-permute-start(f32[2,32,128]{2,1,0:T(8,128)S(1)} %get-tuple-element.43), channel_id=1, source_target_pairs={{0,32},{32,64},{64,96},{96,0},{1,33},{33,65},{65,97},{97,1},{2,34}... | collective-permute-start | bytes 98312 | tf_op jit(solution)/shard_map/ppermute | solution.py:326
  88.1 5.4 %collective-permute-start.12 = (f32[2,32,128]{2,1,0:T(8,128)S(1)}, f32[2,32,128]{2,1,0:T(8,128)S(1)}, u32[]{:S(2)}, u32[]{:S(2)}) collective-permute-start(f32[2,32,128]{2,1,0:T(8,128)S(1)} %get-tuple-element.44), channel_id=1, source_target_pairs={{0,64},{32,96},{64,0},{96,32},{1,65},{33,97},{65,1},{97,33},{2,66}... | collective-permute-start | bytes 98312 | tf_op jit(solution)/shard_map/ppermute | solution.py:326
  90.4 3.9 %collective-permute-start.13 = (f32[2,32,128]{2,1,0:T(8,128)S(1)}, f32[2,32,128]{2,1,0:T(8,128)S(1)}, u32[]{:S(2)}, u32[]{:S(2)}) collective-permute-start(f32[2,32,128]{2,1,0:T(8,128)S(1)} %get-tuple-element.45), channel_id=1, source_target_pairs={{0,96},{32,0},{64,32},{96,64},{1,97},{33,1},{65,33},{97,65},{2,98}... | collective-permute-start | bytes 98312 | tf_op jit(solution)/shard_map/ppermute | solution.py:326
  95.9 20.5 %all-to-all-start.3 = ((f32[16,4,32,128]{3,2,1,0:T(8,128)}), f32[16,4,32,128]{3,2,1,0:T(8,128)S(1)}, u32[]{:S(2)}, u32[]{:S(2)}) async-start(f32[16,4,32,128]{3,2,1,0:T(8,128)} %spread.3), calls=%async_computation.3 | async-start | bytes 2097152 | tf_op jit(solution)/shard_map/all_to_all | solution.py:322
  103.5 12.9 %collective-permute-start.14 = (f32[16,4,32,128]{3,2,1,0:T(8,128)S(1)}, f32[16,4,32,128]{3,2,1,0:T(8,128)S(1)}, u32[]{:S(2)}, u32[]{:S(2)}) collective-permute-start(f32[16,4,32,128]{3,2,1,0:T(8,128)S(1)} %all-to-all-done.2.o0), channel_id=1, source_target_pairs={{0,1},{1,0},{2,3},{3,2},{4,5},{5,4},{6,7},{7,6},{8,9},{9,8},{10,11... | collective-permute-start | bytes 3145736 | tf_op jit(solution)/shard_map/ppermute | solution.py:347
  116.4 24.0 %copy-start.2 = (f32[256,4,128]{2,1,0:T(4,128)S(1)}, f32[256,4,128]{2,1,0:T(4,128)}, u32[]{:S(2)}) copy-start(f32[256,4,128]{2,1,0:T(4,128)} %param.13) | copy-start | bytes 1572868
  116.4 2.7 %collective-permute-start.15 = (f32[16,4,32,128]{3,2,1,0:T(8,128)S(1)}, f32[16,4,32,128]{3,2,1,0:T(8,128)S(1)}, u32[]{:S(2)}, u32[]{:S(2)}) collective-permute-start(f32[16,4,32,128]{3,2,1,0:T(8,128)S(1)} %all-to-all-done.3.o1), channel_id=1, source_target_pairs={{0,1},{1,0},{2,3},{3,2},{4,5},{5,4},{6,7},{7,6},{8,9},{9,8},{10,11... | collective-permute-start | bytes 3145736 | tf_op jit(solution)/shard_map/ppermute | solution.py:347

commit v3 on v2

v3 whole, which is shorter than its diff:
```python
import math

import numpy as np
import jax
import jax.numpy as jnp
from jax import lax
from jax.experimental import pallas as pl
from jax.experimental.pallas import tpu as pltpu
from jax.sharding import Mesh, PartitionSpec as P

F32, BF16 = jnp.float32, jnp.bfloat16
NT = 256
KB, KK = 8, 16
VMEM = pl.BlockSpec(memory_space=pltpu.VMEM)
SMEM = pl.BlockSpec(memory_space=pltpu.SMEM)
HBM = pl.BlockSpec(memory_space=pltpu.HBM)


def dft_table():
    k = np.arange(1, KB * KK + 1)[None, :]
    t = np.arange(NT)[:, None]
    phase = 2.0 * math.pi * ((k * t) % NT) / NT
    c = 1.0 / math.sqrt(KB * KK)
    return np.stack([c * np.cos(phase), -c * np.sin(phase)], axis=2).reshape(NT, NT)


def split_const(table):
    high = table.astype(np.float32).astype(jnp.bfloat16)
    low = (table - high.astype(np.float64)).astype(np.float32).astype(jnp.bfloat16)
    return np.asarray(high), np.asarray(low)


def split(x):
    high = x.astype(BF16)
    return high, (x - high.astype(F32)).astype(BF16)


def mm(a, b, contract=(1, 0)):
    return lax.dot_general(a, b, (((contract[0],), (contract[1],)), ((), ())), preferred_element_type=F32)


def mm3(a, b):
    return mm(a[0], b[0]) + (mm(a[0], b[1]) + mm(a[1], b[0]))


def params(mib):
    return pltpu.CompilerParams(vmem_limit_bytes=mib * 2**20)


def trade(v, pair, shift):
    t = v[(0 - shift) % 4]
    for m in range(1, 4):
        t = jnp.where(pair == m, v[(m - shift) % 4], t)
    return t


def unturn(x, y, sign):
    out = x
    for s in range(1, 4):
        out = jnp.where(y == s, pltpu.roll(x, (sign * 2 * s) % 8, 1), out)
    return out


def forward_kernel(pos_ref, f_hbm, r_hbm, own, oth, rh_ref, rl_ref, f_ref, r_ref, fsem, sem):
    def fetch_f(g):
        cut = pl.ds(g * 4, 4)
        return pltpu.make_async_copy(f_hbm.at[cut], f_ref.at[cut], fsem.at[g])

    def fetch(g, z):
        cut = (pl.ds(g * 4, 4), slice(None), pl.ds(z * 256, 256))
        return pltpu.make_async_copy(r_hbm.at[cut], r_ref.at[cut], sem.at[g * 4 + z])

    fetch_f(0).start()
    for z in range(4):
        fetch(0, z).start()
    core = pos_ref[0]
    row = lax.broadcasted_iota(jnp.int32, (64, 64), 0)
    col = lax.broadcasted_iota(jnp.int32, (64, 64), 1)
    perms = []
    for q in range(4):
        c = (row // 32 + core) % 2
        y = ((row // 2) % 4 + 4 - q) % 4
        src = (row % 2) * 32 + ((row // 8) % 2) * 16 + y * 4 + c * 2 + (row // 16) % 2
        perms.append(jnp.where(col == src, 1.0, 0.0).astype(BF16))
    pair = lax.broadcasted_iota(jnp.int32, (8, 128), 0) // 2

    @pl.loop(0, 4)
    def _(g):
        fetch_f(g).wait()
        lhs = []
        for q in range(4):
            fr, fi = f_ref[g * 4 + q, 0], f_ref[g * 4 + q, 1]
            x = jnp.concatenate(
                [jnp.concatenate([fr, -fi], axis=1), jnp.concatenate([fi, fr], axis=1)], axis=0
            )
            xh, xl = split(x)
            ph, plo = mm(perms[q], xh).astype(BF16), mm(perms[q], xl).astype(BF16)
            lhs.append((ph, jnp.concatenate([ph, plo], axis=0)))
        g8 = pl.ds(pl.multiple_of(g * 8, 8), 8)

        @pl.when(g < 3)
        def _():
            fetch_f(g + 1).start()

        for z in range(4):
            fetch(g, z).wait()

            @pl.when(g < 3)
            def _():
                fetch(g + 1, z).start()

        for z in range(4):
            rows = slice(z * 256, (z + 1) * 256)
            res = []
            for q in range(4):
                k = g * 4 + q
                wh, wl = split(jnp.concatenate([r_ref[k, 0, rows, :], r_ref[k, 1, rows, :]], axis=1))
                rh_ref[k, rows, :] = wh
                rl_ref[k, rows, :] = wl
                acc = mm(lhs[q][1], wh, (1, 1))
                res.append(acc[:64] + (acc[64:] + mm(lhs[q][0], wl, (1, 1))))
            for xh_ in range(2):
                for part in range(8):
                    v = [r[part * 8 : part * 8 + 8, xh_ * 128 : xh_ * 128 + 128] for r in res]
                    out = oth if part // 4 else own
                    for y in range(4):
                        out[z * 2 + xh_, (part % 2) * 4 + y, (part // 2) % 2, g8, :] = trade(v, pair, y)


def forward_panel(pos, focusing, reflection):
    panel = jax.ShapeDtypeStruct((KB, 8, 2, 32, 128), F32)
    half = jax.ShapeDtypeStruct((KK, 1024, 256), BF16)
    return pl.pallas_call(
        forward_kernel,
        in_specs=[SMEM, HBM, HBM],
        out_specs=[VMEM] * 4,
        out_shape=[panel] * 2 + [half] * 2,
        scratch_shapes=[
            pltpu.VMEM((KK, 2, 32, 128), F32),
            pltpu.VMEM((KK, 2, 1024, 128), F32),
            pltpu.SemaphoreType.DMA((4,)),
            pltpu.SemaphoreType.DMA((16,)),
        ],
        compiler_params=params(24),
        cost_estimate=pl.CostEstimate(flops=3 * 2**30, bytes_accessed=21 * 2**20, transcendentals=0),
        name="forward_panel",
    )(pos, focusing, reflection)


def source_kernel(pos_ref, th_ref, tl_ref, tth_ref, ttl_ref, mute_ref, x_ref, time_ref, out_ref):
    y = pos_ref[2]
    cols = []
    for j in range(2):
        groups = []
        for f in range(KB):
            t = [x_ref[f, i, j] for i in range(8)]
            groups.append(((t[0] + t[1]) + (t[2] + t[3])) + ((t[4] + t[5]) + (t[6] + t[7])))
        x = jnp.concatenate(groups, axis=0)
        cols.append(unturn(x.reshape(32, 8, 128), y, -1).reshape(256, 128))
    up = mm3((th_ref[...], tl_ref[...]), split(jnp.concatenate(cols, axis=1)))
    t = lax.broadcasted_iota(jnp.int32, (NT, 128), 0)
    kept = []
    for j in range(2):
        mute = jnp.broadcast_to(mute_ref[j : j + 1, :], (NT, 128))
        val = jnp.where((t < mute) | (t > NT - mute), up[:, j * 128 : (j + 1) * 128], 0.0)
        time_ref[pl.ds(j, NT, stride=2), :] = val
        kept.append(val)
    back = mm3((tth_ref[...], ttl_ref[...]), split(jnp.concatenate(kept, axis=1)))
    for j in range(2):
        b = unturn(back[:, j * 128 : (j + 1) * 128].reshape(32, 8, 128), y, 1).reshape(KB, 32, 128)
        for f in range(KB):
            for i in range(8):
                out_ref[f, i, j] = b[f]


def source_traces(pos, tables, mute, parts):
    return pl.pallas_call(
        source_kernel,
        in_specs=[SMEM] + [VMEM] * 6,
        out_specs=[VMEM] * 2,
        out_shape=[
            jax.ShapeDtypeStruct((NT * 2, 128), F32),
            jax.ShapeDtypeStruct((KB, 8, 2, 32, 128), F32),
        ],
        compiler_params=params(8),
        name="source_traces",
    )(pos, *tables, mute, parts)


def adjoint_kernel(own, oth, rh_ref, rl_ref, out_ref):
    pair = lax.broadcasted_iota(jnp.int32, (8, 128), 0) // 2
    even = (lax.broadcasted_iota(jnp.int32, (64, 128), 0) % 2) == 0

    @pl.loop(0, 4)
    def _(g):
        g8 = pl.ds(pl.multiple_of(g * 8, 8), 8)
        acc = [None] * 4
        for z in range(4):
            lhs = [[None] * 2 for _ in range(4)]
            for xh_ in range(2):
                tiles = [[] for _ in range(4)]
                for part in range(8):
                    ref = oth if (part // 2) % 2 else own
                    v = [ref[z * 2 + xh_, (part % 2) * 4 + y, part // 4, g8, :] for y in range(4)]
                    for q in range(4):
                        tiles[q].append(trade(v, pair, q))
                for q in range(4):
                    lhs[q][xh_] = jnp.concatenate(tiles[q], axis=0)
            rows = slice(z * 256, (z + 1) * 256)
            for q in range(4):
                bh, bl = split(jnp.concatenate(lhs[q], axis=1))
                wh, wl = rh_ref[g * 4 + q, rows, :], rl_ref[g * 4 + q, rows, :]
                both = mm(jnp.concatenate([bh, bl], axis=0), wh)
                add = both[:64] + (both[64:] + mm(bh, wl))
                acc[q] = add if acc[q] is None else acc[q] + add
        res = []
        for q in range(4):
            a, b = acc[q][:, :128], acc[q][:, 128:]
            res.append(a + jnp.where(even, pltpu.roll(b, 63, 0), -pltpu.roll(b, 1, 0)))
        for part in range(8):
            v = [r[part * 8 : part * 8 + 8] for r in res]
            for y in range(4):
                out_ref[(part % 2) * 4 + y, part // 2, g8, :] = trade(v, pair, y)


def adjoint_panel(own, oth, rh, rl):
    return pl.pallas_call(
        adjoint_kernel,
        in_specs=[VMEM] * 4,
        out_specs=VMEM,
        out_shape=jax.ShapeDtypeStruct((8, 4, 32, 128), F32),
        compiler_params=params(8),
        cost_estimate=pl.CostEstimate(flops=3 * 2**30, bytes_accessed=2**20, transcendentals=0),
        name="adjoint_panel",
    )(own, oth, rh, rl)


def receiver_kernel(pos_ref, th_ref, tl_ref, mute_ref, direct_ref, x_ref, out_ref):
    even = pos_ref[0] == 0
    turn = pos_ref[1]
    t = lax.broadcasted_iota(jnp.int32, (NT, 128), 0)
    for c in range(2):
        cols = []
        for j in range(2):
            a = jnp.where(even, x_ref[:, j * 2 + c], x_ref[:, j * 2 + 1 - c])
            cols.append(unturn(a.reshape(32, 8, 128), turn, -1).reshape(256, 128))
        adj = mm3((th_ref[...], tl_ref[...]), split(jnp.concatenate(cols, axis=1)))
        for j in range(2):
            p = c * 2 + j
            mute = jnp.broadcast_to(mute_ref[p : p + 1, :], (NT, 128))
            val = jnp.where((t < mute) | (t > NT - mute), adj[:, j * 128 : (j + 1) * 128], 0.0)
            rows = pl.ds(p, NT, stride=4)
            out_ref[rows, :] = direct_ref[rows, :] - val


def receiver_traces(pos, tables, mute, direct, x):
    return pl.pallas_call(
        receiver_kernel,
        in_specs=[SMEM] + [VMEM] * 5,
        out_specs=VMEM,
        out_shape=jax.ShapeDtypeStruct((NT * 4, 128), F32),
        compiler_params=params(8),
        name="receiver_traces",
    )(pos, *tables, mute, direct, x)


CHIPS = ("z", "xh", "xl", "y")
SWAP = [(0, 1), (1, 0)]


def exchange(x, axes):
    whole = x.reshape((-1,) + x.shape[-3:]) if len(axes) == 4 else x
    return lax.all_to_all(whole, axes, split_axis=0, concat_axis=0, tiled=True).reshape(x.shape)


def body(reflection, focusing, direct_wave, mute_source, mute_receiver):
    core, z, y = lax.axis_index("c"), lax.axis_index("z"), lax.axis_index("y")
    pos = jnp.stack([core, (z & 1) * 2 + lax.axis_index("xh"), y])
    table = dft_table()
    th, tl = split_const(table)

    focusing = pltpu.with_memory_space_constraint(focusing, pltpu.HBM)
    reflection = pltpu.with_memory_space_constraint(reflection, pltpu.HBM)
    own, oth, rh, rl = forward_panel(pos, focusing, reflection)
    parts = exchange(own + lax.ppermute(oth, "c", SWAP), CHIPS)
    time, back = source_traces(pos, (th, tl, th.T, tl.T), mute_source, parts)
    b_own = exchange(back, CHIPS)
    b_oth = lax.ppermute(b_own, "c", SWAP)
    adjoint = adjoint_panel(b_own, b_oth, rh, rl)
    received = exchange(adjoint, ("z", "xh"))
    plus = receiver_traces(
        pos, (th, tl), mute_receiver, direct_wave.reshape(NT * 4, 128), received
    )
    return time.reshape(NT, 2, 128), plus.reshape(NT, 4, 128)


def solution(mesh):
    fine = Mesh(mesh.devices.reshape(4, 2, 2, 4, 2), ("z", "xh", "xl", "y", "c"))
    freq, rcv = ("z", "xh"), ("xl", "y", "c")
    return jax.shard_map(
        body,
        mesh=fine,
        in_specs=(
            P(freq, None, None, rcv),
            P(freq, None, None, rcv),
            P(None, freq, rcv),
            P(rcv, freq),
            P(freq, rcv),
        ),
        out_specs=(P(None, rcv, freq), P(None, freq, rcv)),
        check_vma=False,
    )
```

time: 143 us -> 119 us (0.83)
  blocking collectives: 15 us -> 91.3 us
  starting transfers between devices: 45.2 us -> 0.09 us
  waiting for transfers between devices: 46.8 us -> 8.3 us
  Pallas kernels: 30.8 us -> 17.8 us
  other arithmetic: 3.72 us -> 0.55 us
    all_to_all x1 -> x3, blocking collectives: 15 us -> 91.3 us  [exchange(): lax.all_to_all(whole, axes, split_axis=0, concat_axis=0, tiled=True)]
    all_to_all x4 -> x0, waiting for transfers between devices: 28.5 us -> none  [exchange_xy(): return lax.all_to_all(x, AROUND, split_axis=0, concat_axis=0, tiled=True)]
    all_to_all x4 -> x0, starting transfers between devices: 25.5 us -> none  [exchange_xy(): return lax.all_to_all(x, AROUND, split_axis=0, concat_axis=0, tiled=True)]
    ppermute x16 -> x2, starting transfers between devices: 19.6 us -> 0.09 us  [the longest x1 0.09 us: body(): parts = exchange(own + lax.ppermute(oth, 'c', SWAP), CHIPS)]
    ppermute x16 -> x2, waiting for transfers between devices: 18.3 us -> 8.3 us  [the longest x1 4.16 us: body(): b_oth = lax.ppermute(b_own, 'c', SWAP)]
    pallas_call x7 -> x2, Pallas kernels: 13.6 us -> 5.44 us  [the longest x1 3.63 us: adjoint_panel(): pl.pallas_call(adjoint_kernel, in_specs=[VMEM] * 4, out_specs=VMEM, out_s...]
    pallas_call x1, Pallas kernels: 15.3 us -> 10.5 us  [forward_panel(): pl.pallas_call(forward_kernel, in_specs=[SMEM, HBM, HBM], out_specs=[VMEM...]
    add x2 -> x1, other arithmetic: 3.64 us -> 0.48 us  [body(): parts = exchange(own + lax.ppermute(oth, 'c', SWAP), CHIPS)]
  transfers between devices with their start and end apart: 20 -> 2, of which waited for: 15 -> 2; matrix products, arithmetic and copies ran while one was open for 3% -> 0% of each run, Pallas kernels for 5% -> 0%
where the time goes in v3:
time: 119 us
  blocking collectives  91.3 us (77%)
  Pallas kernels  17.8 us (15%)
  waiting for transfers between devices  8.3 us (7%)
    all_to_all x3, blocking collectives, exchange(): lax.all_to_all(whole, axes, split_axis=0, concat_axis=0, tiled=True)  91.3 us
    pallas_call x1, Pallas kernels, forward_panel(): pl.pallas_call(forward_kernel, in_specs=[SMEM, HBM, HBM], out_specs=[VMEM...  10.5 us
    ppermute x1, waiting for transfers between devices, body(): b_oth = lax.ppermute(b_own, 'c', SWAP)  4.16 us
    ppermute x1, waiting for transfers between devices, body(): parts = exchange(own + lax.ppermute(oth, 'c', SWAP), CHIPS)  4.15 us
    pallas_call x1, Pallas kernels, adjoint_panel(): pl.pallas_call(adjoint_kernel, in_specs=[VMEM] * 4, out_specs=VMEM, out_s...  3.63 us
  transfers between devices with their start and end apart: 2, of which 2 were waited for; matrix products, arithmetic and copies ran while one was open for 0% of the time, Pallas kernels for 0%

profile of v3, /device:TPU:0, one launch (start us, length us, event | category | flops | bytes accessed | tf_op | source)
XLA Modules:
  0.0 118.9 jit_solution(16287452615965312679)
XLA Ops:
  0.6 0.1 pad_add_fusion.pos_ref
  0.7 10.5 %forward_panel.1 = (f32[8,8,2,32,128]{4,3,2,1,0:T(8,128)S(1)}, f32[8,8,2,32,128]{4,3,2,1,0:T(8,128)S(1)}, bf16[16,1024,256]{2,1,0:T(8,128)(2,1)S(1)}, bf16[16,1024,256]{2,1,0:T(8,128)(2,1)S(1)}) custom-call(s32[3]{0:T(128)S(1)} %pad_add_fusion.pos_ref, f32[16,2,32,128]{3,2,1,0:T(8,128)} %f_hbm.1, f32[16,2,1024,128]{3,2,1,0:T(8,128)} %r_hbm.1), custom_call_target="tpu_custom_call" | custom-call | flops 3221225472 | bytes 22020096 | tf_op jit(solution)/shard_map/forward_panel/pallas_call | solution.py:133
  11.2 0.1 collective-permute-start
  11.3 4.1 %collective-permute-done = f32[8,8,2,32,128]{4,3,2,1,0:T(8,128)S(1)} collective-permute-done((f32[8,8,2,32,128]{4,3,2,1,0:T(8,128)S(1)}, f32[8,8,2,32,128]{4,3,2,1,0:T(8,128)S(1)}, u32[]{:S(2)}, u32[]{:S(2)}) %collective-permute-start) | collective-permute-done | bytes 2097184 | tf_op jit(solution)/shard_map/ppermute | solution.py:285
  15.5 0.5 add.7
  16.0 0.0 copy-start.1
  16.0 0.0 copy-start.2
  16.0 0.0 copy-start.3
  16.0 0.0 copy-start.4
  16.0 0.0 copy-start.6
  16.0 41.3 %all_to_all.15 = f32[64,2,32,128]{3,2,1,0:T(8,128)S(1)} all-to-all(f32[64,2,32,128]{3,2,1,0:T(8,128)S(1)} %bitcast.15), channel_id=1, replica_groups=mesh['z'=4,'xh'=2,'xl'=2,'y'=4,'c'=2] {'z','xh','xl','y'}, dimensions={0} | all-to-all | bytes 4194304 | tf_op jit(solution)/shard_map/all_to_all | solution.py:273
  57.4 0.0 copy-done.1
  57.4 0.0 copy-done.2
  57.4 0.0 copy-done.3
  57.4 0.0 copy-done.4
  57.4 0.0 copy-done.6
  57.4 1.8 %source_traces.1 = (f32[512,128]{1,0:T(8,128)}, f32[8,8,2,32,128]{4,3,2,1,0:T(8,128)S(1)}) custom-call(s32[3]{0:T(128)S(1)} %pad_add_fusion.pos_ref, bf16[256,256]{1,0:T(8,128)(2,1)S(1)} %copy-done.2, bf16[256,256]{1,0:T(8,128)(2,1)S(1)} %copy-done.1, bf16[256,256]{1,0:T(8,128)(2,1)S(1)} %copy-done.4, bf16[256,256]{1,0:T(8,128)(2,1)S(1)} %copy-done.3, ...), custom_call_target="tpu_custom_call" | custom-call | tf_op jit(solution)/shard_map/source_traces/pallas_call | solution.py:177
  59.2 34.7 %all_to_all.16 = f32[64,2,32,128]{3,2,1,0:T(8,128)S(1)} all-to-all(f32[64,2,32,128]{3,2,1,0:T(8,128)S(1)} %bitcast.13), channel_id=1, replica_groups=mesh['z'=4,'xh'=2,'xl'=2,'y'=4,'c'=2] {'z','xh','xl','y'}, dimensions={0} | all-to-all | bytes 4194304 | tf_op jit(solution)/shard_map/all_to_all | solution.py:273
  93.9 0.0 collective-permute-start.1
  93.9 4.2 %collective-permute-done.1.oth = f32[8,8,2,32,128]{4,3,2,1,0:T(8,128)S(1)} collective-permute-done((f32[8,8,2,32,128]{4,3,2,1,0:T(8,128)S(1)}, f32[8,8,2,32,128]{4,3,2,1,0:T(8,128)S(1)}, u32[]{:S(2)}, u32[]{:S(2)}) %collective-permute-start.1) | collective-permute-done | bytes 2097184 | tf_op jit(solution)/shard_map/ppermute | solution.py:288
  98.0 0.0 copy-start
  98.0 0.0 copy-start.5
  98.0 3.6 %adjoint_panel.1 = f32[8,4,32,128]{3,2,1,0:T(8,128)S(1)} custom-call(f32[8,8,2,32,128]{4,3,2,1,0:T(8,128)S(1)} %bitcast.12, f32[8,8,2,32,128]{4,3,2,1,0:T(8,128)S(1)} %collective-permute-done.1.oth, bf16[16,1024,256]{2,1,0:T(8,128)(2,1)S(1)} %get-tuple-element.12.rh_ref, bf16[16,1024,256]{2,1,0:T(8,128)(2,1)S(1)} %get-tuple-element.13.rl_ref), custom_call_target="tpu_custom_call" | custom-call | flops 3221225472 | bytes 1048576 | tf_op jit(solution)/shard_map/adjoint_panel/pallas_call | solution.py:227
  101.7 15.3 %all_to_all.17.x_ref = f32[8,4,32,128]{3,2,1,0:T(8,128)S(1)} all-to-all(f32[8,4,32,128]{3,2,1,0:T(8,128)S(1)} %adjoint_panel.1), channel_id=1, replica_groups=mesh['z'=4,'xh'=2,'xl'=2,'y'=4,'c'=2] {'z','xh'}, dimensions={0} | all-to-all | bytes 1048576 | tf_op jit(solution)/shard_map/all_to_all | solution.py:273
  117.0 0.0 copy-done
  117.0 0.0 copy-done.5
  117.0 1.9 %receiver_traces.1 = f32[1024,128]{1,0:T(8,128)} custom-call(s32[3]{0:T(128)S(1)} %pad_add_fusion.pos_ref, bf16[256,256]{1,0:T(8,128)(2,1)S(1)} %copy-done.2, bf16[256,256]{1,0:T(8,128)(2,1)S(1)} %copy-done.1, s32[4,128]{1,0:T(4,128)S(1)} %copy-done.5, f32[1024,128]{1,0:T(8,128)S(1)} %bitcast.14, f32[8,4,32,128]{3,2,1,0:T(8,128)S(1)} %all_to_all.17.x_ref), custom_call_target="tpu_custom_call" | custom-call | tf_op jit(solution)/shard_map/receiver_traces/pallas_call | solution.py:257
Async XLA Ops:
  11.2 4.2 %collective-permute-start = (f32[8,8,2,32,128]{4,3,2,1,0:T(8,128)S(1)}, f32[8,8,2,32,128]{4,3,2,1,0:T(8,128)S(1)}, u32[]{:S(2)}, u32[]{:S(2)}) collective-permute-start(f32[8,8,2,32,128]{4,3,2,1,0:T(8,128)S(1)} %get-tuple-element.9), channel_id=1, source_target_pairs={{0,1},{1,0},{2,3},{3,2},{4,5},{5,4},{6,7},{7,6},{8,9},{9,8},{10,11... | collective-permute-start | bytes 6291464 | tf_op jit(solution)/shard_map/ppermute | solution.py:285
  16.0 41.4 %copy-start.1 = (bf16[256,256]{1,0:T(8,128)(2,1)S(1)}, bf16[256,256]{1,0:T(8,128)(2,1)}, u32[]{:S(2)}) copy-start(bf16[256,256]{1,0:T(8,128)(2,1)} %constant.29.clone.tl_ref) | copy-start | bytes 393220
  16.0 41.4 %copy-start.2 = (bf16[256,256]{1,0:T(8,128)(2,1)S(1)}, bf16[256,256]{1,0:T(8,128)(2,1)}, u32[]{:S(2)}) copy-start(bf16[256,256]{1,0:T(8,128)(2,1)} %constant.28.clone.th_ref) | copy-start | bytes 393220
  16.0 41.4 %copy-start.3 = (bf16[256,256]{1,0:T(8,128)(2,1)S(1)}, bf16[256,256]{1,0:T(8,128)(2,1)}, u32[]{:S(2)}) copy-start(bf16[256,256]{1,0:T(8,128)(2,1)} %constant.31.clone.ttl_ref) | copy-start | bytes 393220
  16.0 41.4 %copy-start.4 = (bf16[256,256]{1,0:T(8,128)(2,1)S(1)}, bf16[256,256]{1,0:T(8,128)(2,1)}, u32[]{:S(2)}) copy-start(bf16[256,256]{1,0:T(8,128)(2,1)} %constant.30.clone.tth_ref) | copy-start | bytes 393220
  16.0 41.4 %copy-start.6 = (s32[2,128]{1,0:T(2,128)S(1)}, s32[2,128]{1,0:T(2,128)}, u32[]{:S(2)}) copy-start(s32[2,128]{1,0:T(2,128)} %mute_ref.2) | copy-start | bytes 3076
  93.9 4.2 %collective-permute-start.1 = (f32[8,8,2,32,128]{4,3,2,1,0:T(8,128)S(1)}, f32[8,8,2,32,128]{4,3,2,1,0:T(8,128)S(1)}, u32[]{:S(2)}, u32[]{:S(2)}) collective-permute-start(f32[8,8,2,32,128]{4,3,2,1,0:T(8,128)S(1)} %bitcast.11), channel_id=1, source_target_pairs={{0,1},{1,0},{2,3},{3,2},{4,5},{5,4},{6,7},{7,6},{8,9},{9,8},{10,11... | collective-permute-start | bytes 6291464 | tf_op jit(solution)/shard_map/ppermute | solution.py:288
  98.0 19.0 %copy-start = (f32[256,4,128]{2,1,0:T(4,128)S(1)}, f32[256,4,128]{2,1,0:T(4,128)}, u32[]{:S(2)}) copy-start(f32[256,4,128]{2,1,0:T(4,128)} %param.11) | copy-start | bytes 1572868
  98.0 19.0 %copy-start.5 = (s32[4,128]{1,0:T(4,128)S(1)}, s32[4,128]{1,0:T(4,128)}, u32[]{:S(2)}) copy-start(s32[4,128]{1,0:T(4,128)} %mute_ref.3) | copy-start | bytes 6148

commit v4 on v3

v4 whole, which is shorter than its diff:
```python
import functools
import math

import numpy as np
import jax
import jax.numpy as jnp
from jax import lax
from jax.experimental import pallas as pl
from jax.experimental.pallas import tpu as pltpu
from jax.sharding import Mesh, PartitionSpec as P

F32, BF16 = jnp.float32, jnp.bfloat16
NT = 256
KB, KK = 8, 16
VMEM = pl.BlockSpec(memory_space=pltpu.VMEM)
SMEM = pl.BlockSpec(memory_space=pltpu.SMEM)
HBM = pl.BlockSpec(memory_space=pltpu.HBM)


def dft_table():
    k = np.arange(1, KB * KK + 1)[None, :]
    t = np.arange(NT)[:, None]
    phase = 2.0 * math.pi * ((k * t) % NT) / NT
    c = 1.0 / math.sqrt(KB * KK)
    return np.stack([c * np.cos(phase), -c * np.sin(phase)], axis=2).reshape(NT, NT)


def split_const(table):
    high = table.astype(np.float32).astype(jnp.bfloat16)
    low = (table - high.astype(np.float64)).astype(np.float32).astype(jnp.bfloat16)
    return np.asarray(high), np.asarray(low)


def split(x):
    high = x.astype(BF16)
    return high, (x - high.astype(F32)).astype(BF16)


def mm(a, b, contract=(1, 0)):
    return lax.dot_general(a, b, (((contract[0],), (contract[1],)), ((), ())), preferred_element_type=F32)


def mm3(a, b):
    return mm(a[0], b[0]) + (mm(a[0], b[1]) + mm(a[1], b[0]))


def params(mib):
    return pltpu.CompilerParams(vmem_limit_bytes=mib * 2**20)


def trade(v, pair, shift):
    t = v[(0 - shift) % 4]
    for m in range(1, 4):
        t = jnp.where(pair == m, v[(m - shift) % 4], t)
    return t


def unturn(x, y, sign):
    out = x
    for s in range(1, 4):
        out = jnp.where(y == s, pltpu.roll(x, (sign * 2 * s) % 8, 1), out)
    return out


def selections(core):
    row = lax.broadcasted_iota(jnp.int32, (64, 64), 0)
    col = lax.broadcasted_iota(jnp.int32, (64, 64), 1)
    out = []
    for q in range(4):
        c = (row // 32 + core) % 2
        y = ((row // 2) % 4 + 4 - q) % 4
        src = (row % 2) * 32 + ((row // 8) % 2) * 16 + y * 4 + c * 2 + (row // 16) % 2
        out.append(jnp.where(col == src, 1.0, 0.0).astype(BF16))
    return out


def group_operand(perms, f_ref, base):
    lhs = []
    for q in range(4):
        fr, fi = f_ref[base + q, 0], f_ref[base + q, 1]
        x = jnp.concatenate(
            [jnp.concatenate([fr, -fi], axis=1), jnp.concatenate([fi, fr], axis=1)], axis=0
        )
        xh, xl = split(x)
        ph, plo = mm(perms[q], xh).astype(BF16), mm(perms[q], xl).astype(BF16)
        lhs.append((ph, jnp.concatenate([ph, plo], axis=0)))
    return lhs


def group_block(g, z, lhs, r_ref, r_base, own, oth, rh_ref, rl_ref):
    pair = lax.broadcasted_iota(jnp.int32, (8, 128), 0) // 2
    rows = slice(z * 256, (z + 1) * 256)
    res = []
    for q in range(4):
        k = r_base + q
        wh, wl = split(jnp.concatenate([r_ref[k, 0, rows, :], r_ref[k, 1, rows, :]], axis=1))
        rh_ref[g * 4 + q, rows, :] = wh
        rl_ref[g * 4 + q, rows, :] = wl
        acc = mm(lhs[q][1], wh, (1, 1))
        res.append(acc[:64] + (acc[64:] + mm(lhs[q][0], wl, (1, 1))))
    for xh_ in range(2):
        for part in range(8):
            v = [r[part * 8 : part * 8 + 8, xh_ * 128 : xh_ * 128 + 128] for r in res]
            out = oth if part // 4 else own
            for y in range(4):
                out[z * 2 + xh_, (part % 2) * 4 + y, (part // 2) % 2, g * 8 : g * 8 + 8, :] = trade(
                    v, pair, y
                )


def forward_first_kernel(pos_ref, f_hbm, r_hbm, own, oth, rh, rl, ahead, f_ref, r_ref, fsem, sem, asem):
    def fetch_f(g):
        cut = pl.ds(g * 4, 4)
        return pltpu.make_async_copy(f_hbm.at[cut], f_ref.at[cut], fsem.at[g])

    def fetch(g, z):
        cut = (pl.ds(g * 4, 4), slice(None), pl.ds(z * 256, 256))
        return pltpu.make_async_copy(r_hbm.at[cut], r_ref.at[cut], sem.at[g * 4 + z])

    def fetch_ahead(k):
        return pltpu.make_async_copy(r_hbm.at[8 + k], ahead.at[k], asem.at[k])

    fetch_f(0).start()
    for z in range(4):
        fetch(0, z).start()
    fetch_f(1).start()
    perms = selections(pos_ref[0])
    fetch_f(0).wait()
    lhs = group_operand(perms, f_ref, 0)
    for z in range(4):
        fetch(0, z).wait()
        fetch(1, z).start()
        group_block(0, z, lhs, r_ref, 0, own, oth, rh, rl)
    fetch_f(1).wait()
    lhs = group_operand(perms, f_ref, 4)
    for z in range(4):
        fetch(1, z).wait()
        fetch_ahead(z).start()
    for z in range(4):
        group_block(1, z, lhs, r_ref, 4, own, oth, rh, rl)
    for k in range(4):
        fetch_ahead(k).wait()


def forward_second_kernel(pos_ref, f_hbm, r_hbm, ahead, own, oth, rh, rl, f_ref, r_ref, fsem, sem):
    def fetch(k):
        return pltpu.make_async_copy(r_hbm.at[12 + k], r_ref.at[k], sem.at[k])

    fcopy = pltpu.make_async_copy(f_hbm.at[pl.ds(8, 8)], f_ref, fsem)
    fcopy.start()
    for k in range(4):
        fetch(k).start()
    perms = selections(pos_ref[0])
    fcopy.wait()
    lhs = group_operand(perms, f_ref, 0)
    for z in range(4):
        group_block(0, z, lhs, ahead, 0, own, oth, rh, rl)
    lhs = group_operand(perms, f_ref, 4)
    for k in range(4):
        fetch(k).wait()
    for z in range(4):
        group_block(1, z, lhs, r_ref, 0, own, oth, rh, rl)


PANEL_HALF = jax.ShapeDtypeStruct((KB, 8, 2, 16, 128), F32)
R_HALF = jax.ShapeDtypeStruct((8, 1024, 256), BF16)
R_GROUP = (4, 2, 1024, 128)


def forward_first(pos, focusing, reflection):
    return pl.pallas_call(
        forward_first_kernel,
        in_specs=[SMEM, HBM, HBM],
        out_specs=[VMEM] * 5,
        out_shape=[PANEL_HALF] * 2 + [R_HALF] * 2 + [jax.ShapeDtypeStruct(R_GROUP, F32)],
        scratch_shapes=[
            pltpu.VMEM((8, 2, 32, 128), F32),
            pltpu.VMEM((8, 2, 1024, 128), F32),
            pltpu.SemaphoreType.DMA((2,)),
            pltpu.SemaphoreType.DMA((8,)),
            pltpu.SemaphoreType.DMA((4,)),
        ],
        compiler_params=params(16),
        cost_estimate=pl.CostEstimate(flops=3 * 2**29, bytes_accessed=14 * 2**20, transcendentals=0),
        name="forward_first",
    )(pos, focusing, reflection)


def forward_second(pos, focusing, reflection, ahead):
    return pl.pallas_call(
        forward_second_kernel,
        in_specs=[SMEM, HBM, HBM, VMEM],
        out_specs=[VMEM] * 4,
        out_shape=[PANEL_HALF] * 2 + [R_HALF] * 2,
        scratch_shapes=[
            pltpu.VMEM((8, 2, 32, 128), F32),
            pltpu.VMEM(R_GROUP, F32),
            pltpu.SemaphoreType.DMA,
            pltpu.SemaphoreType.DMA((4,)),
        ],
        compiler_params=params(12),
        cost_estimate=pl.CostEstimate(flops=3 * 2**29, bytes_accessed=10 * 2**20, transcendentals=0),
        name="forward_second",
    )(pos, focusing, reflection, ahead)


def combine_kernel(own0, oth0, own1, oth1, out_ref):
    out_ref[:, :, 0] = own0[...] + oth0[...]
    out_ref[:, :, 1] = own1[...] + oth1[...]


def combine(own0, oth0, own1, oth1):
    return pl.pallas_call(
        combine_kernel,
        in_specs=[VMEM] * 4,
        out_specs=VMEM,
        out_shape=jax.ShapeDtypeStruct((KB, 8, 2, 2, 16, 128), F32),
        compiler_params=params(4),
        name="combine",
    )(own0, oth0, own1, oth1)


def source_kernel(pos_ref, th_ref, tl_ref, tth_ref, ttl_ref, mute_ref, x_ref, time_ref, out_ref):
    y = pos_ref[2]
    cols = []
    for j in range(2):
        groups = []
        for f in range(KB):
            for h in range(2):
                t = [x_ref[f, i, h, j] for i in range(8)]
                groups.append(((t[0] + t[1]) + (t[2] + t[3])) + ((t[4] + t[5]) + (t[6] + t[7])))
        x = jnp.concatenate(groups, axis=0)
        cols.append(unturn(x.reshape(32, 8, 128), y, -1).reshape(256, 128))
    up = mm3((th_ref[...], tl_ref[...]), split(jnp.concatenate(cols, axis=1)))
    t = lax.broadcasted_iota(jnp.int32, (NT, 128), 0)
    kept = []
    for j in range(2):
        mute = jnp.broadcast_to(mute_ref[j : j + 1, :], (NT, 128))
        val = jnp.where((t < mute) | (t > NT - mute), up[:, j * 128 : (j + 1) * 128], 0.0)
        time_ref[pl.ds(j, NT, stride=2), :] = val
        kept.append(val)
    back = mm3((tth_ref[...], ttl_ref[...]), split(jnp.concatenate(kept, axis=1)))
    for j in range(2):
        b = unturn(back[:, j * 128 : (j + 1) * 128].reshape(32, 8, 128), y, 1)
        b = b.reshape(KB, 2, 16, 128)
        for f in range(KB):
            for h in range(2):
                for i in range(8):
                    out_ref[f, i, h, j] = b[f, h]


def source_traces(pos, tables, mute, parts):
    return pl.pallas_call(
        source_kernel,
        in_specs=[SMEM] + [VMEM] * 6,
        out_specs=[VMEM] * 2,
        out_shape=[
            jax.ShapeDtypeStruct((NT * 2, 128), F32),
            jax.ShapeDtypeStruct((KB, 8, 2, 2, 16, 128), F32),
        ],
        compiler_params=params(8),
        name="source_traces",
    )(pos, *tables, mute, parts)


def adjoint_kernel(second, own, oth, rh0, rl0, rh1, rl1, *rest):
    out_ref = rest[-1]
    pair = lax.broadcasted_iota(jnp.int32, (8, 128), 0) // 2
    even = (lax.broadcasted_iota(jnp.int32, (64, 128), 0) % 2) == 0
    for half, (rh_ref, rl_ref) in enumerate(((rh0, rl0), (rh1, rl1))):
        for g in range(2):
            acc = [None] * 4
            for zz in range(2):
                lhs = [[None] * 2 for _ in range(4)]
                for xh_ in range(2):
                    tiles = [[] for _ in range(4)]
                    f = zz * 2 + xh_
                    for part in range(8):
                        j, xlo = part // 4, part % 2
                        g8 = slice(g * 8, g * 8 + 8)
                        if (part // 2) % 2:
                            v = [oth[f, xlo * 4 + y, half, j, g8, :] for y in range(4)]
                        else:
                            v = [own[second * 4 + f, xlo * 4 + y, half, j, g8, :] for y in range(4)]
                        for q in range(4):
                            tiles[q].append(trade(v, pair, q))
                    for q in range(4):
                        lhs[q][xh_] = jnp.concatenate(tiles[q], axis=0)
                z = second * 2 + zz
                rows = slice(z * 256, (z + 1) * 256)
                for q in range(4):
                    bh, bl = split(jnp.concatenate(lhs[q], axis=1))
                    wh, wl = rh_ref[g * 4 + q, rows, :], rl_ref[g * 4 + q, rows, :]
                    both = mm(jnp.concatenate([bh, bl], axis=0), wh)
                    add = both[:64] + (both[64:] + mm(bh, wl))
                    acc[q] = add if acc[q] is None else acc[q] + add
            res = []
            for q in range(4):
                a, b = acc[q][:, :128], acc[q][:, 128:]
                res.append(a + jnp.where(even, pltpu.roll(b, 63, 0), -pltpu.roll(b, 1, 0)))
            out8 = slice(half * 16 + g * 8, half * 16 + g * 8 + 8)
            for part in range(8):
                v = [r[part * 8 : part * 8 + 8] for r in res]
                for y in range(4):
                    at = ((part % 2) * 4 + y, part // 2, out8, slice(None))
                    t = trade(v, pair, y)
                    out_ref[at] = rest[0][at] + t if second else t


def adjoint_panel(second, own, oth, halves, *before):
    return pl.pallas_call(
        functools.partial(adjoint_kernel, second),
        in_specs=[VMEM] * (6 + len(before)),
        out_specs=VMEM,
        out_shape=jax.ShapeDtypeStruct((8, 4, 32, 128), F32),
        compiler_params=params(8),
        cost_estimate=pl.CostEstimate(flops=3 * 2**29, bytes_accessed=2**20, transcendentals=0),
        name=f"adjoint_panel{second}",
    )(own, oth, *halves, *before)


def receiver_kernel(pos_ref, th_ref, tl_ref, mute_ref, direct_ref, x_ref, out_ref):
    even = pos_ref[0] == 0
    turn = pos_ref[1]
    t = lax.broadcasted_iota(jnp.int32, (NT, 128), 0)
    for c in range(2):
        cols = []
        for j in range(2):
            a = jnp.where(even, x_ref[:, j * 2 + c], x_ref[:, j * 2 + 1 - c])
            cols.append(unturn(a.reshape(32, 8, 128), turn, -1).reshape(256, 128))
        adj = mm3((th_ref[...], tl_ref[...]), split(jnp.concatenate(cols, axis=1)))
        for j in range(2):
            p = c * 2 + j
            mute = jnp.broadcast_to(mute_ref[p : p + 1, :], (NT, 128))
            val = jnp.where((t < mute) | (t > NT - mute), adj[:, j * 128 : (j + 1) * 128], 0.0)
            rows = pl.ds(p, NT, stride=4)
            out_ref[rows, :] = direct_ref[rows, :] - val


def receiver_traces(pos, tables, mute, direct, x):
    return pl.pallas_call(
        receiver_kernel,
        in_specs=[SMEM] + [VMEM] * 5,
        out_specs=VMEM,
        out_shape=jax.ShapeDtypeStruct((NT * 4, 128), F32),
        compiler_params=params(8),
        name="receiver_traces",
    )(pos, *tables, mute, direct, x)


CHIPS = ("z", "xh", "xl", "y")
SWAP = [(0, 1), (1, 0)]


def exchange(x, axes):
    whole = x.reshape((64,) + x.shape[2:]) if len(axes) == 4 else x
    return lax.all_to_all(whole, axes, split_axis=0, concat_axis=0, tiled=True).reshape(x.shape)


def body(reflection, focusing, direct_wave, mute_source, mute_receiver):
    core, z, y = lax.axis_index("c"), lax.axis_index("z"), lax.axis_index("y")
    pos = jnp.stack([core, (z & 1) * 2 + lax.axis_index("xh"), y])
    table = dft_table()
    th, tl = split_const(table)

    focusing = pltpu.with_memory_space_constraint(focusing, pltpu.HBM)
    reflection = pltpu.with_memory_space_constraint(reflection, pltpu.HBM)
    own0, oth0, rh0, rl0, ahead = forward_first(pos, focusing, reflection)
    own1, oth1, rh1, rl1 = forward_second(pos, focusing, reflection, ahead)
    panel = combine(own0, lax.ppermute(oth0, "c", SWAP), own1, lax.ppermute(oth1, "c", SWAP))
    parts = exchange(panel, CHIPS)
    time, back = source_traces(pos, (th, tl, th.T, tl.T), mute_source, parts)
    b_own = exchange(back, CHIPS)
    halves = (rh0, rl0, rh1, rl1)
    b_oth = [lax.ppermute(b_own[i * 4 : i * 4 + 4], "c", SWAP) for i in range(2)]
    adjoint = adjoint_panel(0, b_own, b_oth[0], halves)
    adjoint = adjoint_panel(1, b_own, b_oth[1], halves, adjoint)
    received = exchange(adjoint, ("z", "xh"))
    plus = receiver_traces(
        pos, (th, tl), mute_receiver, direct_wave.reshape(NT * 4, 128), received
    )
    return time.reshape(NT, 2, 128), plus.reshape(NT, 4, 128)


def solution(mesh):
    fine = Mesh(mesh.devices.reshape(4, 2, 2, 4, 2), ("z", "xh", "xl", "y", "c"))
    freq, rcv = ("z", "xh"), ("xl", "y", "c")
    return jax.shard_map(
        body,
        mesh=fine,
        in_specs=(
            P(freq, None, None, rcv),
            P(freq, None, None, rcv),
            P(None, freq, rcv),
            P(rcv, freq),
            P(freq, rcv),
        ),
        out_specs=(P(None, rcv, freq), P(None, freq, rcv)),
        check_vma=False,
    )
```

time: 119 us -> 119 us (level)
  waiting for transfers between devices: 8.3 us -> 4.44 us
  Pallas kernels: 17.8 us -> 20.6 us
    ppermute x2 -> x4, waiting for transfers between devices: 8.3 us -> 4.44 us  [the longest x1 2.28 us: body(): lax.ppermute(oth1, 'c', SWAP)]
    pallas_call x2 -> x5, Pallas kernels: 14.1 us -> 16.9 us  [the longest x1 7.75 us: forward_first(): pl.pallas_call(forward_first_kernel, in_specs=[SMEM, HBM, HBM], out_specs...]
  transfers between devices with their start and end apart: 2 -> 4, of which waited for: 2 -> 2; matrix products, arithmetic and copies ran while one was open for 0% -> 0% of each run, Pallas kernels for 0% -> 6%
where the time goes in v4:
time: 119 us
  blocking collectives  91.8 us (77%)
  Pallas kernels  20.6 us (17%)
  waiting for transfers between devices  4.44 us (4%)
  starting transfers between devices  1.24 us (1%)
    all_to_all x3, blocking collectives, exchange(): lax.all_to_all(whole, axes, split_axis=0, concat_axis=0, tiled=True)  91.8 us
    pallas_call x1, Pallas kernels, forward_first(): pl.pallas_call(forward_first_kernel, in_specs=[SMEM, HBM, HBM], out_specs...  7.75 us
    pallas_call x1, Pallas kernels, forward_second(): pl.pallas_call(forward_second_kernel, in_specs=[SMEM, HBM, HBM, VMEM], ou...  5.63 us
    pallas_call x2, Pallas kernels, adjoint_panel(): pl.pallas_call(functools.partial(adjoint_kernel, second), in_specs=[VMEM]...  3.3 us
  transfers between devices with their start and end apart: 4, of which 2 were waited for; matrix products, arithmetic and copies ran while one was open for 0% of the time, Pallas kernels for 6%

profile of v4, /device:TPU:0, one launch (start us, length us, event | category | flops | bytes accessed | tf_op | source)
XLA Modules:
  0.0 119.1 jit_solution(7018727228650183821)
XLA Ops:
  0.6 0.1 pad_add_fusion.pos_ref
  0.7 7.7 %forward_first.1 = (f32[8,8,2,16,128]{4,3,2,1,0:T(8,128)S(1)}, f32[8,8,2,16,128]{4,3,2,1,0:T(8,128)S(1)}, bf16[8,1024,256]{2,1,0:T(8,128)(2,1)S(1)}, bf16[8,1024...) custom-call(s32[3]{0:T(128)S(1)} %pad_add_fusion.pos_ref, f32[16,2,32,128]{3,2,1,0:T(8,128)} %f_hbm.3, f32[16,2,1024,128]{3,2,1,0:T(8,128)} %r_hbm.3), custom_call_target="tpu_custom_call" | custom-call | flops 1610612736 | bytes 14680064 | tf_op jit(solution)/shard_map/forward_first/pallas_call | solution.py:171
  8.5 0.1 collective-permute-start
  8.6 5.6 %forward_second.1 = (f32[8,8,2,16,128]{4,3,2,1,0:T(8,128)S(1)}, f32[8,8,2,16,128]{4,3,2,1,0:T(8,128)S(1)}, bf16[8,1024,256]{2,1,0:T(8,128)(2,1)S(1)}, bf16[8,1024,256]{2,1,0:T(8,128)(2,1)S(1)}) custom-call(s32[3]{0:T(128)S(1)} %pad_add_fusion.pos_ref, f32[16,2,32,128]{3,2,1,0:T(8,128)} %f_hbm.3, f32[16,2,1024,128]{3,2,1,0:T(8,128)} %r_hbm.3, ...), custom_call_target="tpu_custom_call" | custom-call | flops 1610612736 | bytes 10485760 | tf_op jit(solution)/shard_map/forward_second/pallas_call | solution.py:190
  14.2 0.6 collective-permute-start.1
  14.8 0.0 collective-permute-done.oth0
  14.8 2.3 %collective-permute-done.1.oth1 = f32[8,8,2,16,128]{4,3,2,1,0:T(8,128)S(1)} collective-permute-done((f32[8,8,2,16,128]{4,3,2,1,0:T(8,128)S(1)}, f32[8,8,2,16,128]{4,3,2,1,0:T(8,128)S(1)}, u32[]{:S(2)}, u32[]{:S(2)}) %collective-permute-start.1) | collective-permute-done | bytes 1048608 | tf_op jit(solution)/shard_map/ppermute | solution.py:370
  17.1 0.0 copy-start.1
  17.1 0.0 copy-start.2
  17.1 0.0 copy-start.3
  17.1 0.0 copy-start.4
  17.1 0.0 copy-start.6
  17.1 0.2 combine.1
  17.3 41.6 %all_to_all.15 = f32[64,2,2,16,128]{4,3,2,1,0:T(8,128)S(1)} all-to-all(f32[64,2,2,16,128]{4,3,2,1,0:T(8,128)S(1)} %bitcast.14), channel_id=1, replica_groups=mesh['z'=4,'xh'=2,'xl'=2,'y'=4,'c'=2] {'z','xh','xl','y'}, dimensions={0} | all-to-all | bytes 4194304 | tf_op jit(solution)/shard_map/all_to_all | solution.py:357
  58.9 0.0 copy-done.1
  58.9 0.0 copy-done.2
  58.9 0.0 copy-done.3
  58.9 0.0 copy-done.4
  58.9 0.0 copy-done.6
  58.9 1.8 %source_traces.1 = (f32[512,128]{1,0:T(8,128)}, f32[8,8,2,2,16,128]{5,4,3,2,1,0:T(8,128)S(1)}) custom-call(s32[3]{0:T(128)S(1)} %pad_add_fusion.pos_ref, bf16[256,256]{1,0:T(8,128)(2,1)S(1)} %copy-done.2, bf16[256,256]{1,0:T(8,128)(2,1)S(1)} %copy-done.1, bf16[256,256]{1,0:T(8,128)(2,1)S(1)} %copy-done.4, bf16[256,256]{1,0:T(8,128)(2,1)S(1)} %copy-done.3, ...), custom_call_target="tpu_custom_call" | custom-call | tf_op jit(solution)/shard_map/source_traces/pallas_call | solution.py:253
  60.7 34.7 %all_to_all.16 = f32[64,2,2,16,128]{4,3,2,1,0:T(8,128)S(1)} all-to-all(f32[64,2,2,16,128]{4,3,2,1,0:T(8,128)S(1)} %bitcast.16), channel_id=1, replica_groups=mesh['z'=4,'xh'=2,'xl'=2,'y'=4,'c'=2] {'z','xh','xl','y'}, dimensions={0} | all-to-all | bytes 4194304 | tf_op jit(solution)/shard_map/all_to_all | solution.py:357
  95.4 0.2 fusion
  95.6 0.1 collective-permute-start.3
  95.7 0.5 collective-permute-start.2
  96.2 2.1 %collective-permute-done.3.oth = f32[4,8,2,2,16,128]{5,4,3,2,1,0:T(8,128)S(1)} collective-permute-done((f32[4,8,2,2,16,128]{5,4,3,2,1,0:T(8,128)S(1)}, f32[4,8,2,2,16,128]{5,4,3,2,1,0:T(8,128)S(1)}, u32[]{:S(2)}, u32[]{:S(2)}) %collective-permute-start.3) | collective-permute-done | bytes 1048608 | tf_op jit(solution)/shard_map/ppermute | solution.py:375
  98.3 1.6 %adjoint_panel0.1.rest_0_ = f32[8,4,32,128]{3,2,1,0:T(8,128)S(1)} custom-call(f32[8,8,2,2,16,128]{5,4,3,2,1,0:T(8,128)S(1)} %bitcast.12, f32[4,8,2,2,16,128]{5,4,3,2,1,0:T(8,128)S(1)} %collective-permute-done.3.oth, bf16[8,1024,256]{2,1,0:T(8,128)(2,1)S(1)} %get-tuple-element.20.rh0, bf16[8,1024,256]{2,1,0:T(8,128)(2,1)S(1)} %get-tuple-element.21.rl0, ...), custom_call_target="tpu_custom_call" | custom-call | flops 1610612736 | bytes 1048576 | tf_op jit(solution)/shard_map/adjoint_panel0/pallas_call | solution.py:311
  100.0 0.0 copy-start
  100.0 0.0 copy-start.5
  100.0 0.0 collective-permute-done.2.oth
  100.0 1.7 %adjoint_panel1.1 = f32[8,4,32,128]{3,2,1,0:T(8,128)S(1)} custom-call(f32[8,8,2,2,16,128]{5,4,3,2,1,0:T(8,128)S(1)} %bitcast.13, f32[4,8,2,2,16,128]{5,4,3,2,1,0:T(8,128)S(1)} %collective-permute-done.2.oth, bf16[8,1024,256]{2,1,0:T(8,128)(2,1)S(1)} %get-tuple-element.20.rh0, bf16[8,1024,256]{2,1,0:T(8,128)(2,1)S(1)} %get-tuple-element.21.rl0, ...), custom_call_target="tpu_custom_call" | custom-call | flops 1610612736 | bytes 1048576 | tf_op jit(solution)/shard_map/adjoint_panel1/pallas_call | solution.py:311
  101.7 15.6 %all_to_all.17.x_ref = f32[8,4,32,128]{3,2,1,0:T(8,128)S(1)} all-to-all(f32[8,4,32,128]{3,2,1,0:T(8,128)S(1)} %adjoint_panel1.1), channel_id=1, replica_groups=mesh['z'=4,'xh'=2,'xl'=2,'y'=4,'c'=2] {'z','xh'}, dimensions={0} | all-to-all | bytes 1048576 | tf_op jit(solution)/shard_map/all_to_all | solution.py:357
  117.3 0.0 copy-done
  117.3 0.0 copy-done.5
  117.3 1.9 %receiver_traces.1 = f32[1024,128]{1,0:T(8,128)} custom-call(s32[3]{0:T(128)S(1)} %pad_add_fusion.pos_ref, bf16[256,256]{1,0:T(8,128)(2,1)S(1)} %copy-done.2, bf16[256,256]{1,0:T(8,128)(2,1)S(1)} %copy-done.1, s32[4,128]{1,0:T(4,128)S(1)} %copy-done.5, f32[1024,128]{1,0:T(8,128)S(1)} %bitcast.17, f32[8,4,32,128]{3,2,1,0:T(8,128)S(1)} %all_to_all.17.x_ref), custom_call_target="tpu_custom_call" | custom-call | tf_op jit(solution)/shard_map/receiver_traces/pallas_call | solution.py:341
Async XLA Ops:
  8.5 6.3 %collective-permute-start = (f32[8,8,2,16,128]{4,3,2,1,0:T(8,128)S(1)}, f32[8,8,2,16,128]{4,3,2,1,0:T(8,128)S(1)}, u32[]{:S(2)}, u32[]{:S(2)}) collective-permute-start(f32[8,8,2,16,128]{4,3,2,1,0:T(8,128)S(1)} %get-tuple-element.14), channel_id=1, source_target_pairs={{0,1},{1,0},{2,3},{3,2},{4,5},{5,4},{6,7},{7,6},{8,9},{9,8},{10,11... | collective-permute-start | bytes 3145736 | tf_op jit(solution)/shard_map/ppermute | solution.py:370
  14.2 2.9 %collective-permute-start.1 = (f32[8,8,2,16,128]{4,3,2,1,0:T(8,128)S(1)}, f32[8,8,2,16,128]{4,3,2,1,0:T(8,128)S(1)}, u32[]{:S(2)}, u32[]{:S(2)}) collective-permute-start(f32[8,8,2,16,128]{4,3,2,1,0:T(8,128)S(1)} %get-tuple-element.17), channel_id=1, source_target_pairs={{0,1},{1,0},{2,3},{3,2},{4,5},{5,4},{6,7},{7,6},{8,9},{9,8},{10,11... | collective-permute-start | bytes 3145736 | tf_op jit(solution)/shard_map/ppermute | solution.py:370
  17.1 41.8 %copy-start.1 = (bf16[256,256]{1,0:T(8,128)(2,1)S(1)}, bf16[256,256]{1,0:T(8,128)(2,1)}, u32[]{:S(2)}) copy-start(bf16[256,256]{1,0:T(8,128)(2,1)} %constant.29.clone.tl_ref) | copy-start | bytes 393220
  17.1 41.8 %copy-start.2 = (bf16[256,256]{1,0:T(8,128)(2,1)S(1)}, bf16[256,256]{1,0:T(8,128)(2,1)}, u32[]{:S(2)}) copy-start(bf16[256,256]{1,0:T(8,128)(2,1)} %constant.28.clone.th_ref) | copy-start | bytes 393220
  17.1 41.8 %copy-start.3 = (bf16[256,256]{1,0:T(8,128)(2,1)S(1)}, bf16[256,256]{1,0:T(8,128)(2,1)}, u32[]{:S(2)}) copy-start(bf16[256,256]{1,0:T(8,128)(2,1)} %constant.31.clone.ttl_ref) | copy-start | bytes 393220
  17.1 41.8 %copy-start.4 = (bf16[256,256]{1,0:T(8,128)(2,1)S(1)}, bf16[256,256]{1,0:T(8,128)(2,1)}, u32[]{:S(2)}) copy-start(bf16[256,256]{1,0:T(8,128)(2,1)} %constant.30.clone.tth_ref) | copy-start | bytes 393220
  17.1 41.8 %copy-start.6 = (s32[2,128]{1,0:T(2,128)S(1)}, s32[2,128]{1,0:T(2,128)}, u32[]{:S(2)}) copy-start(s32[2,128]{1,0:T(2,128)} %mute_ref.2) | copy-start | bytes 3076
  95.6 2.7 %collective-permute-start.3 = (f32[4,8,2,2,16,128]{5,4,3,2,1,0:T(8,128)S(1)}, f32[4,8,2,2,16,128]{5,4,3,2,1,0:T(8,128)S(1)}, u32[]{:S(2)}, u32[]{:S(2)}) collective-permute-start(f32[4,8,2,2,16,128]{5,4,3,2,1,0:T(8,128)S(1)} %bitcast.19), channel_id=1, source_target_pairs={{0,1},{1,0},{2,3},{3,2},{4,5},{5,4},{6,7},{7,6},{8,9},{9,8},{10,11... | collective-permute-start | bytes 3145736 | tf_op jit(solution)/shard_map/ppermute | solution.py:375
  95.7 4.3 %collective-permute-start.2 = (f32[4,8,2,2,16,128]{5,4,3,2,1,0:T(8,128)S(1)}, f32[4,8,2,2,16,128]{5,4,3,2,1,0:T(8,128)S(1)}, u32[]{:S(2)}, u32[]{:S(2)}) collective-permute-start(f32[4,8,2,2,16,128]{5,4,3,2,1,0:T(8,128)S(1)} %bitcast.18), channel_id=1, source_target_pairs={{0,1},{1,0},{2,3},{3,2},{4,5},{5,4},{6,7},{7,6},{8,9},{9,8},{10,11... | collective-permute-start | bytes 3145736 | tf_op jit(solution)/shard_map/ppermute | solution.py:375
  100.0 17.3 %copy-start = (f32[256,4,128]{2,1,0:T(4,128)S(1)}, f32[256,4,128]{2,1,0:T(4,128)}, u32[]{:S(2)}) copy-start(f32[256,4,128]{2,1,0:T(4,128)} %param.11) | copy-start | bytes 1572868
  100.0 17.3 %copy-start.5 = (s32[4,128]{1,0:T(4,128)S(1)}, s32[4,128]{1,0:T(4,128)}, u32[]{:S(2)}) copy-start(s32[4,128]{1,0:T(4,128)} %mute_ref.3) | copy-start | bytes 6148

commit v5 on v3

--- a/solution.py
+++ b/solution.py
@@ -1,3 +1,4 @@
+import functools
 import math
 
 import numpy as np
@@ -61,18 +62,42 @@
     return out
 
 
-def forward_kernel(pos_ref, f_hbm, r_hbm, own, oth, rh_ref, rl_ref, f_ref, r_ref, fsem, sem):
+def place(z, xh, xl, y):
+    return z * 16 + ((xh * 2 + xl - y) % 4) * 4 + y
+
+
+def place_groups():
+    order = [None] * 64
+    for z in range(4):
+        for xh in range(2):
+            for xl in range(2):
+                for y in range(4):
+                    order[place(z, xh, xl, y)] = ((z * 2 + xh) * 2 + xl) * 4 + y
+    return [[chip * 2 + core for chip in order] for core in range(2)]
+
+
+AHEAD = 6
+
+
+def forward_kernel(pos_ref, f_hbm, r_hbm, own, oth, rh_ref, rl_ref, f_ref, r_ref, fsem, zsem, sem):
     def fetch_f(g):
         cut = pl.ds(g * 4, 4)
         return pltpu.make_async_copy(f_hbm.at[cut], f_ref.at[cut], fsem.at[g])
 
-    def fetch(g, z):
-        cut = (pl.ds(g * 4, 4), slice(None), pl.ds(z * 256, 256))
-        return pltpu.make_async_copy(r_hbm.at[cut], r_ref.at[cut], sem.at[g * 4 + z])
+    def fetch_first(z):
+        cut = (pl.ds(0, 4), slice(None), pl.ds(z * 256, 256))
+        return pltpu.make_async_copy(r_hbm.at[cut], r_ref.at[cut], zsem.at[z])
+
+    def fetch(k):
+        return pltpu.make_async_copy(r_hbm.at[k], r_ref.at[k], sem.at[k - 4])
 
     fetch_f(0).start()
     for z in range(4):
-        fetch(0, z).start()
+        fetch_first(z).start()
+    for k in range(4, AHEAD):
+        fetch(k).start()
+    for g in range(1, 4):
+        fetch_f(g).start()
     core = pos_ref[0]
     row = lax.broadcasted_iota(jnp.int32, (64, 64), 0)
     col = lax.broadcasted_iota(jnp.int32, (64, 64), 1)
@@ -84,9 +109,7 @@
         perms.append(jnp.where(col == src, 1.0, 0.0).astype(BF16))
     pair = lax.broadcasted_iota(jnp.int32, (8, 128), 0) // 2
 
-    @pl.loop(0, 4)
-    def _(g):
-        fetch_f(g).wait()
+    def operands(g):
         lhs = []
         for q in range(4):
             fr, fi = f_ref[g * 4 + q, 0], f_ref[g * 4 + q, 1]
@@ -96,39 +119,50 @@
             xh, xl = split(x)
             ph, plo = mm(perms[q], xh).astype(BF16), mm(perms[q], xl).astype(BF16)
             lhs.append((ph, jnp.concatenate([ph, plo], axis=0)))
-        g8 = pl.ds(pl.multiple_of(g * 8, 8), 8)
-
-        @pl.when(g < 3)
-        def _():
-            fetch_f(g + 1).start()
+        return lhs
+
+    def block(g, g8, z, lhs):
+        rows = slice(z * 256, (z + 1) * 256)
+        res = []
+        for q in range(4):
+            k = g * 4 + q
+            wh, wl = split(jnp.concatenate([r_ref[k, 0, rows, :], r_ref[k, 1, rows, :]], axis=1))
+            rh_ref[k, rows, :] = wh
+            rl_ref[k, rows, :] = wl
+            acc = mm(lhs[q][1], wh, (1, 1))
+            res.append(acc[:64] + (acc[64:] + mm(lhs[q][0], wl, (1, 1))))
+        for xh_ in range(2):
+            for part in range(8):
+                v = [r[part * 8 : part * 8 + 8, xh_ * 128 : xh_ * 128 + 128] for r in res]
+                out = oth if part // 4 else own
+                for y in range(4):
+                    out[place(z, xh_, part % 2, y), (part // 2) % 2, g8, :] = trade(v, pair, y)
+
+    fetch_f(0).wait()
+    lhs0 = operands(0)
+    for z in range(4):
+        fetch_first(z).wait()
+        fetch(AHEAD + z).start()
+        block(0, slice(0, 8), z, lhs0)
+
+    @pl.loop(1, 4)
+    def _(g):
+        fetch_f(g).wait()
+        lhs = operands(g)
+        for q in range(4):
+            k = g * 4 + q
+            fetch(k).wait()
+
+            @pl.when(k + AHEAD < KK)
+            def _():
+                fetch(k + AHEAD).start()
 
         for z in range(4):
-            fetch(g, z).wait()
-
-            @pl.when(g < 3)
-            def _():
-                fetch(g + 1, z).start()
-
-        for z in range(4):
-            rows = slice(z * 256, (z + 1) * 256)
-            res = []
-            for q in range(4):
-                k = g * 4 + q
-                wh, wl = split(jnp.concatenate([r_ref[k, 0, rows, :], r_ref[k, 1, rows, :]], axis=1))
-                rh_ref[k, rows, :] = wh
-                rl_ref[k, rows, :] = wl
-                acc = mm(lhs[q][1], wh, (1, 1))
-                res.append(acc[:64] + (acc[64:] + mm(lhs[q][0], wl, (1, 1))))
-            for xh_ in range(2):
-                for part in range(8):
-                    v = [r[part * 8 : part * 8 + 8, xh_ * 128 : xh_ * 128 + 128] for r in res]
-                    out = oth if part // 4 else own
-                    for y in range(4):
-                        out[z * 2 + xh_, (part % 2) * 4 + y, (part // 2) % 2, g8, :] = trade(v, pair, y)
+            block(g, pl.ds(pl.multiple_of(g * 8, 8), 8), z, lhs)
 
 
 def forward_panel(pos, focusing, reflection):
-    panel = jax.ShapeDtypeStruct((KB, 8, 2, 32, 128), F32)
+    panel = jax.ShapeDtypeStruct((64, 2, 32, 128), F32)
     half = jax.ShapeDtypeStruct((KK, 1024, 256), BF16)
     return pl.pallas_call(
         forward_kernel,
@@ -139,7 +173,8 @@
             pltpu.VMEM((KK, 2, 32, 128), F32),
             pltpu.VMEM((KK, 2, 1024, 128), F32),
             pltpu.SemaphoreType.DMA((4,)),
-            pltpu.SemaphoreType.DMA((16,)),
+            pltpu.SemaphoreType.DMA((4,)),
+            pltpu.SemaphoreType.DMA((12,)),
         ],
         compiler_params=params(24),
         cost_estimate=pl.CostEstimate(flops=3 * 2**30, bytes_accessed=21 * 2**20, transcendentals=0),
@@ -148,15 +183,15 @@
 
 
 def source_kernel(pos_ref, th_ref, tl_ref, tth_ref, ttl_ref, mute_ref, x_ref, time_ref, out_ref):
-    y = pos_ref[2]
+    turn = pos_ref[2]
     cols = []
     for j in range(2):
         groups = []
         for f in range(KB):
-            t = [x_ref[f, i, j] for i in range(8)]
+            t = [x_ref[place(f // 2, f % 2, i // 4, i % 4), j] for i in range(8)]
             groups.append(((t[0] + t[1]) + (t[2] + t[3])) + ((t[4] + t[5]) + (t[6] + t[7])))
         x = jnp.concatenate(groups, axis=0)
-        cols.append(unturn(x.reshape(32, 8, 128), y, -1).reshape(256, 128))
+        cols.append(unturn(x.reshape(32, 8, 128), turn, -1).reshape(256, 128))
     up = mm3((th_ref[...], tl_ref[...]), split(jnp.concatenate(cols, axis=1)))
     t = lax.broadcasted_iota(jnp.int32, (NT, 128), 0)
     kept = []
@@ -167,10 +202,11 @@
         kept.append(val)
     back = mm3((tth_ref[...], ttl_ref[...]), split(jnp.concatenate(kept, axis=1)))
     for j in range(2):
-        b = unturn(back[:, j * 128 : (j + 1) * 128].reshape(32, 8, 128), y, 1).reshape(KB, 32, 128)
+        b = unturn(back[:, j * 128 : (j + 1) * 128].reshape(32, 8, 128), turn, 1)
+        b = b.reshape(KB, 32, 128)
         for f in range(KB):
             for i in range(8):
-                out_ref[f, i, j] = b[f]
+                out_ref[place(f // 2, f % 2, i // 4, i % 4), j] = b[f]
 
 
 def source_traces(pos, tables, mute, parts):
@@ -180,14 +216,15 @@
         out_specs=[VMEM] * 2,
         out_shape=[
             jax.ShapeDtypeStruct((NT * 2, 128), F32),
-            jax.ShapeDtypeStruct((KB, 8, 2, 32, 128), F32),
+            jax.ShapeDtypeStruct((64, 2, 32, 128), F32),
         ],
         compiler_params=params(8),
         name="source_traces",
     )(pos, *tables, mute, parts)
 
 
-def adjoint_kernel(own, oth, rh_ref, rl_ref, out_ref):
+def adjoint_kernel(second, own, oth, rh_ref, rl_ref, *rest):
+    out_ref = rest[-1]
     pair = lax.broadcasted_iota(jnp.int32, (8, 128), 0) // 2
     even = (lax.broadcasted_iota(jnp.int32, (64, 128), 0) % 2) == 0
 
@@ -195,13 +232,17 @@
     def _(g):
         g8 = pl.ds(pl.multiple_of(g * 8, 8), 8)
         acc = [None] * 4
-        for z in range(4):
+        for zz in range(2):
+            z = second * 2 + zz
             lhs = [[None] * 2 for _ in range(4)]
             for xh_ in range(2):
                 tiles = [[] for _ in range(4)]
                 for part in range(8):
-                    ref = oth if (part // 2) % 2 else own
-                    v = [ref[z * 2 + xh_, (part % 2) * 4 + y, part // 4, g8, :] for y in range(4)]
+                    j, xlo = part // 4, part % 2
+                    if (part // 2) % 2:
+                        v = [oth[place(zz, xh_, xlo, y), j, g8, :] for y in range(4)]
+                    else:
+                        v = [own[place(z, xh_, xlo, y), j, g8, :] for y in range(4)]
                     for q in range(4):
                         tiles[q].append(trade(v, pair, q))
                 for q in range(4):
@@ -220,19 +261,21 @@
         for part in range(8):
             v = [r[part * 8 : part * 8 + 8] for r in res]
             for y in range(4):
-                out_ref[(part % 2) * 4 + y, part // 2, g8, :] = trade(v, pair, y)
-
-
-def adjoint_panel(own, oth, rh, rl):
+                at = ((part % 2) * 4 + y, part // 2, g8, slice(None))
+                t = trade(v, pair, y)
+                out_ref[at] = rest[0][at] + t if second else t
+
+
+def adjoint_panel(second, own, oth, rh, rl, *before):
     return pl.pallas_call(
-        adjoint_kernel,
-        in_specs=[VMEM] * 4,
+        functools.partial(adjoint_kernel, second),
+        in_specs=[VMEM] * (4 + len(before)),
         out_specs=VMEM,
         out_shape=jax.ShapeDtypeStruct((8, 4, 32, 128), F32),
         compiler_params=params(8),
-        cost_estimate=pl.CostEstimate(flops=3 * 2**30, bytes_accessed=2**20, transcendentals=0),
-        name="adjoint_panel",
-    )(own, oth, rh, rl)
+        cost_estimate=pl.CostEstimate(flops=3 * 2**29, bytes_accessed=2**20, transcendentals=0),
+        name=f"adjoint_panel{second}",
+    )(own, oth, rh, rl, *before)
 
 
 def receiver_kernel(pos_ref, th_ref, tl_ref, mute_ref, direct_ref, x_ref, out_ref):
@@ -264,13 +307,14 @@
     )(pos, *tables, mute, direct, x)
 
 
-CHIPS = ("z", "xh", "xl", "y")
 SWAP = [(0, 1), (1, 0)]
-
-
-def exchange(x, axes):
-    whole = x.reshape((-1,) + x.shape[-3:]) if len(axes) == 4 else x
-    return lax.all_to_all(whole, axes, split_axis=0, concat_axis=0, tiled=True).reshape(x.shape)
+EVERY = ("z", "xh", "xl", "y", "c")
+
+
+def exchange(x):
+    return lax.all_to_all(
+        x, EVERY, split_axis=0, concat_axis=0, tiled=True, axis_index_groups=place_groups()
+    )
 
 
 def body(reflection, focusing, direct_wave, mute_source, mute_receiver):
@@ -282,12 +326,13 @@
     focusing = pltpu.with_memory_space_constraint(focusing, pltpu.HBM)
     reflection = pltpu.with_memory_space_constraint(reflection, pltpu.HBM)
     own, oth, rh, rl = forward_panel(pos, focusing, reflection)
-    parts = exchange(own + lax.ppermute(oth, "c", SWAP), CHIPS)
+    parts = exchange(own + lax.ppermute(oth, "c", SWAP))
     time, back = source_traces(pos, (th, tl, th.T, tl.T), mute_source, parts)
-    b_own = exchange(back, CHIPS)
-    b_oth = lax.ppermute(b_own, "c", SWAP)
-    adjoint = adjoint_panel(b_own, b_oth, rh, rl)
-    received = exchange(adjoint, ("z", "xh"))
+    b_own = exchange(back)
+    b_oth = [lax.ppermute(b_own[i * 32 : i * 32 + 32], "c", SWAP) for i in range(2)]
+    adjoint = adjoint_panel(0, b_own, b_oth[0], rh, rl)
+    adjoint = adjoint_panel(1, b_own, b_oth[1], rh, rl, adjoint)
+    received = lax.all_to_all(adjoint, ("z", "xh"), split_axis=0, concat_axis=0, tiled=True)
     plus = receiver_traces(
         pos, (th, tl), mute_receiver, direct_wave.reshape(NT * 4, 128), received
     )

time: 119 us -> 117 us (0.983)
  waiting for transfers between devices: 8.3 us -> 6.3 us
    ppermute x2 -> x3, waiting for transfers between devices: 8.3 us -> 6.3 us  [the longest x1 4.15 us: body(): parts = exchange(own + lax.ppermute(oth, 'c', SWAP))]
    pallas_call x1 -> x2, Pallas kernels: 3.63 us -> 4.32 us  [adjoint_panel(): pl.pallas_call(functools.partial(adjoint_kernel, second), in_specs=[VMEM]...]
  transfers between devices with their start and end apart: 2 -> 3, of which waited for: 2 -> 2; matrix products, arithmetic and copies ran while one was open for 0% -> 0% of each run, Pallas kernels for 0% -> 2%
where the time goes in v5:
time: 117 us
  blocking collectives  90.4 us (77%)
  Pallas kernels  17.8 us (15%)
  waiting for transfers between devices  6.3 us (5%)
    all_to_all x2, blocking collectives, exchange(): lax.all_to_all(x, EVERY, split_axis=0, concat_axis=0, tiled=True, axis_in...  75.5 us
    all_to_all x1, blocking collectives, body(): lax.all_to_all(adjoint, ('z', 'xh'), split_axis=0, concat_axis=0, tiled=T...  15 us
    pallas_call x1, Pallas kernels, forward_panel(): pl.pallas_call(forward_kernel, in_specs=[SMEM, HBM, HBM], out_specs=[VMEM...  9.76 us
    pallas_call x2, Pallas kernels, adjoint_panel(): pl.pallas_call(functools.partial(adjoint_kernel, second), in_specs=[VMEM]...  4.32 us
    ppermute x1, waiting for transfers between devices, body(): parts = exchange(own + lax.ppermute(oth, 'c', SWAP))  4.15 us
  transfers between devices with their start and end apart: 3, of which 2 were waited for; matrix products, arithmetic and copies ran while one was open for 0% of the time, Pallas kernels for 2%

profile of v5, /device:TPU:0, one launch (start us, length us, event | category | flops | bytes accessed | tf_op | source)
XLA Modules:
  0.0 116.7 jit_solution(3015362755948788932)
XLA Ops:
  0.6 0.1 pad_add_fusion.pos_ref
  0.7 9.8 %forward_panel.1 = (f32[64,2,32,128]{3,2,1,0:T(8,128)S(1)}, f32[64,2,32,128]{3,2,1,0:T(8,128)S(1)}, bf16[16,1024,256]{2,1,0:T(8,128)(2,1)S(1)}, bf16[16,1024,256]{2,1,0:T(8,128)(2,1)S(1)}) custom-call(s32[3]{0:T(128)S(1)} %pad_add_fusion.pos_ref, f32[16,2,32,128]{3,2,1,0:T(8,128)} %f_hbm.1, f32[16,2,1024,128]{3,2,1,0:T(8,128)} %r_hbm.1), custom_call_target="tpu_custom_call" | custom-call | flops 3221225472 | bytes 22020096 | tf_op jit(solution)/shard_map/forward_panel/pallas_call | solution.py:167
  10.5 0.1 collective-permute-start
  10.6 4.1 %collective-permute-done = f32[64,2,32,128]{3,2,1,0:T(8,128)S(1)} collective-permute-done((f32[64,2,32,128]{3,2,1,0:T(8,128)S(1)}, f32[64,2,32,128]{3,2,1,0:T(8,128)S(1)}, u32[]{:S(2)}, u32[]{:S(2)}) %collective-permute-start) | collective-permute-done | bytes 2097184 | tf_op jit(solution)/shard_map/ppermute | solution.py:329
  14.7 0.5 add.7
  15.2 0.0 copy-start.1
  15.2 0.0 copy-start.2
  15.2 0.0 copy-start.3
  15.2 0.0 copy-start.4
  15.3 0.0 copy-start.6
  15.3 41.1 %all_to_all.15.x_ref = f32[64,2,32,128]{3,2,1,0:T(8,128)S(1)} all-to-all(f32[64,2,32,128]{3,2,1,0:T(8,128)S(1)} %add.7), channel_id=1, replica_groups={{0,10,20,30,8,18,28,6,16,26,4,14,24,2,12,22,32,42,52,62,40,50,60,38,48,..., dimensions={0} | all-to-all | bytes 4194304 | tf_op jit(solution)/shard_map/all_to_all | solution.py:315
  56.4 0.0 copy-done.1
  56.4 0.0 copy-done.2
  56.4 0.0 copy-done.3
  56.4 0.0 copy-done.4
  56.4 0.0 copy-done.6
  56.4 1.8 %source_traces.1 = (f32[512,128]{1,0:T(8,128)}, f32[64,2,32,128]{3,2,1,0:T(8,128)S(1)}) custom-call(s32[3]{0:T(128)S(1)} %pad_add_fusion.pos_ref, bf16[256,256]{1,0:T(8,128)(2,1)S(1)} %copy-done.2, bf16[256,256]{1,0:T(8,128)(2,1)S(1)} %copy-done.1, bf16[256,256]{1,0:T(8,128)(2,1)S(1)} %copy-done.4, bf16[256,256]{1,0:T(8,128)(2,1)S(1)} %copy-done.3, ...), custom_call_target="tpu_custom_call" | custom-call | tf_op jit(solution)/shard_map/source_traces/pallas_call | solution.py:213
  58.2 34.3 %all_to_all.16.own = f32[64,2,32,128]{3,2,1,0:T(8,128)S(1)} all-to-all(f32[64,2,32,128]{3,2,1,0:T(8,128)S(1)} %get-tuple-element.11), channel_id=1, replica_groups={{0,10,20,30,8,18,28,6,16,26,4,14,24,2,12,22,32,42,52,62,40,50,60,38,48,..., dimensions={0} | all-to-all | bytes 4194304 | tf_op jit(solution)/shard_map/all_to_all | solution.py:315
  92.6 0.2 fusion
  92.8 0.1 collective-permute-start.2
  92.8 0.5 collective-permute-start.1
  93.3 2.1 %collective-permute-done.2.oth = f32[32,2,32,128]{3,2,1,0:T(8,128)S(1)} collective-permute-done((f32[32,2,32,128]{3,2,1,0:T(8,128)S(1)}, f32[32,2,32,128]{3,2,1,0:T(8,128)S(1)}, u32[]{:S(2)}, u32[]{:S(2)}) %collective-permute-start.2) | collective-permute-done | bytes 1048608 | tf_op jit(solution)/shard_map/ppermute | solution.py:332
  95.5 2.1 %adjoint_panel0.1.rest_0_ = f32[8,4,32,128]{3,2,1,0:T(8,128)S(1)} custom-call(f32[64,2,32,128]{3,2,1,0:T(8,128)S(1)} %all_to_all.16.own, f32[32,2,32,128]{3,2,1,0:T(8,128)S(1)} %collective-permute-done.2.oth, bf16[16,1024,256]{2,1,0:T(8,128)(2,1)S(1)} %get-tuple-element.12.rh_ref, bf16[16,1024,256]{2,1,0:T(8,128)(2,1)S(1)} %get-tuple-element.13.rl_ref), custom_call_target="tpu_custom_call" | custom-call | flops 1610612736 | bytes 1048576 | tf_op jit(solution)/shard_map/adjoint_panel0/pallas_call | solution.py:270
  97.6 0.0 copy-start
  97.7 0.0 copy-start.5
  97.7 0.0 collective-permute-done.1.oth
  97.7 2.2 %adjoint_panel1.1 = f32[8,4,32,128]{3,2,1,0:T(8,128)S(1)} custom-call(f32[64,2,32,128]{3,2,1,0:T(8,128)S(1)} %all_to_all.16.own, f32[32,2,32,128]{3,2,1,0:T(8,128)S(1)} %collective-permute-done.1.oth, bf16[16,1024,256]{2,1,0:T(8,128)(2,1)S(1)} %get-tuple-element.12.rh_ref, bf16[16,1024,256]{2,1,0:T(8,128)(2,1)S(1)} %get-tuple-element.13.rl_ref, ...), custom_call_target="tpu_custom_call" | custom-call | flops 1610612736 | bytes 1048576 | tf_op jit(solution)/shard_map/adjoint_panel1/pallas_call | solution.py:270
  99.9 15.0 %all_to_all.17.x_ref = f32[8,4,32,128]{3,2,1,0:T(8,128)S(1)} all-to-all(f32[8,4,32,128]{3,2,1,0:T(8,128)S(1)} %adjoint_panel1.1), channel_id=1, replica_groups=mesh['z'=4,'xh'=2,'xl'=2,'y'=4,'c'=2] {'z','xh'}, dimensions={0} | all-to-all | bytes 1048576 | tf_op jit(solution)/shard_map/all_to_all | solution.py:335
  114.8 0.0 copy-done
  114.8 0.0 copy-done.5
  114.8 1.9 %receiver_traces.1 = f32[1024,128]{1,0:T(8,128)} custom-call(s32[3]{0:T(128)S(1)} %pad_add_fusion.pos_ref, bf16[256,256]{1,0:T(8,128)(2,1)S(1)} %copy-done.2, bf16[256,256]{1,0:T(8,128)(2,1)S(1)} %copy-done.1, s32[4,128]{1,0:T(4,128)S(1)} %copy-done.5, f32[1024,128]{1,0:T(8,128)S(1)} %bitcast.6, f32[8,4,32,128]{3,2,1,0:T(8,128)S(1)} %all_to_all.17.x_ref), custom_call_target="tpu_custom_call" | custom-call | tf_op jit(solution)/shard_map/receiver_traces/pallas_call | solution.py:300
Async XLA Ops:
  10.5 4.2 %collective-permute-start = (f32[64,2,32,128]{3,2,1,0:T(8,128)S(1)}, f32[64,2,32,128]{3,2,1,0:T(8,128)S(1)}, u32[]{:S(2)}, u32[]{:S(2)}) collective-permute-start(f32[64,2,32,128]{3,2,1,0:T(8,128)S(1)} %get-tuple-element.9), channel_id=1, source_target_pairs={{0,1},{1,0},{2,3},{3,2},{4,5},{5,4},{6,7},{7,6},{8,9},{9,8},{10,11... | collective-permute-start | bytes 6291464 | tf_op jit(solution)/shard_map/ppermute | solution.py:329
  15.2 41.2 %copy-start.1 = (bf16[256,256]{1,0:T(8,128)(2,1)S(1)}, bf16[256,256]{1,0:T(8,128)(2,1)}, u32[]{:S(2)}) copy-start(bf16[256,256]{1,0:T(8,128)(2,1)} %constant.29.clone.tl_ref) | copy-start | bytes 393220
  15.2 41.2 %copy-start.2 = (bf16[256,256]{1,0:T(8,128)(2,1)S(1)}, bf16[256,256]{1,0:T(8,128)(2,1)}, u32[]{:S(2)}) copy-start(bf16[256,256]{1,0:T(8,128)(2,1)} %constant.28.clone.th_ref) | copy-start | bytes 393220
  15.2 41.2 %copy-start.3 = (bf16[256,256]{1,0:T(8,128)(2,1)S(1)}, bf16[256,256]{1,0:T(8,128)(2,1)}, u32[]{:S(2)}) copy-start(bf16[256,256]{1,0:T(8,128)(2,1)} %constant.31.clone.ttl_ref) | copy-start | bytes 393220
  15.2 41.2 %copy-start.4 = (bf16[256,256]{1,0:T(8,128)(2,1)S(1)}, bf16[256,256]{1,0:T(8,128)(2,1)}, u32[]{:S(2)}) copy-start(bf16[256,256]{1,0:T(8,128)(2,1)} %constant.30.clone.tth_ref) | copy-start | bytes 393220
  15.3 41.2 %copy-start.6 = (s32[2,128]{1,0:T(2,128)S(1)}, s32[2,128]{1,0:T(2,128)}, u32[]{:S(2)}) copy-start(s32[2,128]{1,0:T(2,128)} %mute_ref.2) | copy-start | bytes 3076
  92.8 2.7 %collective-permute-start.2 = (f32[32,2,32,128]{3,2,1,0:T(8,128)S(1)}, f32[32,2,32,128]{3,2,1,0:T(8,128)S(1)}, u32[]{:S(2)}, u32[]{:S(2)}) collective-permute-start(f32[32,2,32,128]{3,2,1,0:T(8,128)S(1)} %get-tuple-element.14), channel_id=1, source_target_pairs={{0,1},{1,0},{2,3},{3,2},{4,5},{5,4},{6,7},{7,6},{8,9},{9,8},{10,11... | collective-permute-start | bytes 3145736 | tf_op jit(solution)/shard_map/ppermute | solution.py:332
  92.8 4.8 %collective-permute-start.1 = (f32[32,2,32,128]{3,2,1,0:T(8,128)S(1)}, f32[32,2,32,128]{3,2,1,0:T(8,128)S(1)}, u32[]{:S(2)}, u32[]{:S(2)}) collective-permute-start(f32[32,2,32,128]{3,2,1,0:T(8,128)S(1)} %get-tuple-element.15), channel_id=1, source_target_pairs={{0,1},{1,0},{2,3},{3,2},{4,5},{5,4},{6,7},{7,6},{8,9},{9,8},{10,11... | collective-permute-start | bytes 3145736 | tf_op jit(solution)/shard_map/ppermute | solution.py:332
  97.6 17.2 %copy-start = (f32[256,4,128]{2,1,0:T(4,128)S(1)}, f32[256,4,128]{2,1,0:T(4,128)}, u32[]{:S(2)}) copy-start(f32[256,4,128]{2,1,0:T(4,128)} %param.11) | copy-start | bytes 1572868
  97.7 17.2 %copy-start.5 = (s32[4,128]{1,0:T(4,128)S(1)}, s32[4,128]{1,0:T(4,128)}, u32[]{:S(2)}) copy-start(s32[4,128]{1,0:T(4,128)} %mute_ref.3) | copy-start | bytes 6148

commit v6 on v5

--- a/solution.py
+++ b/solution.py
@@ -79,22 +79,16 @@
 AHEAD = 6
 
 
-def forward_kernel(pos_ref, f_hbm, r_hbm, own, oth, rh_ref, rl_ref, f_ref, r_ref, fsem, zsem, sem):
+def forward_kernel(pos_ref, f_hbm, r_hbm, own, oth, rh_ref, rl_ref, f_ref, r_ref, fsem, sem):
     def fetch_f(g):
         cut = pl.ds(g * 4, 4)
         return pltpu.make_async_copy(f_hbm.at[cut], f_ref.at[cut], fsem.at[g])
 
-    def fetch_first(z):
-        cut = (pl.ds(0, 4), slice(None), pl.ds(z * 256, 256))
-        return pltpu.make_async_copy(r_hbm.at[cut], r_ref.at[cut], zsem.at[z])
-
     def fetch(k):
-        return pltpu.make_async_copy(r_hbm.at[k], r_ref.at[k], sem.at[k - 4])
+        return pltpu.make_async_copy(r_hbm.at[k], r_ref.at[k], sem.at[k])
 
     fetch_f(0).start()
-    for z in range(4):
-        fetch_first(z).start()
-    for k in range(4, AHEAD):
+    for k in range(AHEAD):
         fetch(k).start()
     for g in range(1, 4):
         fetch_f(g).start()
@@ -138,17 +132,11 @@
                 for y in range(4):
                     out[place(z, xh_, part % 2, y), (part // 2) % 2, g8, :] = trade(v, pair, y)
 
-    fetch_f(0).wait()
-    lhs0 = operands(0)
-    for z in range(4):
-        fetch_first(z).wait()
-        fetch(AHEAD + z).start()
-        block(0, slice(0, 8), z, lhs0)
-
-    @pl.loop(1, 4)
+    @pl.loop(0, 4)
     def _(g):
         fetch_f(g).wait()
         lhs = operands(g)
+        g8 = pl.ds(pl.multiple_of(g * 8, 8), 8)
         for q in range(4):
             k = g * 4 + q
             fetch(k).wait()
@@ -158,7 +146,7 @@
                 fetch(k + AHEAD).start()
 
         for z in range(4):
-            block(g, pl.ds(pl.multiple_of(g * 8, 8), 8), z, lhs)
+            block(g, g8, z, lhs)
 
 
 def forward_panel(pos, focusing, reflection):
@@ -173,8 +161,7 @@
             pltpu.VMEM((KK, 2, 32, 128), F32),
             pltpu.VMEM((KK, 2, 1024, 128), F32),
             pltpu.SemaphoreType.DMA((4,)),
-            pltpu.SemaphoreType.DMA((4,)),
-            pltpu.SemaphoreType.DMA((12,)),
+            pltpu.SemaphoreType.DMA((16,)),
         ],
         compiler_params=params(24),
         cost_estimate=pl.CostEstimate(flops=3 * 2**30, bytes_accessed=21 * 2**20, transcendentals=0),
@@ -228,9 +215,8 @@
     pair = lax.broadcasted_iota(jnp.int32, (8, 128), 0) // 2
     even = (lax.broadcasted_iota(jnp.int32, (64, 128), 0) % 2) == 0
 
-    @pl.loop(0, 4)
-    def _(g):
-        g8 = pl.ds(pl.multiple_of(g * 8, 8), 8)
+    for g in range(4):
+        g8 = slice(g * 8, g * 8 + 8)
         acc = [None] * 4
         for zz in range(2):
             z = second * 2 + zz
@@ -278,30 +264,38 @@
     )(own, oth, rh, rl, *before)
 
 
-def receiver_kernel(pos_ref, th_ref, tl_ref, mute_ref, direct_ref, x_ref, out_ref):
-    even = pos_ref[0] == 0
-    turn = pos_ref[1]
-    t = lax.broadcasted_iota(jnp.int32, (NT, 128), 0)
-    for c in range(2):
-        cols = []
-        for j in range(2):
+def receiver_kernel(pos_ref, th_ref, tl_ref, mute_ref, direct_ref, x_ref, out_ref, high, low):
+    step = pl.program_id(0)
+    t = lax.broadcasted_iota(jnp.int32, (NT // 2, 128), 0) + step * (NT // 2)
+
+    @pl.when(step == 0)
+    def _():
+        even = pos_ref[0] == 0
+        turn = pos_ref[1]
+        for p in range(4):
+            c, j = p // 2, p % 2
             a = jnp.where(even, x_ref[:, j * 2 + c], x_ref[:, j * 2 + 1 - c])
-            cols.append(unturn(a.reshape(32, 8, 128), turn, -1).reshape(256, 128))
-        adj = mm3((th_ref[...], tl_ref[...]), split(jnp.concatenate(cols, axis=1)))
-        for j in range(2):
-            p = c * 2 + j
-            mute = jnp.broadcast_to(mute_ref[p : p + 1, :], (NT, 128))
-            val = jnp.where((t < mute) | (t > NT - mute), adj[:, j * 128 : (j + 1) * 128], 0.0)
-            rows = pl.ds(p, NT, stride=4)
-            out_ref[rows, :] = direct_ref[rows, :] - val
+            a = unturn(a.reshape(32, 8, 128), turn, -1).reshape(256, 128)
+            high[:, p * 128 : p * 128 + 128], low[:, p * 128 : p * 128 + 128] = split(a)
+
+    adj = mm3((th_ref[...], tl_ref[...]), (high[...], low[...]))
+    for p in range(4):
+        mute = jnp.broadcast_to(mute_ref[p : p + 1, :], (NT // 2, 128))
+        val = jnp.where((t < mute) | (t > NT - mute), adj[:, p * 128 : (p + 1) * 128], 0.0)
+        rows = pl.ds(p, NT // 2, stride=4)
+        out_ref[rows, :] = direct_ref[rows, :] - val
 
 
 def receiver_traces(pos, tables, mute, direct, x):
+    half = pl.BlockSpec((NT // 2, NT), lambda i: (i, 0))
+    rows = pl.BlockSpec((NT * 2, 128), lambda i: (i, 0))
     return pl.pallas_call(
         receiver_kernel,
-        in_specs=[SMEM] + [VMEM] * 5,
-        out_specs=VMEM,
+        grid=(2,),
+        in_specs=[SMEM, half, half, VMEM, rows, VMEM],
+        out_specs=rows,
         out_shape=jax.ShapeDtypeStruct((NT * 4, 128), F32),
+        scratch_shapes=[pltpu.VMEM((NT, 512), BF16)] * 2,
         compiler_params=params(8),
         name="receiver_traces",
     )(pos, *tables, mute, direct, x)

time: 117 us -> 116 us (level)
  transfers between devices with their start and end apart: 3 -> 3, of which waited for: 2 -> 2; matrix products, arithmetic and copies ran while one was open for 0% -> 0% of each run, Pallas kernels for 2% -> 1%
where the time goes in v6:
time: 116 us
  blocking collectives  90.4 us (78%)
  Pallas kernels  16.9 us (15%)
  waiting for transfers between devices  6.3 us (5%)
    all_to_all x2, blocking collectives, exchange(): lax.all_to_all(x, EVERY, split_axis=0, concat_axis=0, tiled=True, axis_in...  75.5 us
    all_to_all x1, blocking collectives, body(): lax.all_to_all(adjoint, ('z', 'xh'), split_axis=0, concat_axis=0, tiled=T...  15 us
    pallas_call x1, Pallas kernels, forward_panel(): pl.pallas_call(forward_kernel, in_specs=[SMEM, HBM, HBM], out_specs=[VMEM...  9.79 us
    ppermute x1, waiting for transfers between devices, body(): parts = exchange(own + lax.ppermute(oth, 'c', SWAP))  4.15 us
    pallas_call x2, Pallas kernels, adjoint_panel(): pl.pallas_call(functools.partial(adjoint_kernel, second), in_specs=[VMEM]...  3.25 us
  transfers between devices with their start and end apart: 3, of which 2 were waited for; matrix products, arithmetic and copies ran while one was open for 0% of the time, Pallas kernels for 1%

profile of v6, /device:TPU:0, one launch (start us, length us, event | category | flops | bytes accessed | tf_op | source)
XLA Modules:
  0.0 115.8 jit_solution(11546935751730147622)
XLA Ops:
  0.6 0.1 pad_add_fusion.pos_ref
  0.7 9.8 %forward_panel.1 = (f32[64,2,32,128]{3,2,1,0:T(8,128)S(1)}, f32[64,2,32,128]{3,2,1,0:T(8,128)S(1)}, bf16[16,1024,256]{2,1,0:T(8,128)(2,1)S(1)}, bf16[16,1024,256]{2,1,0:T(8,128)(2,1)S(1)}) custom-call(s32[3]{0:T(128)S(1)} %pad_add_fusion.pos_ref, f32[16,2,32,128]{3,2,1,0:T(8,128)} %f_hbm.1, f32[16,2,1024,128]{3,2,1,0:T(8,128)} %r_hbm.1), custom_call_target="tpu_custom_call" | custom-call | flops 3221225472 | bytes 22020096 | tf_op jit(solution)/shard_map/forward_panel/pallas_call | solution.py:155
  10.5 0.1 collective-permute-start
  10.6 4.1 %collective-permute-done = f32[64,2,32,128]{3,2,1,0:T(8,128)S(1)} collective-permute-done((f32[64,2,32,128]{3,2,1,0:T(8,128)S(1)}, f32[64,2,32,128]{3,2,1,0:T(8,128)S(1)}, u32[]{:S(2)}, u32[]{:S(2)}) %collective-permute-start) | collective-permute-done | bytes 2097184 | tf_op jit(solution)/shard_map/ppermute | solution.py:323
  14.8 0.5 add.7
  15.2 0.0 copy-start.1
  15.2 0.0 copy-start.2
  15.3 0.0 copy-start.3
  15.3 0.0 copy-start.4
  15.3 0.0 copy-start.6
  15.3 41.1 %all_to_all.15.x_ref = f32[64,2,32,128]{3,2,1,0:T(8,128)S(1)} all-to-all(f32[64,2,32,128]{3,2,1,0:T(8,128)S(1)} %add.7), channel_id=1, replica_groups={{0,10,20,30,8,18,28,6,16,26,4,14,24,2,12,22,32,42,52,62,40,50,60,38,48,..., dimensions={0} | all-to-all | bytes 4194304 | tf_op jit(solution)/shard_map/all_to_all | solution.py:309
  56.4 0.0 copy-done.1
  56.4 0.0 copy-done.2
  56.4 0.0 copy-done.3
  56.4 0.0 copy-done.4
  56.5 0.0 copy-done.6
  56.5 1.8 %source_traces.1 = (f32[512,128]{1,0:T(8,128)}, f32[64,2,32,128]{3,2,1,0:T(8,128)S(1)}) custom-call(s32[3]{0:T(128)S(1)} %pad_add_fusion.pos_ref, bf16[256,256]{1,0:T(8,128)(2,1)S(1)} %copy-done.2, bf16[256,256]{1,0:T(8,128)(2,1)S(1)} %copy-done.1, bf16[256,256]{1,0:T(8,128)(2,1)S(1)} %copy-done.4, bf16[256,256]{1,0:T(8,128)(2,1)S(1)} %copy-done.3, ...), custom_call_target="tpu_custom_call" | custom-call | tf_op jit(solution)/shard_map/source_traces/pallas_call | solution.py:200
  58.3 34.3 %all_to_all.16.own = f32[64,2,32,128]{3,2,1,0:T(8,128)S(1)} all-to-all(f32[64,2,32,128]{3,2,1,0:T(8,128)S(1)} %get-tuple-element.11), channel_id=1, replica_groups={{0,10,20,30,8,18,28,6,16,26,4,14,24,2,12,22,32,42,52,62,40,50,60,38,48,..., dimensions={0} | all-to-all | bytes 4194304 | tf_op jit(solution)/shard_map/all_to_all | solution.py:309
  92.6 0.2 fusion
  92.8 0.1 collective-permute-start.2
  92.9 0.5 collective-permute-start.1
  93.4 2.1 %collective-permute-done.2.oth = f32[32,2,32,128]{3,2,1,0:T(8,128)S(1)} collective-permute-done((f32[32,2,32,128]{3,2,1,0:T(8,128)S(1)}, f32[32,2,32,128]{3,2,1,0:T(8,128)S(1)}, u32[]{:S(2)}, u32[]{:S(2)}) %collective-permute-start.2) | collective-permute-done | bytes 1048608 | tf_op jit(solution)/shard_map/ppermute | solution.py:326
  95.5 1.6 %adjoint_panel0.1.rest_0_ = f32[8,4,32,128]{3,2,1,0:T(8,128)S(1)} custom-call(f32[64,2,32,128]{3,2,1,0:T(8,128)S(1)} %all_to_all.16.own, f32[32,2,32,128]{3,2,1,0:T(8,128)S(1)} %collective-permute-done.2.oth, bf16[16,1024,256]{2,1,0:T(8,128)(2,1)S(1)} %get-tuple-element.12.rh_ref, bf16[16,1024,256]{2,1,0:T(8,128)(2,1)S(1)} %get-tuple-element.13.rl_ref), custom_call_target="tpu_custom_call" | custom-call | flops 1610612736 | bytes 1048576 | tf_op jit(solution)/shard_map/adjoint_panel0/pallas_call | solution.py:256
  97.1 0.0 copy-start
  97.2 0.0 copy-start.5
  97.2 0.0 collective-permute-done.1.oth
  97.2 1.6 %adjoint_panel1.1 = f32[8,4,32,128]{3,2,1,0:T(8,128)S(1)} custom-call(f32[64,2,32,128]{3,2,1,0:T(8,128)S(1)} %all_to_all.16.own, f32[32,2,32,128]{3,2,1,0:T(8,128)S(1)} %collective-permute-done.1.oth, bf16[16,1024,256]{2,1,0:T(8,128)(2,1)S(1)} %get-tuple-element.12.rh_ref, bf16[16,1024,256]{2,1,0:T(8,128)(2,1)S(1)} %get-tuple-element.13.rl_ref, ...), custom_call_target="tpu_custom_call" | custom-call | flops 1610612736 | bytes 1048576 | tf_op jit(solution)/shard_map/adjoint_panel1/pallas_call | solution.py:256
  98.8 15.0 %all_to_all.17.x_ref = f32[8,4,32,128]{3,2,1,0:T(8,128)S(1)} all-to-all(f32[8,4,32,128]{3,2,1,0:T(8,128)S(1)} %adjoint_panel1.1), channel_id=1, replica_groups=mesh['z'=4,'xh'=2,'xl'=2,'y'=4,'c'=2] {'z','xh'}, dimensions={0} | all-to-all | bytes 1048576 | tf_op jit(solution)/shard_map/all_to_all | solution.py:329
  113.8 0.0 copy-done
  113.8 0.0 copy-done.5
  113.8 2.0 %receiver_traces.1 = f32[1024,128]{1,0:T(8,128)} custom-call(s32[3]{0:T(128)S(1)} %pad_add_fusion.pos_ref, bf16[256,256]{1,0:T(8,128)(2,1)S(1)} %copy-done.2, bf16[256,256]{1,0:T(8,128)(2,1)S(1)} %copy-done.1, s32[4,128]{1,0:T(4,128)S(1)} %copy-done.5, f32[1024,128]{1,0:T(8,128)S(1)} %bitcast.6, f32[8,4,32,128]{3,2,1,0:T(8,128)S(1)} %all_to_all.17.x_ref), custom_call_target="tpu_custom_call" | custom-call | tf_op jit(solution)/shard_map/receiver_traces/pallas_call | solution.py:292
Async XLA Ops:
  10.5 4.2 %collective-permute-start = (f32[64,2,32,128]{3,2,1,0:T(8,128)S(1)}, f32[64,2,32,128]{3,2,1,0:T(8,128)S(1)}, u32[]{:S(2)}, u32[]{:S(2)}) collective-permute-start(f32[64,2,32,128]{3,2,1,0:T(8,128)S(1)} %get-tuple-element.9), channel_id=1, source_target_pairs={{0,1},{1,0},{2,3},{3,2},{4,5},{5,4},{6,7},{7,6},{8,9},{9,8},{10,11... | collective-permute-start | bytes 6291464 | tf_op jit(solution)/shard_map/ppermute | solution.py:323
  15.2 41.2 %copy-start.1 = (bf16[256,256]{1,0:T(8,128)(2,1)S(1)}, bf16[256,256]{1,0:T(8,128)(2,1)}, u32[]{:S(2)}) copy-start(bf16[256,256]{1,0:T(8,128)(2,1)} %constant.29.clone.tl_ref) | copy-start | bytes 393220
  15.2 41.2 %copy-start.2 = (bf16[256,256]{1,0:T(8,128)(2,1)S(1)}, bf16[256,256]{1,0:T(8,128)(2,1)}, u32[]{:S(2)}) copy-start(bf16[256,256]{1,0:T(8,128)(2,1)} %constant.28.clone.th_ref) | copy-start | bytes 393220
  15.3 41.2 %copy-start.3 = (bf16[256,256]{1,0:T(8,128)(2,1)S(1)}, bf16[256,256]{1,0:T(8,128)(2,1)}, u32[]{:S(2)}) copy-start(bf16[256,256]{1,0:T(8,128)(2,1)} %constant.31.clone.ttl_ref) | copy-start | bytes 393220
  15.3 41.2 %copy-start.4 = (bf16[256,256]{1,0:T(8,128)(2,1)S(1)}, bf16[256,256]{1,0:T(8,128)(2,1)}, u32[]{:S(2)}) copy-start(bf16[256,256]{1,0:T(8,128)(2,1)} %constant.30.clone.tth_ref) | copy-start | bytes 393220
  15.3 41.2 %copy-start.6 = (s32[2,128]{1,0:T(2,128)S(1)}, s32[2,128]{1,0:T(2,128)}, u32[]{:S(2)}) copy-start(s32[2,128]{1,0:T(2,128)} %mute_ref.2) | copy-start | bytes 3076
  92.8 2.7 %collective-permute-start.2 = (f32[32,2,32,128]{3,2,1,0:T(8,128)S(1)}, f32[32,2,32,128]{3,2,1,0:T(8,128)S(1)}, u32[]{:S(2)}, u32[]{:S(2)}) collective-permute-start(f32[32,2,32,128]{3,2,1,0:T(8,128)S(1)} %get-tuple-element.14), channel_id=1, source_target_pairs={{0,1},{1,0},{2,3},{3,2},{4,5},{5,4},{6,7},{7,6},{8,9},{9,8},{10,11... | collective-permute-start | bytes 3145736 | tf_op jit(solution)/shard_map/ppermute | solution.py:326
  92.9 4.3 %collective-permute-start.1 = (f32[32,2,32,128]{3,2,1,0:T(8,128)S(1)}, f32[32,2,32,128]{3,2,1,0:T(8,128)S(1)}, u32[]{:S(2)}, u32[]{:S(2)}) collective-permute-start(f32[32,2,32,128]{3,2,1,0:T(8,128)S(1)} %get-tuple-element.15), channel_id=1, source_target_pairs={{0,1},{1,0},{2,3},{3,2},{4,5},{5,4},{6,7},{7,6},{8,9},{9,8},{10,11... | collective-permute-start | bytes 3145736 | tf_op jit(solution)/shard_map/ppermute | solution.py:326
  97.1 16.6 %copy-start = (f32[256,4,128]{2,1,0:T(4,128)S(1)}, f32[256,4,128]{2,1,0:T(4,128)}, u32[]{:S(2)}) copy-start(f32[256,4,128]{2,1,0:T(4,128)} %param.11) | copy-start | bytes 1572868
  97.2 16.6 %copy-start.5 = (s32[4,128]{1,0:T(4,128)S(1)}, s32[4,128]{1,0:T(4,128)}, u32[]{:S(2)}) copy-start(s32[4,128]{1,0:T(4,128)} %mute_ref.3) | copy-start | bytes 6148

commit v7 on v5

--- a/solution.py
+++ b/solution.py
@@ -76,25 +76,19 @@
     return [[chip * 2 + core for chip in order] for core in range(2)]
 
 
-AHEAD = 6
-
-
-def forward_kernel(pos_ref, f_hbm, r_hbm, own, oth, rh_ref, rl_ref, f_ref, r_ref, fsem, zsem, sem):
+AHEAD = 7
+
+
+def forward_kernel(pos_ref, f_hbm, r_hbm, own, oth, rh_ref, rl_ref, f_ref, r_ref, fsem, sem):
     def fetch_f(g):
         cut = pl.ds(g * 4, 4)
         return pltpu.make_async_copy(f_hbm.at[cut], f_ref.at[cut], fsem.at[g])
 
-    def fetch_first(z):
-        cut = (pl.ds(0, 4), slice(None), pl.ds(z * 256, 256))
-        return pltpu.make_async_copy(r_hbm.at[cut], r_ref.at[cut], zsem.at[z])
-
     def fetch(k):
-        return pltpu.make_async_copy(r_hbm.at[k], r_ref.at[k], sem.at[k - 4])
+        return pltpu.make_async_copy(r_hbm.at[k], r_ref.at[k], sem.at[k])
 
     fetch_f(0).start()
-    for z in range(4):
-        fetch_first(z).start()
-    for k in range(4, AHEAD):
+    for k in range(AHEAD):
         fetch(k).start()
     for g in range(1, 4):
         fetch_f(g).start()
@@ -129,8 +123,13 @@
             wh, wl = split(jnp.concatenate([r_ref[k, 0, rows, :], r_ref[k, 1, rows, :]], axis=1))
             rh_ref[k, rows, :] = wh
             rl_ref[k, rows, :] = wl
-            acc = mm(lhs[q][1], wh, (1, 1))
-            res.append(acc[:64] + (acc[64:] + mm(lhs[q][0], wl, (1, 1))))
+            if q % 2:
+                low = jnp.concatenate([lhs[q][0], jnp.zeros_like(lhs[q][0])], axis=0)
+                acc = (mm(wh, lhs[q][1], (1, 1)) + mm(wl, low, (1, 1))).T
+                res.append(acc[:64] + acc[64:])
+            else:
+                acc = mm(lhs[q][1], wh, (1, 1))
+                res.append(acc[:64] + (acc[64:] + mm(lhs[q][0], wl, (1, 1))))
         for xh_ in range(2):
             for part in range(8):
                 v = [r[part * 8 : part * 8 + 8, xh_ * 128 : xh_ * 128 + 128] for r in res]
@@ -138,17 +137,11 @@
                 for y in range(4):
                     out[place(z, xh_, part % 2, y), (part // 2) % 2, g8, :] = trade(v, pair, y)
 
-    fetch_f(0).wait()
-    lhs0 = operands(0)
-    for z in range(4):
-        fetch_first(z).wait()
-        fetch(AHEAD + z).start()
-        block(0, slice(0, 8), z, lhs0)
-
-    @pl.loop(1, 4)
+    @pl.loop(0, 4)
     def _(g):
         fetch_f(g).wait()
         lhs = operands(g)
+        g8 = pl.ds(pl.multiple_of(g * 8, 8), 8)
         for q in range(4):
             k = g * 4 + q
             fetch(k).wait()
@@ -158,7 +151,7 @@
                 fetch(k + AHEAD).start()
 
         for z in range(4):
-            block(g, pl.ds(pl.multiple_of(g * 8, 8), 8), z, lhs)
+            block(g, g8, z, lhs)
 
 
 def forward_panel(pos, focusing, reflection):
@@ -173,8 +166,7 @@
             pltpu.VMEM((KK, 2, 32, 128), F32),
             pltpu.VMEM((KK, 2, 1024, 128), F32),
             pltpu.SemaphoreType.DMA((4,)),
-            pltpu.SemaphoreType.DMA((4,)),
-            pltpu.SemaphoreType.DMA((12,)),
+            pltpu.SemaphoreType.DMA((16,)),
         ],
         compiler_params=params(24),
         cost_estimate=pl.CostEstimate(flops=3 * 2**30, bytes_accessed=21 * 2**20, transcendentals=0),
@@ -182,7 +174,7 @@
     )(pos, focusing, reflection)
 
 
-def source_kernel(pos_ref, th_ref, tl_ref, tth_ref, ttl_ref, mute_ref, x_ref, time_ref, out_ref):
+def source_kernel(pos_ref, th_ref, tl_ref, tth_ref, ttl_ref, mute_ref, x_ref, time_hbm, out_ref, time_ref, sem):
     turn = pos_ref[2]
     cols = []
     for j in range(2):
@@ -200,6 +192,8 @@
         val = jnp.where((t < mute) | (t > NT - mute), up[:, j * 128 : (j + 1) * 128], 0.0)
         time_ref[pl.ds(j, NT, stride=2), :] = val
         kept.append(val)
+    copy = pltpu.make_async_copy(time_ref, time_hbm, sem)
+    copy.start()
     back = mm3((tth_ref[...], ttl_ref[...]), split(jnp.concatenate(kept, axis=1)))
     for j in range(2):
         b = unturn(back[:, j * 128 : (j + 1) * 128].reshape(32, 8, 128), turn, 1)
@@ -207,17 +201,19 @@
         for f in range(KB):
             for i in range(8):
                 out_ref[place(f // 2, f % 2, i // 4, i % 4), j] = b[f]
+    copy.wait()
 
 
 def source_traces(pos, tables, mute, parts):
     return pl.pallas_call(
         source_kernel,
         in_specs=[SMEM] + [VMEM] * 6,
-        out_specs=[VMEM] * 2,
+        out_specs=[HBM, VMEM],
         out_shape=[
             jax.ShapeDtypeStruct((NT * 2, 128), F32),
             jax.ShapeDtypeStruct((64, 2, 32, 128), F32),
         ],
+        scratch_shapes=[pltpu.VMEM((NT * 2, 128), F32), pltpu.SemaphoreType.DMA],
         compiler_params=params(8),
         name="source_traces",
     )(pos, *tables, mute, parts)
@@ -228,9 +224,8 @@
     pair = lax.broadcasted_iota(jnp.int32, (8, 128), 0) // 2
     even = (lax.broadcasted_iota(jnp.int32, (64, 128), 0) % 2) == 0
 
-    @pl.loop(0, 4)
-    def _(g):
-        g8 = pl.ds(pl.multiple_of(g * 8, 8), 8)
+    for g in range(4):
+        g8 = slice(g * 8, g * 8 + 8)
         acc = [None] * 4
         for zz in range(2):
             z = second * 2 + zz

time: 117 us -> 115 us (0.983)
  Pallas kernels: 17.8 us -> 15.6 us
  transfers between devices with their start and end apart: 3 -> 3, of which waited for: 2 -> 2; matrix products, arithmetic and copies ran while one was open for 0% -> 0% of each run, Pallas kernels for 2% -> 1%
where the time goes in v7:
time: 115 us
  blocking collectives  90.4 us (79%)
  Pallas kernels  15.6 us (14%)
  waiting for transfers between devices  6.3 us (5%)
    all_to_all x2, blocking collectives, exchange(): lax.all_to_all(x, EVERY, split_axis=0, concat_axis=0, tiled=True, axis_in...  75.5 us
    all_to_all x1, blocking collectives, body(): lax.all_to_all(adjoint, ('z', 'xh'), split_axis=0, concat_axis=0, tiled=T...  15 us
    pallas_call x1, Pallas kernels, forward_panel(): pl.pallas_call(forward_kernel, in_specs=[SMEM, HBM, HBM], out_specs=[VMEM...  8.65 us
    ppermute x1, waiting for transfers between devices, body(): parts = exchange(own + lax.ppermute(oth, 'c', SWAP))  4.15 us
    pallas_call x2, Pallas kernels, adjoint_panel(): pl.pallas_call(functools.partial(adjoint_kernel, second), in_specs=[VMEM]...  3.26 us
  transfers between devices with their start and end apart: 3, of which 2 were waited for; matrix products, arithmetic and copies ran while one was open for 0% of the time, Pallas kernels for 1%

profile of v7, /device:TPU:0, one launch (start us, length us, event | category | flops | bytes accessed | tf_op | source)
XLA Modules:
  0.0 114.6 jit_solution(6591681945535287361)
XLA Ops:
  0.6 0.1 pad_add_fusion.pos_ref
  0.7 8.6 %forward_panel.1 = (f32[64,2,32,128]{3,2,1,0:T(8,128)S(1)}, f32[64,2,32,128]{3,2,1,0:T(8,128)S(1)}, bf16[16,1024,256]{2,1,0:T(8,128)(2,1)S(1)}, bf16[16,1024,256]{2,1,0:T(8,128)(2,1)S(1)}) custom-call(s32[3]{0:T(128)S(1)} %pad_add_fusion.pos_ref, f32[16,2,32,128]{3,2,1,0:T(8,128)} %f_hbm.1, f32[16,2,1024,128]{3,2,1,0:T(8,128)} %r_hbm.1), custom_call_target="tpu_custom_call" | custom-call | flops 3221225472 | bytes 22020096 | tf_op jit(solution)/shard_map/forward_panel/pallas_call | solution.py:160
  9.4 0.1 collective-permute-start
  9.5 4.1 %collective-permute-done = f32[64,2,32,128]{3,2,1,0:T(8,128)S(1)} collective-permute-done((f32[64,2,32,128]{3,2,1,0:T(8,128)S(1)}, f32[64,2,32,128]{3,2,1,0:T(8,128)S(1)}, u32[]{:S(2)}, u32[]{:S(2)}) %collective-permute-start) | collective-permute-done | bytes 2097184 | tf_op jit(solution)/shard_map/ppermute | solution.py:324
  13.6 0.5 add.7
  14.1 0.0 copy-start.1
  14.1 0.0 copy-start.2
  14.1 0.0 copy-start.3
  14.1 0.0 copy-start.4
  14.1 0.0 copy-start.6
  14.2 41.1 %all_to_all.15.x_ref = f32[64,2,32,128]{3,2,1,0:T(8,128)S(1)} all-to-all(f32[64,2,32,128]{3,2,1,0:T(8,128)S(1)} %add.7), channel_id=1, replica_groups={{0,10,20,30,8,18,28,6,16,26,4,14,24,2,12,22,32,42,52,62,40,50,60,38,48,..., dimensions={0} | all-to-all | bytes 4194304 | tf_op jit(solution)/shard_map/all_to_all | solution.py:310
  55.3 0.0 copy-done.1
  55.3 0.0 copy-done.2
  55.3 0.0 copy-done.3
  55.3 0.0 copy-done.4
  55.3 0.0 copy-done.6
  55.3 1.8 %source_traces.1 = (f32[512,128]{1,0:T(8,128)}, f32[64,2,32,128]{3,2,1,0:T(8,128)S(1)}) custom-call(s32[3]{0:T(128)S(1)} %pad_add_fusion.pos_ref, bf16[256,256]{1,0:T(8,128)(2,1)S(1)} %copy-done.2, bf16[256,256]{1,0:T(8,128)(2,1)S(1)} %copy-done.1, bf16[256,256]{1,0:T(8,128)(2,1)S(1)} %copy-done.4, bf16[256,256]{1,0:T(8,128)(2,1)S(1)} %copy-done.3, ...), custom_call_target="tpu_custom_call" | custom-call | tf_op jit(solution)/shard_map/source_traces/pallas_call | solution.py:208
  57.2 34.3 %all_to_all.16.own = f32[64,2,32,128]{3,2,1,0:T(8,128)S(1)} all-to-all(f32[64,2,32,128]{3,2,1,0:T(8,128)S(1)} %get-tuple-element.11), channel_id=1, replica_groups={{0,10,20,30,8,18,28,6,16,26,4,14,24,2,12,22,32,42,52,62,40,50,60,38,48,..., dimensions={0} | all-to-all | bytes 4194304 | tf_op jit(solution)/shard_map/all_to_all | solution.py:310
  91.5 0.2 fusion
  91.7 0.1 collective-permute-start.2
  91.8 0.5 collective-permute-start.1
  92.3 2.1 %collective-permute-done.2.oth = f32[32,2,32,128]{3,2,1,0:T(8,128)S(1)} collective-permute-done((f32[32,2,32,128]{3,2,1,0:T(8,128)S(1)}, f32[32,2,32,128]{3,2,1,0:T(8,128)S(1)}, u32[]{:S(2)}, u32[]{:S(2)}) %collective-permute-start.2) | collective-permute-done | bytes 1048608 | tf_op jit(solution)/shard_map/ppermute | solution.py:327
  94.4 1.6 %adjoint_panel0.1.rest_0_ = f32[8,4,32,128]{3,2,1,0:T(8,128)S(1)} custom-call(f32[64,2,32,128]{3,2,1,0:T(8,128)S(1)} %all_to_all.16.own, f32[32,2,32,128]{3,2,1,0:T(8,128)S(1)} %collective-permute-done.2.oth, bf16[16,1024,256]{2,1,0:T(8,128)(2,1)S(1)} %get-tuple-element.12.rh_ref, bf16[16,1024,256]{2,1,0:T(8,128)(2,1)S(1)} %get-tuple-element.13.rl_ref), custom_call_target="tpu_custom_call" | custom-call | flops 1610612736 | bytes 1048576 | tf_op jit(solution)/shard_map/adjoint_panel0/pallas_call | solution.py:265
  96.1 0.0 copy-start
  96.1 0.0 copy-start.5
  96.1 0.0 collective-permute-done.1.oth
  96.1 1.6 %adjoint_panel1.1 = f32[8,4,32,128]{3,2,1,0:T(8,128)S(1)} custom-call(f32[64,2,32,128]{3,2,1,0:T(8,128)S(1)} %all_to_all.16.own, f32[32,2,32,128]{3,2,1,0:T(8,128)S(1)} %collective-permute-done.1.oth, bf16[16,1024,256]{2,1,0:T(8,128)(2,1)S(1)} %get-tuple-element.12.rh_ref, bf16[16,1024,256]{2,1,0:T(8,128)(2,1)S(1)} %get-tuple-element.13.rl_ref, ...), custom_call_target="tpu_custom_call" | custom-call | flops 1610612736 | bytes 1048576 | tf_op jit(solution)/shard_map/adjoint_panel1/pallas_call | solution.py:265
  97.7 15.0 %all_to_all.17.x_ref = f32[8,4,32,128]{3,2,1,0:T(8,128)S(1)} all-to-all(f32[8,4,32,128]{3,2,1,0:T(8,128)S(1)} %adjoint_panel1.1), channel_id=1, replica_groups=mesh['z'=4,'xh'=2,'xl'=2,'y'=4,'c'=2] {'z','xh'}, dimensions={0} | all-to-all | bytes 1048576 | tf_op jit(solution)/shard_map/all_to_all | solution.py:330
  112.7 0.0 copy-done
  112.7 0.0 copy-done.5
  112.7 1.9 %receiver_traces.1 = f32[1024,128]{1,0:T(8,128)} custom-call(s32[3]{0:T(128)S(1)} %pad_add_fusion.pos_ref, bf16[256,256]{1,0:T(8,128)(2,1)S(1)} %copy-done.2, bf16[256,256]{1,0:T(8,128)(2,1)S(1)} %copy-done.1, s32[4,128]{1,0:T(4,128)S(1)} %copy-done.5, f32[1024,128]{1,0:T(8,128)S(1)} %bitcast.6, f32[8,4,32,128]{3,2,1,0:T(8,128)S(1)} %all_to_all.17.x_ref), custom_call_target="tpu_custom_call" | custom-call | tf_op jit(solution)/shard_map/receiver_traces/pallas_call | solution.py:295
Async XLA Ops:
  9.4 4.2 %collective-permute-start = (f32[64,2,32,128]{3,2,1,0:T(8,128)S(1)}, f32[64,2,32,128]{3,2,1,0:T(8,128)S(1)}, u32[]{:S(2)}, u32[]{:S(2)}) collective-permute-start(f32[64,2,32,128]{3,2,1,0:T(8,128)S(1)} %get-tuple-element.9), channel_id=1, source_target_pairs={{0,1},{1,0},{2,3},{3,2},{4,5},{5,4},{6,7},{7,6},{8,9},{9,8},{10,11... | collective-permute-start | bytes 6291464 | tf_op jit(solution)/shard_map/ppermute | solution.py:324
  14.1 41.2 %copy-start.1 = (bf16[256,256]{1,0:T(8,128)(2,1)S(1)}, bf16[256,256]{1,0:T(8,128)(2,1)}, u32[]{:S(2)}) copy-start(bf16[256,256]{1,0:T(8,128)(2,1)} %constant.29.clone.tl_ref) | copy-start | bytes 393220
  14.1 41.2 %copy-start.2 = (bf16[256,256]{1,0:T(8,128)(2,1)S(1)}, bf16[256,256]{1,0:T(8,128)(2,1)}, u32[]{:S(2)}) copy-start(bf16[256,256]{1,0:T(8,128)(2,1)} %constant.28.clone.th_ref) | copy-start | bytes 393220
  14.1 41.2 %copy-start.3 = (bf16[256,256]{1,0:T(8,128)(2,1)S(1)}, bf16[256,256]{1,0:T(8,128)(2,1)}, u32[]{:S(2)}) copy-start(bf16[256,256]{1,0:T(8,128)(2,1)} %constant.31.clone.ttl_ref) | copy-start | bytes 393220
  14.1 41.2 %copy-start.4 = (bf16[256,256]{1,0:T(8,128)(2,1)S(1)}, bf16[256,256]{1,0:T(8,128)(2,1)}, u32[]{:S(2)}) copy-start(bf16[256,256]{1,0:T(8,128)(2,1)} %constant.30.clone.tth_ref) | copy-start | bytes 393220
  14.1 41.2 %copy-start.6 = (s32[2,128]{1,0:T(2,128)S(1)}, s32[2,128]{1,0:T(2,128)}, u32[]{:S(2)}) copy-start(s32[2,128]{1,0:T(2,128)} %mute_ref.2) | copy-start | bytes 3076
  91.7 2.7 %collective-permute-start.2 = (f32[32,2,32,128]{3,2,1,0:T(8,128)S(1)}, f32[32,2,32,128]{3,2,1,0:T(8,128)S(1)}, u32[]{:S(2)}, u32[]{:S(2)}) collective-permute-start(f32[32,2,32,128]{3,2,1,0:T(8,128)S(1)} %get-tuple-element.14), channel_id=1, source_target_pairs={{0,1},{1,0},{2,3},{3,2},{4,5},{5,4},{6,7},{7,6},{8,9},{9,8},{10,11... | collective-permute-start | bytes 3145736 | tf_op jit(solution)/shard_map/ppermute | solution.py:327
  91.8 4.3 %collective-permute-start.1 = (f32[32,2,32,128]{3,2,1,0:T(8,128)S(1)}, f32[32,2,32,128]{3,2,1,0:T(8,128)S(1)}, u32[]{:S(2)}, u32[]{:S(2)}) collective-permute-start(f32[32,2,32,128]{3,2,1,0:T(8,128)S(1)} %get-tuple-element.15), channel_id=1, source_target_pairs={{0,1},{1,0},{2,3},{3,2},{4,5},{5,4},{6,7},{7,6},{8,9},{9,8},{10,11... | collective-permute-start | bytes 3145736 | tf_op jit(solution)/shard_map/ppermute | solution.py:327
  96.1 16.6 %copy-start = (f32[256,4,128]{2,1,0:T(4,128)S(1)}, f32[256,4,128]{2,1,0:T(4,128)}, u32[]{:S(2)}) copy-start(f32[256,4,128]{2,1,0:T(4,128)} %param.11) | copy-start | bytes 1572868
  96.1 16.6 %copy-start.5 = (s32[4,128]{1,0:T(4,128)S(1)}, s32[4,128]{1,0:T(4,128)}, u32[]{:S(2)}) copy-start(s32[4,128]{1,0:T(4,128)} %mute_ref.3) | copy-start | bytes 6148

commit v8 on v7

--- a/solution.py
+++ b/solution.py
@@ -174,7 +174,7 @@
     )(pos, focusing, reflection)
 
 
-def source_kernel(pos_ref, th_ref, tl_ref, tth_ref, ttl_ref, mute_ref, x_ref, time_hbm, out_ref, time_ref, sem):
+def source_kernel(pos_ref, th_ref, tl_ref, tth_ref, ttl_ref, mute_ref, x_ref, time_ref, out_ref):
     turn = pos_ref[2]
     cols = []
     for j in range(2):
@@ -192,8 +192,6 @@
         val = jnp.where((t < mute) | (t > NT - mute), up[:, j * 128 : (j + 1) * 128], 0.0)
         time_ref[pl.ds(j, NT, stride=2), :] = val
         kept.append(val)
-    copy = pltpu.make_async_copy(time_ref, time_hbm, sem)
-    copy.start()
     back = mm3((tth_ref[...], ttl_ref[...]), split(jnp.concatenate(kept, axis=1)))
     for j in range(2):
         b = unturn(back[:, j * 128 : (j + 1) * 128].reshape(32, 8, 128), turn, 1)
@@ -201,19 +199,17 @@
         for f in range(KB):
             for i in range(8):
                 out_ref[place(f // 2, f % 2, i // 4, i % 4), j] = b[f]
-    copy.wait()
 
 
 def source_traces(pos, tables, mute, parts):
     return pl.pallas_call(
         source_kernel,
         in_specs=[SMEM] + [VMEM] * 6,
-        out_specs=[HBM, VMEM],
+        out_specs=[VMEM] * 2,
         out_shape=[
             jax.ShapeDtypeStruct((NT * 2, 128), F32),
             jax.ShapeDtypeStruct((64, 2, 32, 128), F32),
         ],
-        scratch_shapes=[pltpu.VMEM((NT * 2, 128), F32), pltpu.SemaphoreType.DMA],
         compiler_params=params(8),
         name="source_traces",
     )(pos, *tables, mute, parts)
@@ -273,7 +269,11 @@
     )(own, oth, rh, rl, *before)
 
 
-def receiver_kernel(pos_ref, th_ref, tl_ref, mute_ref, direct_ref, x_ref, out_ref):
+def receiver_kernel(
+    pos_ref, th_ref, tl_ref, mute_ref, direct_ref, x_ref, time_ref, out_ref, time_hbm, sem
+):
+    copy = pltpu.make_async_copy(time_ref, time_hbm, sem)
+    copy.start()
     even = pos_ref[0] == 0
     turn = pos_ref[1]
     t = lax.broadcasted_iota(jnp.int32, (NT, 128), 0)
@@ -289,17 +289,22 @@
             val = jnp.where((t < mute) | (t > NT - mute), adj[:, j * 128 : (j + 1) * 128], 0.0)
             rows = pl.ds(p, NT, stride=4)
             out_ref[rows, :] = direct_ref[rows, :] - val
-
-
-def receiver_traces(pos, tables, mute, direct, x):
+    copy.wait()
+
+
+def receiver_traces(pos, tables, mute, direct, x, time):
     return pl.pallas_call(
         receiver_kernel,
-        in_specs=[SMEM] + [VMEM] * 5,
-        out_specs=VMEM,
-        out_shape=jax.ShapeDtypeStruct((NT * 4, 128), F32),
+        in_specs=[SMEM] + [VMEM] * 6,
+        out_specs=[VMEM, HBM],
+        out_shape=[
+            jax.ShapeDtypeStruct((NT * 4, 128), F32),
+            jax.ShapeDtypeStruct((NT * 2, 128), F32),
+        ],
+        scratch_shapes=[pltpu.SemaphoreType.DMA],
         compiler_params=params(8),
         name="receiver_traces",
-    )(pos, *tables, mute, direct, x)
+    )(pos, *tables, mute, direct, x, time)
 
 
 SWAP = [(0, 1), (1, 0)]
@@ -328,8 +333,8 @@
     adjoint = adjoint_panel(0, b_own, b_oth[0], rh, rl)
     adjoint = adjoint_panel(1, b_own, b_oth[1], rh, rl, adjoint)
     received = lax.all_to_all(adjoint, ("z", "xh"), split_axis=0, concat_axis=0, tiled=True)
-    plus = receiver_traces(
-        pos, (th, tl), mute_receiver, direct_wave.reshape(NT * 4, 128), received
+    plus, time = receiver_traces(
+        pos, (th, tl), mute_receiver, direct_wave.reshape(NT * 4, 128), received, time
     )
     return time.reshape(NT, 2, 128), plus.reshape(NT, 4, 128)
 

time: 115 us -> 115 us (level)
  no operation moved by 1% of the time
where the time goes in v8:
time: 115 us; the launch traced here: 114 us
  blocking collectives  90.4 us (79%)
  Pallas kernels  15.4 us (13%)
  waiting for transfers between devices  6.3 us (5%)
    all_to_all x2, blocking collectives, exchange(): lax.all_to_all(x, EVERY, split_axis=0, concat_axis=0, tiled=True, axis_in...  75.5 us
    all_to_all x1, blocking collectives, body(): lax.all_to_all(adjoint, ('z', 'xh'), split_axis=0, concat_axis=0, tiled=T...  15 us
    pallas_call x1, Pallas kernels, forward_panel(): pl.pallas_call(forward_kernel, in_specs=[SMEM, HBM, HBM], out_specs=[VMEM...  8.65 us
    ppermute x1, waiting for transfers between devices, body(): parts = exchange(own + lax.ppermute(oth, 'c', SWAP))  4.15 us
    pallas_call x2, Pallas kernels, adjoint_panel(): pl.pallas_call(functools.partial(adjoint_kernel, second), in_specs=[VMEM]...  3.26 us
  transfers between devices with their start and end apart: 3, of which 2 were waited for; matrix products, arithmetic and copies ran while one was open for 0% of the time, Pallas kernels for 1%

profile of v8, /device:TPU:0, one launch (start us, length us, event | category | flops | bytes accessed | tf_op | source)
XLA Modules:
  0.0 114.4 jit_solution(10216088467890911765)
XLA Ops:
  0.6 0.1 pad_add_fusion.pos_ref
  0.7 8.6 %forward_panel.1 = (f32[64,2,32,128]{3,2,1,0:T(8,128)S(1)}, f32[64,2,32,128]{3,2,1,0:T(8,128)S(1)}, bf16[16,1024,256]{2,1,0:T(8,128)(2,1)S(1)}, bf16[16,1024,256]{2,1,0:T(8,128)(2,1)S(1)}) custom-call(s32[3]{0:T(128)S(1)} %pad_add_fusion.pos_ref, f32[16,2,32,128]{3,2,1,0:T(8,128)} %f_hbm.1, f32[16,2,1024,128]{3,2,1,0:T(8,128)} %r_hbm.1), custom_call_target="tpu_custom_call" | custom-call | flops 3221225472 | bytes 22020096 | tf_op jit(solution)/shard_map/forward_panel/pallas_call | solution.py:160
  9.4 0.1 collective-permute-start
  9.5 4.1 %collective-permute-done = f32[64,2,32,128]{3,2,1,0:T(8,128)S(1)} collective-permute-done((f32[64,2,32,128]{3,2,1,0:T(8,128)S(1)}, f32[64,2,32,128]{3,2,1,0:T(8,128)S(1)}, u32[]{:S(2)}, u32[]{:S(2)}) %collective-permute-start) | collective-permute-done | bytes 2097184 | tf_op jit(solution)/shard_map/ppermute | solution.py:329
  13.6 0.5 add.7
  14.1 0.0 copy-start.1
  14.1 0.0 copy-start.2
  14.1 0.0 copy-start.3
  14.1 0.0 copy-start.4
  14.1 0.0 copy-start.6
  14.2 41.1 %all_to_all.15.x_ref = f32[64,2,32,128]{3,2,1,0:T(8,128)S(1)} all-to-all(f32[64,2,32,128]{3,2,1,0:T(8,128)S(1)} %add.7), channel_id=1, replica_groups={{0,10,20,30,8,18,28,6,16,26,4,14,24,2,12,22,32,42,52,62,40,50,60,38,48,..., dimensions={0} | all-to-all | bytes 4194304 | tf_op jit(solution)/shard_map/all_to_all | solution.py:315
  55.3 0.0 copy-done.1
  55.3 0.0 copy-done.2
  55.3 0.0 copy-done.3
  55.3 0.0 copy-done.4
  55.3 0.0 copy-done.6
  55.3 1.5 %source_traces.1 = (f32[512,128]{1,0:T(8,128)S(1)}, f32[64,2,32,128]{3,2,1,0:T(8,128)S(1)}) custom-call(s32[3]{0:T(128)S(1)} %pad_add_fusion.pos_ref, bf16[256,256]{1,0:T(8,128)(2,1)S(1)} %copy-done.2, bf16[256,256]{1,0:T(8,128)(2,1)S(1)} %copy-done.1, bf16[256,256]{1,0:T(8,128)(2,1)S(1)} %copy-done.4, bf16[256,256]{1,0:T(8,128)(2,1)S(1)} %copy-done.3, ...), custom_call_target="tpu_custom_call" | custom-call | tf_op jit(solution)/shard_map/source_traces/pallas_call | solution.py:205
  56.8 34.3 %all_to_all.16.own = f32[64,2,32,128]{3,2,1,0:T(8,128)S(1)} all-to-all(f32[64,2,32,128]{3,2,1,0:T(8,128)S(1)} %get-tuple-element.12), channel_id=1, replica_groups={{0,10,20,30,8,18,28,6,16,26,4,14,24,2,12,22,32,42,52,62,40,50,60,38,48,..., dimensions={0} | all-to-all | bytes 4194304 | tf_op jit(solution)/shard_map/all_to_all | solution.py:315
  91.1 0.2 fusion
  91.3 0.1 collective-permute-start.2
  91.4 0.5 collective-permute-start.1
  91.9 2.1 %collective-permute-done.2.oth = f32[32,2,32,128]{3,2,1,0:T(8,128)S(1)} collective-permute-done((f32[32,2,32,128]{3,2,1,0:T(8,128)S(1)}, f32[32,2,32,128]{3,2,1,0:T(8,128)S(1)}, u32[]{:S(2)}, u32[]{:S(2)}) %collective-permute-start.2) | collective-permute-done | bytes 1048608 | tf_op jit(solution)/shard_map/ppermute | solution.py:332
  94.1 1.6 %adjoint_panel0.1.rest_0_ = f32[8,4,32,128]{3,2,1,0:T(8,128)S(1)} custom-call(f32[64,2,32,128]{3,2,1,0:T(8,128)S(1)} %all_to_all.16.own, f32[32,2,32,128]{3,2,1,0:T(8,128)S(1)} %collective-permute-done.2.oth, bf16[16,1024,256]{2,1,0:T(8,128)(2,1)S(1)} %get-tuple-element.13.rh_ref, bf16[16,1024,256]{2,1,0:T(8,128)(2,1)S(1)} %get-tuple-element.14.rl_ref), custom_call_target="tpu_custom_call" | custom-call | flops 1610612736 | bytes 1048576 | tf_op jit(solution)/shard_map/adjoint_panel0/pallas_call | solution.py:261
  95.7 0.0 copy-start
  95.7 0.0 copy-start.5
  95.7 0.0 collective-permute-done.1.oth
  95.7 1.6 %adjoint_panel1.1 = f32[8,4,32,128]{3,2,1,0:T(8,128)S(1)} custom-call(f32[64,2,32,128]{3,2,1,0:T(8,128)S(1)} %all_to_all.16.own, f32[32,2,32,128]{3,2,1,0:T(8,128)S(1)} %collective-permute-done.1.oth, bf16[16,1024,256]{2,1,0:T(8,128)(2,1)S(1)} %get-tuple-element.13.rh_ref, bf16[16,1024,256]{2,1,0:T(8,128)(2,1)S(1)} %get-tuple-element.14.rl_ref, ...), custom_call_target="tpu_custom_call" | custom-call | flops 1610612736 | bytes 1048576 | tf_op jit(solution)/shard_map/adjoint_panel1/pallas_call | solution.py:261
  97.4 15.0 %all_to_all.17.x_ref = f32[8,4,32,128]{3,2,1,0:T(8,128)S(1)} all-to-all(f32[8,4,32,128]{3,2,1,0:T(8,128)S(1)} %adjoint_panel1.1), channel_id=1, replica_groups=mesh['z'=4,'xh'=2,'xl'=2,'y'=4,'c'=2] {'z','xh'}, dimensions={0} | all-to-all | bytes 1048576 | tf_op jit(solution)/shard_map/all_to_all | solution.py:335
  112.3 0.0 copy-done
  112.3 0.0 copy-done.5
  112.3 2.0 %receiver_traces.1 = (f32[1024,128]{1,0:T(8,128)}, f32[512,128]{1,0:T(8,128)}) custom-call(s32[3]{0:T(128)S(1)} %pad_add_fusion.pos_ref, bf16[256,256]{1,0:T(8,128)(2,1)S(1)} %copy-done.2, bf16[256,256]{1,0:T(8,128)(2,1)S(1)} %copy-done.1, s32[4,128]{1,0:T(4,128)S(1)} %copy-done.5, f32[1024,128]{1,0:T(8,128)S(1)} %bitcast.6, ...), custom_call_target="tpu_custom_call" | custom-call | tf_op jit(solution)/shard_map/receiver_traces/pallas_call | solution.py:296
Async XLA Ops:
  9.4 4.2 %collective-permute-start = (f32[64,2,32,128]{3,2,1,0:T(8,128)S(1)}, f32[64,2,32,128]{3,2,1,0:T(8,128)S(1)}, u32[]{:S(2)}, u32[]{:S(2)}) collective-permute-start(f32[64,2,32,128]{3,2,1,0:T(8,128)S(1)} %get-tuple-element.11), channel_id=1, source_target_pairs={{0,1},{1,0},{2,3},{3,2},{4,5},{5,4},{6,7},{7,6},{8,9},{9,8},{10,11... | collective-permute-start | bytes 6291464 | tf_op jit(solution)/shard_map/ppermute | solution.py:329
  14.1 41.2 %copy-start.1 = (bf16[256,256]{1,0:T(8,128)(2,1)S(1)}, bf16[256,256]{1,0:T(8,128)(2,1)}, u32[]{:S(2)}) copy-start(bf16[256,256]{1,0:T(8,128)(2,1)} %constant.29.clone.tl_ref) | copy-start | bytes 393220
  14.1 41.2 %copy-start.2 = (bf16[256,256]{1,0:T(8,128)(2,1)S(1)}, bf16[256,256]{1,0:T(8,128)(2,1)}, u32[]{:S(2)}) copy-start(bf16[256,256]{1,0:T(8,128)(2,1)} %constant.28.clone.th_ref) | copy-start | bytes 393220
  14.1 41.2 %copy-start.3 = (bf16[256,256]{1,0:T(8,128)(2,1)S(1)}, bf16[256,256]{1,0:T(8,128)(2,1)}, u32[]{:S(2)}) copy-start(bf16[256,256]{1,0:T(8,128)(2,1)} %constant.31.clone.ttl_ref) | copy-start | bytes 393220
  14.1 41.2 %copy-start.4 = (bf16[256,256]{1,0:T(8,128)(2,1)S(1)}, bf16[256,256]{1,0:T(8,128)(2,1)}, u32[]{:S(2)}) copy-start(bf16[256,256]{1,0:T(8,128)(2,1)} %constant.30.clone.tth_ref) | copy-start | bytes 393220
  14.1 41.2 %copy-start.6 = (s32[2,128]{1,0:T(2,128)S(1)}, s32[2,128]{1,0:T(2,128)}, u32[]{:S(2)}) copy-start(s32[2,128]{1,0:T(2,128)} %mute_ref.2) | copy-start | bytes 3076
  91.3 2.7 %collective-permute-start.2 = (f32[32,2,32,128]{3,2,1,0:T(8,128)S(1)}, f32[32,2,32,128]{3,2,1,0:T(8,128)S(1)}, u32[]{:S(2)}, u32[]{:S(2)}) collective-permute-start(f32[32,2,32,128]{3,2,1,0:T(8,128)S(1)} %get-tuple-element.18), channel_id=1, source_target_pairs={{0,1},{1,0},{2,3},{3,2},{4,5},{5,4},{6,7},{7,6},{8,9},{9,8},{10,11... | collective-permute-start | bytes 3145736 | tf_op jit(solution)/shard_map/ppermute | solution.py:332
  91.4 4.3 %collective-permute-start.1 = (f32[32,2,32,128]{3,2,1,0:T(8,128)S(1)}, f32[32,2,32,128]{3,2,1,0:T(8,128)S(1)}, u32[]{:S(2)}, u32[]{:S(2)}) collective-permute-start(f32[32,2,32,128]{3,2,1,0:T(8,128)S(1)} %get-tuple-element.19), channel_id=1, source_target_pairs={{0,1},{1,0},{2,3},{3,2},{4,5},{5,4},{6,7},{7,6},{8,9},{9,8},{10,11... | collective-permute-start | bytes 3145736 | tf_op jit(solution)/shard_map/ppermute | solution.py:332
  95.7 16.6 %copy-start = (f32[256,4,128]{2,1,0:T(4,128)S(1)}, f32[256,4,128]{2,1,0:T(4,128)}, u32[]{:S(2)}) copy-start(f32[256,4,128]{2,1,0:T(4,128)} %param.11) | copy-start | bytes 1572868
  95.7 16.6 %copy-start.5 = (s32[4,128]{1,0:T(4,128)S(1)}, s32[4,128]{1,0:T(4,128)}, u32[]{:S(2)}) copy-start(s32[4,128]{1,0:T(4,128)} %mute_ref.3) | copy-start | bytes 6148

commit v9 on v7

--- a/solution.py
+++ b/solution.py
@@ -63,17 +63,7 @@
 
 
 def place(z, xh, xl, y):
-    return z * 16 + ((xh * 2 + xl - y) % 4) * 4 + y
-
-
-def place_groups():
-    order = [None] * 64
-    for z in range(4):
-        for xh in range(2):
-            for xl in range(2):
-                for y in range(4):
-                    order[place(z, xh, xl, y)] = ((z * 2 + xh) * 2 + xl) * 4 + y
-    return [[chip * 2 + core for chip in order] for core in range(2)]
+    return ((z * 2 + xl) * 2 + xh) * 4 + y
 
 
 AHEAD = 7
@@ -174,7 +164,7 @@
     )(pos, focusing, reflection)
 
 
-def source_kernel(pos_ref, th_ref, tl_ref, tth_ref, ttl_ref, mute_ref, x_ref, time_hbm, out_ref, time_ref, sem):
+def source_kernel(pos_ref, th_ref, tl_ref, tth_ref, ttl_ref, mute_ref, x_ref, time_ref, out_ref):
     turn = pos_ref[2]
     cols = []
     for j in range(2):
@@ -192,8 +182,6 @@
         val = jnp.where((t < mute) | (t > NT - mute), up[:, j * 128 : (j + 1) * 128], 0.0)
         time_ref[pl.ds(j, NT, stride=2), :] = val
         kept.append(val)
-    copy = pltpu.make_async_copy(time_ref, time_hbm, sem)
-    copy.start()
     back = mm3((tth_ref[...], ttl_ref[...]), split(jnp.concatenate(kept, axis=1)))
     for j in range(2):
         b = unturn(back[:, j * 128 : (j + 1) * 128].reshape(32, 8, 128), turn, 1)
@@ -201,26 +189,26 @@
         for f in range(KB):
             for i in range(8):
                 out_ref[place(f // 2, f % 2, i // 4, i % 4), j] = b[f]
-    copy.wait()
 
 
 def source_traces(pos, tables, mute, parts):
     return pl.pallas_call(
         source_kernel,
         in_specs=[SMEM] + [VMEM] * 6,
-        out_specs=[HBM, VMEM],
+        out_specs=[VMEM] * 2,
         out_shape=[
             jax.ShapeDtypeStruct((NT * 2, 128), F32),
             jax.ShapeDtypeStruct((64, 2, 32, 128), F32),
         ],
-        scratch_shapes=[pltpu.VMEM((NT * 2, 128), F32), pltpu.SemaphoreType.DMA],
         compiler_params=params(8),
         name="source_traces",
     )(pos, *tables, mute, parts)
 
 
-def adjoint_kernel(second, own, oth, rh_ref, rl_ref, *rest):
-    out_ref = rest[-1]
+def adjoint_kernel(second, own, oth, rh_ref, rl_ref, extra_ref, out_ref, time_hbm=None, sem=None):
+    if not second:
+        copy = pltpu.make_async_copy(extra_ref, time_hbm, sem)
+        copy.start()
     pair = lax.broadcasted_iota(jnp.int32, (8, 128), 0) // 2
     even = (lax.broadcasted_iota(jnp.int32, (64, 128), 0) % 2) == 0
 
@@ -258,19 +246,24 @@
             for y in range(4):
                 at = ((part % 2) * 4 + y, part // 2, g8, slice(None))
                 t = trade(v, pair, y)
-                out_ref[at] = rest[0][at] + t if second else t
-
-
-def adjoint_panel(second, own, oth, rh, rl, *before):
+                out_ref[at] = extra_ref[at] + t if second else t
+    if not second:
+        copy.wait()
+
+
+def adjoint_panel(second, own, oth, rh, rl, extra):
+    panel = jax.ShapeDtypeStruct((8, 4, 32, 128), F32)
+    time = jax.ShapeDtypeStruct((NT * 2, 128), F32)
     return pl.pallas_call(
         functools.partial(adjoint_kernel, second),
-        in_specs=[VMEM] * (4 + len(before)),
-        out_specs=VMEM,
-        out_shape=jax.ShapeDtypeStruct((8, 4, 32, 128), F32),
+        in_specs=[VMEM] * 5,
+        out_specs=VMEM if second else [VMEM, HBM],
+        out_shape=panel if second else [panel, time],
+        scratch_shapes=[] if second else [pltpu.SemaphoreType.DMA],
         compiler_params=params(8),
         cost_estimate=pl.CostEstimate(flops=3 * 2**29, bytes_accessed=2**20, transcendentals=0),
         name=f"adjoint_panel{second}",
-    )(own, oth, rh, rl, *before)
+    )(own, oth, rh, rl, extra)
 
 
 def receiver_kernel(pos_ref, th_ref, tl_ref, mute_ref, direct_ref, x_ref, out_ref):
@@ -303,13 +296,11 @@
 
 
 SWAP = [(0, 1), (1, 0)]
-EVERY = ("z", "xh", "xl", "y", "c")
-
-
-def exchange(x):
-    return lax.all_to_all(
-        x, EVERY, split_axis=0, concat_axis=0, tiled=True, axis_index_groups=place_groups()
-    )
+CHIPS = ("z", "xl", "xh", "y")
+
+
+def exchange(x, axes):
+    return lax.all_to_all(x, axes, split_axis=0, concat_axis=0, tiled=True)
 
 
 def body(reflection, focusing, direct_wave, mute_source, mute_receiver):
@@ -321,13 +312,13 @@
     focusing = pltpu.with_memory_space_constraint(focusing, pltpu.HBM)
     reflection = pltpu.with_memory_space_constraint(reflection, pltpu.HBM)
     own, oth, rh, rl = forward_panel(pos, focusing, reflection)
-    parts = exchange(own + lax.ppermute(oth, "c", SWAP))
+    parts = exchange(own + lax.ppermute(oth, "c", SWAP), CHIPS)
     time, back = source_traces(pos, (th, tl, th.T, tl.T), mute_source, parts)
-    b_own = exchange(back)
+    b_own = exchange(back, CHIPS)
     b_oth = [lax.ppermute(b_own[i * 32 : i * 32 + 32], "c", SWAP) for i in range(2)]
-    adjoint = adjoint_panel(0, b_own, b_oth[0], rh, rl)
+    adjoint, time = adjoint_panel(0, b_own, b_oth[0], rh, rl, time)
     adjoint = adjoint_panel(1, b_own, b_oth[1], rh, rl, adjoint)
-    received = lax.all_to_all(adjoint, ("z", "xh"), split_axis=0, concat_axis=0, tiled=True)
+    received = exchange(adjoint, ("z", "xh"))
     plus = receiver_traces(
         pos, (th, tl), mute_receiver, direct_wave.reshape(NT * 4, 128), received
     )

time: 115 us -> 114 us (level)
  no operation moved by 1% of the time
where the time goes in v9:
time: 114 us
  blocking collectives  90 us (79%)
  Pallas kernels  15.2 us (13%)
  waiting for transfers between devices  6.3 us (6%)
    all_to_all x3, blocking collectives, exchange(): return lax.all_to_all(x, axes, split_axis=0, concat_axis=0, tiled=True)  90 us
    pallas_call x1, Pallas kernels, forward_panel(): pl.pallas_call(forward_kernel, in_specs=[SMEM, HBM, HBM], out_specs=[VMEM...  8.65 us
    ppermute x1, waiting for transfers between devices, body(): parts = exchange(own + lax.ppermute(oth, 'c', SWAP), CHIPS)  4.15 us
    pallas_call x2, Pallas kernels, adjoint_panel(): pl.pallas_call(functools.partial(adjoint_kernel, second), in_specs=[VMEM]...  3.27 us
  transfers between devices with their start and end apart: 3, of which 2 were waited for; matrix products, arithmetic and copies ran while one was open for 0% of the time, Pallas kernels for 1%

profile of v9, /device:TPU:0, one launch (start us, length us, event | category | flops | bytes accessed | tf_op | source)
XLA Modules:
  0.0 113.9 jit_solution(4334159769607591972)
XLA Ops:
  0.6 0.1 pad_add_fusion.pos_ref
  0.7 8.6 %forward_panel.1 = (f32[64,2,32,128]{3,2,1,0:T(8,128)S(1)}, f32[64,2,32,128]{3,2,1,0:T(8,128)S(1)}, bf16[16,1024,256]{2,1,0:T(8,128)(2,1)S(1)}, bf16[16,1024,256]{2,1,0:T(8,128)(2,1)S(1)}) custom-call(s32[3]{0:T(128)S(1)} %pad_add_fusion.pos_ref, f32[16,2,32,128]{3,2,1,0:T(8,128)} %f_hbm.1, f32[16,2,1024,128]{3,2,1,0:T(8,128)} %r_hbm.1), custom_call_target="tpu_custom_call" | custom-call | flops 3221225472 | bytes 22020096 | tf_op jit(solution)/shard_map/forward_panel/pallas_call | solution.py:150
  9.4 0.1 collective-permute-start
  9.5 4.1 %collective-permute-done = f32[64,2,32,128]{3,2,1,0:T(8,128)S(1)} collective-permute-done((f32[64,2,32,128]{3,2,1,0:T(8,128)S(1)}, f32[64,2,32,128]{3,2,1,0:T(8,128)S(1)}, u32[]{:S(2)}, u32[]{:S(2)}) %collective-permute-start) | collective-permute-done | bytes 2097184 | tf_op jit(solution)/shard_map/ppermute | solution.py:315
  13.6 0.5 add.7
  14.1 0.0 copy-start.1
  14.1 0.0 copy-start.2
  14.1 0.0 copy-start.3
  14.1 0.0 copy-start.4
  14.1 0.0 copy-start.6
  14.2 41.3 %all_to_all.15.x_ref = f32[64,2,32,128]{3,2,1,0:T(8,128)S(1)} all-to-all(f32[64,2,32,128]{3,2,1,0:T(8,128)S(1)} %add.7), channel_id=1, replica_groups=mesh['z'=4,'xh'=2,'xl'=2,'y'=4,'c'=2] {'z','xl','xh','y'}, dimensions={0} | all-to-all | bytes 4194304 | tf_op jit(solution)/shard_map/all_to_all | solution.py:303
  55.5 0.0 copy-done.1
  55.5 0.0 copy-done.2
  55.5 0.0 copy-done.3
  55.5 0.0 copy-done.4
  55.5 0.0 copy-done.6
  55.5 1.5 %source_traces.1 = (f32[512,128]{1,0:T(8,128)S(1)}, f32[64,2,32,128]{3,2,1,0:T(8,128)S(1)}) custom-call(s32[3]{0:T(128)S(1)} %pad_add_fusion.pos_ref, bf16[256,256]{1,0:T(8,128)(2,1)S(1)} %copy-done.2, bf16[256,256]{1,0:T(8,128)(2,1)S(1)} %copy-done.1, bf16[256,256]{1,0:T(8,128)(2,1)S(1)} %copy-done.4, bf16[256,256]{1,0:T(8,128)(2,1)S(1)} %copy-done.3, ...), custom_call_target="tpu_custom_call" | custom-call | tf_op jit(solution)/shard_map/source_traces/pallas_call | solution.py:195
  56.9 34.0 %all_to_all.16.own = f32[64,2,32,128]{3,2,1,0:T(8,128)S(1)} all-to-all(f32[64,2,32,128]{3,2,1,0:T(8,128)S(1)} %get-tuple-element.12), channel_id=1, replica_groups=mesh['z'=4,'xh'=2,'xl'=2,'y'=4,'c'=2] {'z','xl','xh','y'}, dimensions={0} | all-to-all | bytes 4194304 | tf_op jit(solution)/shard_map/all_to_all | solution.py:303
  90.9 0.3 fusion
  91.2 0.1 collective-permute-start.1
  91.3 0.5 collective-permute-start.2
  91.8 2.1 %collective-permute-done.1.oth = f32[32,2,32,128]{3,2,1,0:T(8,128)S(1)} collective-permute-done((f32[32,2,32,128]{3,2,1,0:T(8,128)S(1)}, f32[32,2,32,128]{3,2,1,0:T(8,128)S(1)}, u32[]{:S(2)}, u32[]{:S(2)}) %collective-permute-start.1) | collective-permute-done | bytes 1048608 | tf_op jit(solution)/shard_map/ppermute | solution.py:318
  93.9 1.6 %adjoint_panel0.1 = (f32[8,4,32,128]{3,2,1,0:T(8,128)S(1)}, f32[512,128]{1,0:T(8,128)}) custom-call(f32[64,2,32,128]{3,2,1,0:T(8,128)S(1)} %all_to_all.16.own, f32[32,2,32,128]{3,2,1,0:T(8,128)S(1)} %collective-permute-done.1.oth, bf16[16,1024,256]{2,1,0:T(8,128)(2,1)S(1)} %get-tuple-element.13.rh_ref, bf16[16,1024,256]{2,1,0:T(8,128)(2,1)S(1)} %get-tuple-element.14.rl_ref, ...), custom_call_target="tpu_custom_call" | custom-call | flops 1610612736 | bytes 1048576 | tf_op jit(solution)/shard_map/adjoint_panel0/pallas_call | solution.py:257
  95.6 0.0 collective-permute-done.2.oth
  95.6 0.0 copy-start
  95.6 0.0 copy-start.5
  95.6 1.6 %adjoint_panel1.1 = f32[8,4,32,128]{3,2,1,0:T(8,128)S(1)} custom-call(f32[64,2,32,128]{3,2,1,0:T(8,128)S(1)} %all_to_all.16.own, f32[32,2,32,128]{3,2,1,0:T(8,128)S(1)} %collective-permute-done.2.oth, bf16[16,1024,256]{2,1,0:T(8,128)(2,1)S(1)} %get-tuple-element.13.rh_ref, bf16[16,1024,256]{2,1,0:T(8,128)(2,1)S(1)} %get-tuple-element.14.rl_ref, ...), custom_call_target="tpu_custom_call" | custom-call | flops 1610612736 | bytes 1048576 | tf_op jit(solution)/shard_map/adjoint_panel1/pallas_call | solution.py:257
  97.2 14.7 %all_to_all.17.x_ref = f32[8,4,32,128]{3,2,1,0:T(8,128)S(1)} all-to-all(f32[8,4,32,128]{3,2,1,0:T(8,128)S(1)} %adjoint_panel1.1), channel_id=1, replica_groups=mesh['z'=4,'xh'=2,'xl'=2,'y'=4,'c'=2] {'z','xh'}, dimensions={0} | all-to-all | bytes 1048576 | tf_op jit(solution)/shard_map/all_to_all | solution.py:303
  112.0 0.0 copy-done
  112.0 0.0 copy-done.5
  112.0 1.9 %receiver_traces.1 = f32[1024,128]{1,0:T(8,128)} custom-call(s32[3]{0:T(128)S(1)} %pad_add_fusion.pos_ref, bf16[256,256]{1,0:T(8,128)(2,1)S(1)} %copy-done.2, bf16[256,256]{1,0:T(8,128)(2,1)S(1)} %copy-done.1, s32[4,128]{1,0:T(4,128)S(1)} %copy-done.5, f32[1024,128]{1,0:T(8,128)S(1)} %bitcast.6, f32[8,4,32,128]{3,2,1,0:T(8,128)S(1)} %all_to_all.17.x_ref), custom_call_target="tpu_custom_call" | custom-call | tf_op jit(solution)/shard_map/receiver_traces/pallas_call | solution.py:288
Async XLA Ops:
  9.4 4.2 %collective-permute-start = (f32[64,2,32,128]{3,2,1,0:T(8,128)S(1)}, f32[64,2,32,128]{3,2,1,0:T(8,128)S(1)}, u32[]{:S(2)}, u32[]{:S(2)}) collective-permute-start(f32[64,2,32,128]{3,2,1,0:T(8,128)S(1)} %get-tuple-element.11), channel_id=1, source_target_pairs={{0,1},{1,0},{2,3},{3,2},{4,5},{5,4},{6,7},{7,6},{8,9},{9,8},{10,11... | collective-permute-start | bytes 6291464 | tf_op jit(solution)/shard_map/ppermute | solution.py:315
  14.1 41.4 %copy-start.1 = (bf16[256,256]{1,0:T(8,128)(2,1)S(1)}, bf16[256,256]{1,0:T(8,128)(2,1)}, u32[]{:S(2)}) copy-start(bf16[256,256]{1,0:T(8,128)(2,1)} %constant.29.clone.tl_ref) | copy-start | bytes 393220
  14.1 41.4 %copy-start.2 = (bf16[256,256]{1,0:T(8,128)(2,1)S(1)}, bf16[256,256]{1,0:T(8,128)(2,1)}, u32[]{:S(2)}) copy-start(bf16[256,256]{1,0:T(8,128)(2,1)} %constant.28.clone.th_ref) | copy-start | bytes 393220
  14.1 41.3 %copy-start.3 = (bf16[256,256]{1,0:T(8,128)(2,1)S(1)}, bf16[256,256]{1,0:T(8,128)(2,1)}, u32[]{:S(2)}) copy-start(bf16[256,256]{1,0:T(8,128)(2,1)} %constant.31.clone.ttl_ref) | copy-start | bytes 393220
  14.1 41.3 %copy-start.4 = (bf16[256,256]{1,0:T(8,128)(2,1)S(1)}, bf16[256,256]{1,0:T(8,128)(2,1)}, u32[]{:S(2)}) copy-start(bf16[256,256]{1,0:T(8,128)(2,1)} %constant.30.clone.tth_ref) | copy-start | bytes 393220
  14.1 41.3 %copy-start.6 = (s32[2,128]{1,0:T(2,128)S(1)}, s32[2,128]{1,0:T(2,128)}, u32[]{:S(2)}) copy-start(s32[2,128]{1,0:T(2,128)} %mute_ref.2) | copy-start | bytes 3076
  91.2 2.7 %collective-permute-start.1 = (f32[32,2,32,128]{3,2,1,0:T(8,128)S(1)}, f32[32,2,32,128]{3,2,1,0:T(8,128)S(1)}, u32[]{:S(2)}, u32[]{:S(2)}) collective-permute-start(f32[32,2,32,128]{3,2,1,0:T(8,128)S(1)} %get-tuple-element.19), channel_id=1, source_target_pairs={{0,1},{1,0},{2,3},{3,2},{4,5},{5,4},{6,7},{7,6},{8,9},{9,8},{10,11... | collective-permute-start | bytes 3145736 | tf_op jit(solution)/shard_map/ppermute | solution.py:318
  91.3 4.3 %collective-permute-start.2 = (f32[32,2,32,128]{3,2,1,0:T(8,128)S(1)}, f32[32,2,32,128]{3,2,1,0:T(8,128)S(1)}, u32[]{:S(2)}, u32[]{:S(2)}) collective-permute-start(f32[32,2,32,128]{3,2,1,0:T(8,128)S(1)} %get-tuple-element.18), channel_id=1, source_target_pairs={{0,1},{1,0},{2,3},{3,2},{4,5},{5,4},{6,7},{7,6},{8,9},{9,8},{10,11... | collective-permute-start | bytes 3145736 | tf_op jit(solution)/shard_map/ppermute | solution.py:318
  95.6 16.4 %copy-start = (f32[256,4,128]{2,1,0:T(4,128)S(1)}, f32[256,4,128]{2,1,0:T(4,128)}, u32[]{:S(2)}) copy-start(f32[256,4,128]{2,1,0:T(4,128)} %param.11) | copy-start | bytes 1572868
  95.6 16.4 %copy-start.5 = (s32[4,128]{1,0:T(4,128)S(1)}, s32[4,128]{1,0:T(4,128)}, u32[]{:S(2)}) copy-start(s32[4,128]{1,0:T(4,128)} %mute_ref.3) | copy-start | bytes 6148

commit v10 on v9

--- a/solution.py
+++ b/solution.py
@@ -63,7 +63,7 @@
 
 
 def place(z, xh, xl, y):
-    return ((z * 2 + xl) * 2 + xh) * 4 + y
+    return ((xh * 4 + z) * 2 + xl) * 4 + y
 
 
 AHEAD = 7
@@ -223,7 +223,7 @@
                 for part in range(8):
                     j, xlo = part // 4, part % 2
                     if (part // 2) % 2:
-                        v = [oth[place(zz, xh_, xlo, y), j, g8, :] for y in range(4)]
+                        v = [oth[((xh_ * 2 + zz) * 2 + xlo) * 4 + y, j, g8, :] for y in range(4)]
                     else:
                         v = [own[place(z, xh_, xlo, y), j, g8, :] for y in range(4)]
                     for q in range(4):
@@ -266,37 +266,46 @@
     )(own, oth, rh, rl, extra)
 
 
-def receiver_kernel(pos_ref, th_ref, tl_ref, mute_ref, direct_ref, x_ref, out_ref):
+def receiver_kernel(pos_ref, th_ref, tl_ref, mute_ref, direct_ref, x_ref, out_hbm, out_ref, sem):
     even = pos_ref[0] == 0
     turn = pos_ref[1]
-    t = lax.broadcasted_iota(jnp.int32, (NT, 128), 0)
+    adj = []
     for c in range(2):
         cols = []
         for j in range(2):
             a = jnp.where(even, x_ref[:, j * 2 + c], x_ref[:, j * 2 + 1 - c])
             cols.append(unturn(a.reshape(32, 8, 128), turn, -1).reshape(256, 128))
-        adj = mm3((th_ref[...], tl_ref[...]), split(jnp.concatenate(cols, axis=1)))
-        for j in range(2):
-            p = c * 2 + j
-            mute = jnp.broadcast_to(mute_ref[p : p + 1, :], (NT, 128))
-            val = jnp.where((t < mute) | (t > NT - mute), adj[:, j * 128 : (j + 1) * 128], 0.0)
-            rows = pl.ds(p, NT, stride=4)
-            out_ref[rows, :] = direct_ref[rows, :] - val
+        adj.append(mm3((th_ref[...], tl_ref[...]), split(jnp.concatenate(cols, axis=1))))
+    copies = []
+    for b in range(4):
+        t = lax.broadcasted_iota(jnp.int32, (64, 128), 0) + b * 64
+        for p in range(4):
+            mute = jnp.broadcast_to(mute_ref[p : p + 1, :], (64, 128))
+            val = adj[p // 2][b * 64 : b * 64 + 64, (p % 2) * 128 : (p % 2) * 128 + 128]
+            rows = pl.ds(b * 256 + p, 64, stride=4)
+            kept = jnp.where((t < mute) | (t > NT - mute), val, 0.0)
+            out_ref[rows, :] = direct_ref[rows, :] - kept
+        cut = pl.ds(b * 256, 256)
+        copies.append(pltpu.make_async_copy(out_ref.at[cut], out_hbm.at[cut], sem.at[b]))
+        copies[b].start()
+    for copy in copies:
+        copy.wait()
 
 
 def receiver_traces(pos, tables, mute, direct, x):
     return pl.pallas_call(
         receiver_kernel,
         in_specs=[SMEM] + [VMEM] * 5,
-        out_specs=VMEM,
+        out_specs=HBM,
         out_shape=jax.ShapeDtypeStruct((NT * 4, 128), F32),
+        scratch_shapes=[pltpu.VMEM((NT * 4, 128), F32), pltpu.SemaphoreType.DMA((4,))],
         compiler_params=params(8),
         name="receiver_traces",
     )(pos, *tables, mute, direct, x)
 
 
 SWAP = [(0, 1), (1, 0)]
-CHIPS = ("z", "xl", "xh", "y")
+CHIPS = ("xh", "z", "xl", "y")
 
 
 def exchange(x, axes):
@@ -315,7 +324,10 @@
     parts = exchange(own + lax.ppermute(oth, "c", SWAP), CHIPS)
     time, back = source_traces(pos, (th, tl, th.T, tl.T), mute_source, parts)
     b_own = exchange(back, CHIPS)
-    b_oth = [lax.ppermute(b_own[i * 32 : i * 32 + 32], "c", SWAP) for i in range(2)]
+    by_z = b_own.reshape(2, 4, 8, 2, 32, 128)
+    b_oth = [
+        lax.ppermute(by_z[:, i * 2 : i * 2 + 2].reshape(32, 2, 32, 128), "c", SWAP) for i in range(2)
+    ]
     adjoint, time = adjoint_panel(0, b_own, b_oth[0], rh, rl, time)
     adjoint = adjoint_panel(1, b_own, b_oth[1], rh, rl, adjoint)
     received = exchange(adjoint, ("z", "xh"))

time: 114 us -> 116 us (1.018)
  blocking collectives: 90 us -> 91.9 us
    all_to_all x3, blocking collectives: 90 us -> 91.9 us  [exchange(): return lax.all_to_all(x, axes, split_axis=0, concat_axis=0, tiled=True)]
where the time goes in v10:
time: 116 us
  blocking collectives  91.9 us (79%)
  Pallas kernels  15.2 us (13%)
  waiting for transfers between devices  6.3 us (5%)
    all_to_all x3, blocking collectives, exchange(): return lax.all_to_all(x, axes, split_axis=0, concat_axis=0, tiled=True)  91.9 us
    pallas_call x1, Pallas kernels, forward_panel(): pl.pallas_call(forward_kernel, in_specs=[SMEM, HBM, HBM], out_specs=[VMEM...  8.65 us
    ppermute x1, waiting for transfers between devices, body(): parts = exchange(own + lax.ppermute(oth, 'c', SWAP), CHIPS)  4.15 us
    pallas_call x2, Pallas kernels, adjoint_panel(): pl.pallas_call(functools.partial(adjoint_kernel, second), in_specs=[VMEM]...  3.27 us
  transfers between devices with their start and end apart: 3, of which 2 were waited for; matrix products, arithmetic and copies ran while one was open for 0% of the time, Pallas kernels for 1%

profile of v10, /device:TPU:0, one launch (start us, length us, event | category | flops | bytes accessed | tf_op | source)
XLA Modules:
  0.0 115.7 jit_solution(12910295349019969868)
XLA Ops:
  0.6 0.1 pad_add_fusion.pos_ref
  0.7 8.6 %forward_panel.1 = (f32[64,2,32,128]{3,2,1,0:T(8,128)S(1)}, f32[64,2,32,128]{3,2,1,0:T(8,128)S(1)}, bf16[16,1024,256]{2,1,0:T(8,128)(2,1)S(1)}, bf16[16,1024,256]{2,1,0:T(8,128)(2,1)S(1)}) custom-call(s32[3]{0:T(128)S(1)} %pad_add_fusion.pos_ref, f32[16,2,32,128]{3,2,1,0:T(8,128)} %f_hbm.1, f32[16,2,1024,128]{3,2,1,0:T(8,128)} %r_hbm.1), custom_call_target="tpu_custom_call" | custom-call | flops 3221225472 | bytes 22020096 | tf_op jit(solution)/shard_map/forward_panel/pallas_call | solution.py:150
  9.4 0.1 collective-permute-start
  9.5 4.1 %collective-permute-done = f32[64,2,32,128]{3,2,1,0:T(8,128)S(1)} collective-permute-done((f32[64,2,32,128]{3,2,1,0:T(8,128)S(1)}, f32[64,2,32,128]{3,2,1,0:T(8,128)S(1)}, u32[]{:S(2)}, u32[]{:S(2)}) %collective-permute-start) | collective-permute-done | bytes 2097184 | tf_op jit(solution)/shard_map/ppermute | solution.py:324
  13.6 0.5 add.7
  14.1 0.0 copy-start.1
  14.1 0.0 copy-start.2
  14.1 0.0 copy-start.3
  14.1 0.0 copy-start.4
  14.1 0.0 copy-start.6
  14.2 41.3 %all_to_all.15.x_ref = f32[64,2,32,128]{3,2,1,0:T(8,128)S(1)} all-to-all(f32[64,2,32,128]{3,2,1,0:T(8,128)S(1)} %add.7), channel_id=1, replica_groups=mesh['z'=4,'xh'=2,'xl'=2,'y'=4,'c'=2] {'xh','z','xl','y'}, dimensions={0} | all-to-all | bytes 4194304 | tf_op jit(solution)/shard_map/all_to_all | solution.py:312
  55.5 0.0 copy-done.1
  55.5 0.0 copy-done.2
  55.5 0.0 copy-done.3
  55.5 0.0 copy-done.4
  55.5 0.0 copy-done.6
  55.5 1.5 %source_traces.1 = (f32[512,128]{1,0:T(8,128)S(1)}, f32[64,2,32,128]{3,2,1,0:T(8,128)S(1)}) custom-call(s32[3]{0:T(128)S(1)} %pad_add_fusion.pos_ref, bf16[256,256]{1,0:T(8,128)(2,1)S(1)} %copy-done.2, bf16[256,256]{1,0:T(8,128)(2,1)S(1)} %copy-done.1, bf16[256,256]{1,0:T(8,128)(2,1)S(1)} %copy-done.4, bf16[256,256]{1,0:T(8,128)(2,1)S(1)} %copy-done.3, ...), custom_call_target="tpu_custom_call" | custom-call | tf_op jit(solution)/shard_map/source_traces/pallas_call | solution.py:195
  57.0 35.5 %all_to_all.16.own = f32[64,2,32,128]{3,2,1,0:T(8,128)S(1)} all-to-all(f32[64,2,32,128]{3,2,1,0:T(8,128)S(1)} %get-tuple-element.12), channel_id=1, replica_groups=mesh['z'=4,'xh'=2,'xl'=2,'y'=4,'c'=2] {'xh','z','xl','y'}, dimensions={0} | all-to-all | bytes 4194304 | tf_op jit(solution)/shard_map/all_to_all | solution.py:312
  92.5 0.3 fusion
  92.7 0.1 collective-permute-start.1
  92.8 0.5 collective-permute-start.2
  93.3 2.1 %collective-permute-done.1.oth = f32[32,2,32,128]{3,2,1,0:T(8,128)S(1)} collective-permute-done((f32[32,2,32,128]{3,2,1,0:T(8,128)S(1)}, f32[32,2,32,128]{3,2,1,0:T(8,128)S(1)}, u32[]{:S(2)}, u32[]{:S(2)}) %collective-permute-start.1) | collective-permute-done | bytes 1048608 | tf_op jit(solution)/shard_map/ppermute | solution.py:329
  95.5 1.6 %adjoint_panel0.1 = (f32[8,4,32,128]{3,2,1,0:T(8,128)S(1)}, f32[512,128]{1,0:T(8,128)}) custom-call(f32[64,2,32,128]{3,2,1,0:T(8,128)S(1)} %all_to_all.16.own, f32[32,2,32,128]{3,2,1,0:T(8,128)S(1)} %collective-permute-done.1.oth, bf16[16,1024,256]{2,1,0:T(8,128)(2,1)S(1)} %get-tuple-element.13.rh_ref, bf16[16,1024,256]{2,1,0:T(8,128)(2,1)S(1)} %get-tuple-element.14.rl_ref, ...), custom_call_target="tpu_custom_call" | custom-call | flops 1610612736 | bytes 1048576 | tf_op jit(solution)/shard_map/adjoint_panel0/pallas_call | solution.py:257
  97.1 0.0 collective-permute-done.2.oth
  97.2 0.0 copy-start
  97.2 0.0 copy-start.5
  97.2 1.6 %adjoint_panel1.1 = f32[8,4,32,128]{3,2,1,0:T(8,128)S(1)} custom-call(f32[64,2,32,128]{3,2,1,0:T(8,128)S(1)} %all_to_all.16.own, f32[32,2,32,128]{3,2,1,0:T(8,128)S(1)} %collective-permute-done.2.oth, bf16[16,1024,256]{2,1,0:T(8,128)(2,1)S(1)} %get-tuple-element.13.rh_ref, bf16[16,1024,256]{2,1,0:T(8,128)(2,1)S(1)} %get-tuple-element.14.rl_ref, ...), custom_call_target="tpu_custom_call" | custom-call | flops 1610612736 | bytes 1048576 | tf_op jit(solution)/shard_map/adjoint_panel1/pallas_call | solution.py:257
  98.8 15.1 %all_to_all.17.x_ref = f32[8,4,32,128]{3,2,1,0:T(8,128)S(1)} all-to-all(f32[8,4,32,128]{3,2,1,0:T(8,128)S(1)} %adjoint_panel1.1), channel_id=1, replica_groups=mesh['z'=4,'xh'=2,'xl'=2,'y'=4,'c'=2] {'z','xh'}, dimensions={0} | all-to-all | bytes 1048576 | tf_op jit(solution)/shard_map/all_to_all | solution.py:312
  113.9 0.0 copy-done
  113.9 0.0 copy-done.5
  113.9 1.8 %receiver_traces.1 = f32[1024,128]{1,0:T(8,128)} custom-call(s32[3]{0:T(128)S(1)} %pad_add_fusion.pos_ref, bf16[256,256]{1,0:T(8,128)(2,1)S(1)} %copy-done.2, bf16[256,256]{1,0:T(8,128)(2,1)S(1)} %copy-done.1, s32[4,128]{1,0:T(4,128)S(1)} %copy-done.5, f32[1024,128]{1,0:T(8,128)S(1)} %bitcast.10, f32[8,4,32,128]{3,2,1,0:T(8,128)S(1)} %all_to_all.17.x_ref), custom_call_target="tpu_custom_call" | custom-call | tf_op jit(solution)/shard_map/receiver_traces/pallas_call | solution.py:296
Async XLA Ops:
  9.4 4.2 %collective-permute-start = (f32[64,2,32,128]{3,2,1,0:T(8,128)S(1)}, f32[64,2,32,128]{3,2,1,0:T(8,128)S(1)}, u32[]{:S(2)}, u32[]{:S(2)}) collective-permute-start(f32[64,2,32,128]{3,2,1,0:T(8,128)S(1)} %get-tuple-element.11), channel_id=1, source_target_pairs={{0,1},{1,0},{2,3},{3,2},{4,5},{5,4},{6,7},{7,6},{8,9},{9,8},{10,11... | collective-permute-start | bytes 6291464 | tf_op jit(solution)/shard_map/ppermute | solution.py:324
  14.1 41.4 %copy-start.1 = (bf16[256,256]{1,0:T(8,128)(2,1)S(1)}, bf16[256,256]{1,0:T(8,128)(2,1)}, u32[]{:S(2)}) copy-start(bf16[256,256]{1,0:T(8,128)(2,1)} %constant.29.clone.tl_ref) | copy-start | bytes 393220
  14.1 41.4 %copy-start.2 = (bf16[256,256]{1,0:T(8,128)(2,1)S(1)}, bf16[256,256]{1,0:T(8,128)(2,1)}, u32[]{:S(2)}) copy-start(bf16[256,256]{1,0:T(8,128)(2,1)} %constant.28.clone.th_ref) | copy-start | bytes 393220
  14.1 41.4 %copy-start.3 = (bf16[256,256]{1,0:T(8,128)(2,1)S(1)}, bf16[256,256]{1,0:T(8,128)(2,1)}, u32[]{:S(2)}) copy-start(bf16[256,256]{1,0:T(8,128)(2,1)} %constant.31.clone.ttl_ref) | copy-start | bytes 393220
  14.1 41.4 %copy-start.4 = (bf16[256,256]{1,0:T(8,128)(2,1)S(1)}, bf16[256,256]{1,0:T(8,128)(2,1)}, u32[]{:S(2)}) copy-start(bf16[256,256]{1,0:T(8,128)(2,1)} %constant.30.clone.tth_ref) | copy-start | bytes 393220
  14.1 41.4 %copy-start.6 = (s32[2,128]{1,0:T(2,128)S(1)}, s32[2,128]{1,0:T(2,128)}, u32[]{:S(2)}) copy-start(s32[2,128]{1,0:T(2,128)} %mute_ref.2) | copy-start | bytes 3076
  92.7 2.7 %collective-permute-start.1 = (f32[32,2,32,128]{3,2,1,0:T(8,128)S(1)}, f32[32,2,32,128]{3,2,1,0:T(8,128)S(1)}, u32[]{:S(2)}, u32[]{:S(2)}) collective-permute-start(f32[32,2,32,128]{3,2,1,0:T(8,128)S(1)} %bitcast.12), channel_id=1, source_target_pairs={{0,1},{1,0},{2,3},{3,2},{4,5},{5,4},{6,7},{7,6},{8,9},{9,8},{10,11... | collective-permute-start | bytes 3145736 | tf_op jit(solution)/shard_map/ppermute | solution.py:329
  92.8 4.3 %collective-permute-start.2 = (f32[32,2,32,128]{3,2,1,0:T(8,128)S(1)}, f32[32,2,32,128]{3,2,1,0:T(8,128)S(1)}, u32[]{:S(2)}, u32[]{:S(2)}) collective-permute-start(f32[32,2,32,128]{3,2,1,0:T(8,128)S(1)} %bitcast.11), channel_id=1, source_target_pairs={{0,1},{1,0},{2,3},{3,2},{4,5},{5,4},{6,7},{7,6},{8,9},{9,8},{10,11... | collective-permute-start | bytes 3145736 | tf_op jit(solution)/shard_map/ppermute | solution.py:329
  97.2 16.8 %copy-start = (f32[256,4,128]{2,1,0:T(4,128)S(1)}, f32[256,4,128]{2,1,0:T(4,128)}, u32[]{:S(2)}) copy-start(f32[256,4,128]{2,1,0:T(4,128)} %param.11) | copy-start | bytes 1572868
  97.2 16.8 %copy-start.5 = (s32[4,128]{1,0:T(4,128)S(1)}, s32[4,128]{1,0:T(4,128)}, u32[]{:S(2)}) copy-start(s32[4,128]{1,0:T(4,128)} %mute_ref.3) | copy-start | bytes 6148

commit v11 on v10

--- a/solution.py
+++ b/solution.py
@@ -41,7 +41,9 @@
 
 
 def mm3(a, b):
-    return mm(a[0], b[0]) + (mm(a[0], b[1]) + mm(a[1], b[0]))
+    return mm(
+        jnp.concatenate([a[0], a[0], a[1]], axis=1), jnp.concatenate([b[0], b[1], b[0]], axis=0)
+    )
 
 
 def params(mib):
@@ -63,7 +65,7 @@
 
 
 def place(z, xh, xl, y):
-    return ((xh * 4 + z) * 2 + xl) * 4 + y
+    return ((z * 2 + xl) * 2 + xh) * 4 + y
 
 
 AHEAD = 7
@@ -223,7 +225,7 @@
                 for part in range(8):
                     j, xlo = part // 4, part % 2
                     if (part // 2) % 2:
-                        v = [oth[((xh_ * 2 + zz) * 2 + xlo) * 4 + y, j, g8, :] for y in range(4)]
+                        v = [oth[place(zz, xh_, xlo, y), j, g8, :] for y in range(4)]
                     else:
                         v = [own[place(z, xh_, xlo, y), j, g8, :] for y in range(4)]
                     for q in range(4):
@@ -305,7 +307,7 @@
 
 
 SWAP = [(0, 1), (1, 0)]
-CHIPS = ("xh", "z", "xl", "y")
+CHIPS = ("z", "xl", "xh", "y")
 
 
 def exchange(x, axes):
@@ -324,10 +326,7 @@
     parts = exchange(own + lax.ppermute(oth, "c", SWAP), CHIPS)
     time, back = source_traces(pos, (th, tl, th.T, tl.T), mute_source, parts)
     b_own = exchange(back, CHIPS)
-    by_z = b_own.reshape(2, 4, 8, 2, 32, 128)
-    b_oth = [
-        lax.ppermute(by_z[:, i * 2 : i * 2 + 2].reshape(32, 2, 32, 128), "c", SWAP) for i in range(2)
-    ]
+    b_oth = [lax.ppermute(b_own[i * 32 : i * 32 + 32], "c", SWAP) for i in range(2)]
     adjoint, time = adjoint_panel(0, b_own, b_oth[0], rh, rl, time)
     adjoint = adjoint_panel(1, b_own, b_oth[1], rh, rl, adjoint)
     received = exchange(adjoint, ("z", "xh"))

time: 116 us -> 114 us (0.983)
  blocking collectives: 91.9 us -> 90 us
    all_to_all x3, blocking collectives: 91.9 us -> 90 us  [exchange(): return lax.all_to_all(x, axes, split_axis=0, concat_axis=0, tiled=True)]
where the time goes in v11:
time: 114 us
  blocking collectives  90 us (79%)
  Pallas kernels  15.2 us (13%)
  waiting for transfers between devices  6.3 us (6%)
    all_to_all x3, blocking collectives, exchange(): return lax.all_to_all(x, axes, split_axis=0, concat_axis=0, tiled=True)  90 us
    pallas_call x1, Pallas kernels, forward_panel(): pl.pallas_call(forward_kernel, in_specs=[SMEM, HBM, HBM], out_specs=[VMEM...  8.65 us
    ppermute x1, waiting for transfers between devices, body(): parts = exchange(own + lax.ppermute(oth, 'c', SWAP), CHIPS)  4.15 us
    pallas_call x2, Pallas kernels, adjoint_panel(): pl.pallas_call(functools.partial(adjoint_kernel, second), in_specs=[VMEM]...  3.27 us
  transfers between devices with their start and end apart: 3, of which 2 were waited for; matrix products, arithmetic and copies ran while one was open for 0% of the time, Pallas kernels for 1%

profile of v11, /device:TPU:0, one launch (start us, length us, event | category | flops | bytes accessed | tf_op | source)
XLA Modules:
  0.0 113.8 jit_solution(8444327516102746568)
XLA Ops:
  0.6 0.1 pad_add_fusion.pos_ref
  0.7 8.6 %forward_panel.1 = (f32[64,2,32,128]{3,2,1,0:T(8,128)S(1)}, f32[64,2,32,128]{3,2,1,0:T(8,128)S(1)}, bf16[16,1024,256]{2,1,0:T(8,128)(2,1)S(1)}, bf16[16,1024,256]{2,1,0:T(8,128)(2,1)S(1)}) custom-call(s32[3]{0:T(128)S(1)} %pad_add_fusion.pos_ref, f32[16,2,32,128]{3,2,1,0:T(8,128)} %f_hbm.1, f32[16,2,1024,128]{3,2,1,0:T(8,128)} %r_hbm.1), custom_call_target="tpu_custom_call" | custom-call | flops 3221225472 | bytes 22020096 | tf_op jit(solution)/shard_map/forward_panel/pallas_call | solution.py:152
  9.4 0.1 collective-permute-start
  9.5 4.1 %collective-permute-done = f32[64,2,32,128]{3,2,1,0:T(8,128)S(1)} collective-permute-done((f32[64,2,32,128]{3,2,1,0:T(8,128)S(1)}, f32[64,2,32,128]{3,2,1,0:T(8,128)S(1)}, u32[]{:S(2)}, u32[]{:S(2)}) %collective-permute-start) | collective-permute-done | bytes 2097184 | tf_op jit(solution)/shard_map/ppermute | solution.py:326
  13.6 0.5 add.7
  14.1 0.0 copy-start.1
  14.1 0.0 copy-start.2
  14.1 0.0 copy-start.3
  14.1 0.0 copy-start.4
  14.1 0.0 copy-start.6
  14.2 41.3 %all_to_all.15.x_ref = f32[64,2,32,128]{3,2,1,0:T(8,128)S(1)} all-to-all(f32[64,2,32,128]{3,2,1,0:T(8,128)S(1)} %add.7), channel_id=1, replica_groups=mesh['z'=4,'xh'=2,'xl'=2,'y'=4,'c'=2] {'z','xl','xh','y'}, dimensions={0} | all-to-all | bytes 4194304 | tf_op jit(solution)/shard_map/all_to_all | solution.py:314
  55.5 0.0 copy-done.1
  55.5 0.0 copy-done.2
  55.5 0.0 copy-done.3
  55.5 0.0 copy-done.4
  55.5 0.0 copy-done.6
  55.5 1.5 %source_traces.1 = (f32[512,128]{1,0:T(8,128)S(1)}, f32[64,2,32,128]{3,2,1,0:T(8,128)S(1)}) custom-call(s32[3]{0:T(128)S(1)} %pad_add_fusion.pos_ref, bf16[256,256]{1,0:T(8,128)(2,1)S(1)} %copy-done.2, bf16[256,256]{1,0:T(8,128)(2,1)S(1)} %copy-done.1, bf16[256,256]{1,0:T(8,128)(2,1)S(1)} %copy-done.4, bf16[256,256]{1,0:T(8,128)(2,1)S(1)} %copy-done.3, ...), custom_call_target="tpu_custom_call" | custom-call | tf_op jit(solution)/shard_map/source_traces/pallas_call | solution.py:197
  57.0 34.0 %all_to_all.16.own = f32[64,2,32,128]{3,2,1,0:T(8,128)S(1)} all-to-all(f32[64,2,32,128]{3,2,1,0:T(8,128)S(1)} %get-tuple-element.12), channel_id=1, replica_groups=mesh['z'=4,'xh'=2,'xl'=2,'y'=4,'c'=2] {'z','xl','xh','y'}, dimensions={0} | all-to-all | bytes 4194304 | tf_op jit(solution)/shard_map/all_to_all | solution.py:314
  90.9 0.3 fusion
  91.2 0.1 collective-permute-start.1
  91.3 0.5 collective-permute-start.2
  91.8 2.1 %collective-permute-done.1.oth = f32[32,2,32,128]{3,2,1,0:T(8,128)S(1)} collective-permute-done((f32[32,2,32,128]{3,2,1,0:T(8,128)S(1)}, f32[32,2,32,128]{3,2,1,0:T(8,128)S(1)}, u32[]{:S(2)}, u32[]{:S(2)}) %collective-permute-start.1) | collective-permute-done | bytes 1048608 | tf_op jit(solution)/shard_map/ppermute | solution.py:329
  93.9 1.6 %adjoint_panel0.1 = (f32[8,4,32,128]{3,2,1,0:T(8,128)S(1)}, f32[512,128]{1,0:T(8,128)}) custom-call(f32[64,2,32,128]{3,2,1,0:T(8,128)S(1)} %all_to_all.16.own, f32[32,2,32,128]{3,2,1,0:T(8,128)S(1)} %collective-permute-done.1.oth, bf16[16,1024,256]{2,1,0:T(8,128)(2,1)S(1)} %get-tuple-element.13.rh_ref, bf16[16,1024,256]{2,1,0:T(8,128)(2,1)S(1)} %get-tuple-element.14.rl_ref, ...), custom_call_target="tpu_custom_call" | custom-call | flops 1610612736 | bytes 1048576 | tf_op jit(solution)/shard_map/adjoint_panel0/pallas_call | solution.py:259
  95.6 0.0 collective-permute-done.2.oth
  95.6 0.0 copy-start
  95.6 0.0 copy-start.5
  95.6 1.6 %adjoint_panel1.1 = f32[8,4,32,128]{3,2,1,0:T(8,128)S(1)} custom-call(f32[64,2,32,128]{3,2,1,0:T(8,128)S(1)} %all_to_all.16.own, f32[32,2,32,128]{3,2,1,0:T(8,128)S(1)} %collective-permute-done.2.oth, bf16[16,1024,256]{2,1,0:T(8,128)(2,1)S(1)} %get-tuple-element.13.rh_ref, bf16[16,1024,256]{2,1,0:T(8,128)(2,1)S(1)} %get-tuple-element.14.rl_ref, ...), custom_call_target="tpu_custom_call" | custom-call | flops 1610612736 | bytes 1048576 | tf_op jit(solution)/shard_map/adjoint_panel1/pallas_call | solution.py:259
  97.2 14.7 %all_to_all.17.x_ref = f32[8,4,32,128]{3,2,1,0:T(8,128)S(1)} all-to-all(f32[8,4,32,128]{3,2,1,0:T(8,128)S(1)} %adjoint_panel1.1), channel_id=1, replica_groups=mesh['z'=4,'xh'=2,'xl'=2,'y'=4,'c'=2] {'z','xh'}, dimensions={0} | all-to-all | bytes 1048576 | tf_op jit(solution)/shard_map/all_to_all | solution.py:314
  112.0 0.0 copy-done
  112.0 0.0 copy-done.5
  112.0 1.8 %receiver_traces.1 = f32[1024,128]{1,0:T(8,128)} custom-call(s32[3]{0:T(128)S(1)} %pad_add_fusion.pos_ref, bf16[256,256]{1,0:T(8,128)(2,1)S(1)} %copy-done.2, bf16[256,256]{1,0:T(8,128)(2,1)S(1)} %copy-done.1, s32[4,128]{1,0:T(4,128)S(1)} %copy-done.5, f32[1024,128]{1,0:T(8,128)S(1)} %bitcast.6, f32[8,4,32,128]{3,2,1,0:T(8,128)S(1)} %all_to_all.17.x_ref), custom_call_target="tpu_custom_call" | custom-call | tf_op jit(solution)/shard_map/receiver_traces/pallas_call | solution.py:298
Async XLA Ops:
  9.4 4.2 %collective-permute-start = (f32[64,2,32,128]{3,2,1,0:T(8,128)S(1)}, f32[64,2,32,128]{3,2,1,0:T(8,128)S(1)}, u32[]{:S(2)}, u32[]{:S(2)}) collective-permute-start(f32[64,2,32,128]{3,2,1,0:T(8,128)S(1)} %get-tuple-element.11), channel_id=1, source_target_pairs={{0,1},{1,0},{2,3},{3,2},{4,5},{5,4},{6,7},{7,6},{8,9},{9,8},{10,11... | collective-permute-start | bytes 6291464 | tf_op jit(solution)/shard_map/ppermute | solution.py:326
  14.1 41.4 %copy-start.1 = (bf16[256,256]{1,0:T(8,128)(2,1)S(1)}, bf16[256,256]{1,0:T(8,128)(2,1)}, u32[]{:S(2)}) copy-start(bf16[256,256]{1,0:T(8,128)(2,1)} %constant.29.clone.tl_ref) | copy-start | bytes 393220
  14.1 41.4 %copy-start.2 = (bf16[256,256]{1,0:T(8,128)(2,1)S(1)}, bf16[256,256]{1,0:T(8,128)(2,1)}, u32[]{:S(2)}) copy-start(bf16[256,256]{1,0:T(8,128)(2,1)} %constant.28.clone.th_ref) | copy-start | bytes 393220
  14.1 41.3 %copy-start.3 = (bf16[256,256]{1,0:T(8,128)(2,1)S(1)}, bf16[256,256]{1,0:T(8,128)(2,1)}, u32[]{:S(2)}) copy-start(bf16[256,256]{1,0:T(8,128)(2,1)} %constant.31.clone.ttl_ref) | copy-start | bytes 393220
  14.1 41.3 %copy-start.4 = (bf16[256,256]{1,0:T(8,128)(2,1)S(1)}, bf16[256,256]{1,0:T(8,128)(2,1)}, u32[]{:S(2)}) copy-start(bf16[256,256]{1,0:T(8,128)(2,1)} %constant.30.clone.tth_ref) | copy-start | bytes 393220
  14.1 41.3 %copy-start.6 = (s32[2,128]{1,0:T(2,128)S(1)}, s32[2,128]{1,0:T(2,128)}, u32[]{:S(2)}) copy-start(s32[2,128]{1,0:T(2,128)} %mute_ref.2) | copy-start | bytes 3076
  91.2 2.7 %collective-permute-start.1 = (f32[32,2,32,128]{3,2,1,0:T(8,128)S(1)}, f32[32,2,32,128]{3,2,1,0:T(8,128)S(1)}, u32[]{:S(2)}, u32[]{:S(2)}) collective-permute-start(f32[32,2,32,128]{3,2,1,0:T(8,128)S(1)} %get-tuple-element.19), channel_id=1, source_target_pairs={{0,1},{1,0},{2,3},{3,2},{4,5},{5,4},{6,7},{7,6},{8,9},{9,8},{10,11... | collective-permute-start | bytes 3145736 | tf_op jit(solution)/shard_map/ppermute | solution.py:329
  91.3 4.3 %collective-permute-start.2 = (f32[32,2,32,128]{3,2,1,0:T(8,128)S(1)}, f32[32,2,32,128]{3,2,1,0:T(8,128)S(1)}, u32[]{:S(2)}, u32[]{:S(2)}) collective-permute-start(f32[32,2,32,128]{3,2,1,0:T(8,128)S(1)} %get-tuple-element.18), channel_id=1, source_target_pairs={{0,1},{1,0},{2,3},{3,2},{4,5},{5,4},{6,7},{7,6},{8,9},{9,8},{10,11... | collective-permute-start | bytes 3145736 | tf_op jit(solution)/shard_map/ppermute | solution.py:329
  95.6 16.4 %copy-start = (f32[256,4,128]{2,1,0:T(4,128)S(1)}, f32[256,4,128]{2,1,0:T(4,128)}, u32[]{:S(2)}) copy-start(f32[256,4,128]{2,1,0:T(4,128)} %param.11) | copy-start | bytes 1572868
  95.6 16.4 %copy-start.5 = (s32[4,128]{1,0:T(4,128)S(1)}, s32[4,128]{1,0:T(4,128)}, u32[]{:S(2)}) copy-start(s32[4,128]{1,0:T(4,128)} %mute_ref.3) | copy-start | bytes 6148
